TPU v7x, 512 devices: a whole 4x8x8 slice. The times are simulated.
512 devices in a mesh: half: 2 (over core), dom: 32 (over z, y_lo), slab: 8 (over y_hi, x).
Axes of the slice: x: 4, y: 8 (y_hi: 2, y_lo: 4; y = y_hi * 4 + y_lo), z: 8, core: 2. Of those that a mesh axis runs over, the one named last changes fastest.
Arguments:
- volume: float32 [2, 8192, 400], P('half', 'slab')
- images: bfloat16 [2, 32768, 400], P('half', 'dom'), may hold values from -18 to 18
- tap_index: int32 [2, 8, 8, 32768], P('half', 'slab', None, 'dom'), may hold values from 0 to 1023, as said below
- tap_weight: float32 [2, 8, 8, 32768], P('half', 'slab', None, 'dom'), may hold values from 0.2 to 1
- classes: int32 [2, 512], P('half', 'dom'), may hold values from 0 to 15
- shifts: int32 [2, 2, 512], P('half', None, 'dom'), may hold values from -8 to 8
- defocus: float32 [16], replicated, may hold values from 0.5 to 3
Outputs:
- updated: float32 [2, 8192, 400], P('half', 'slab')
Inputs may be any that keep to these rules, and one draw needn't show every extreme that they name: `tap_index`: the 8 taps of one line and slab read 8 consecutive map lines.
All inputs are finite; a program needn't handle non-finite values.
Results may differ from a plain program's by a relative error of at most 0.0035.
Values may be sent and summed in bfloat16 or wider, within the bound.
No kernel may reach another device: no remote copies, remote signals or barrier semaphores. Data moves between devices by JAX's collectives and lax.ppermute only.
A program may use at most 64 MiB of HBM per device.

v0:
```python
import math

import jax
import jax.numpy as jnp
from jax import lax
from jax.sharding import PartitionSpec as P

LPI = 64


CTF_GAIN = 30.0
PHASE_ZERO = 0.1
STEP_SCALE = 0.5


def swapped(value, axis, distance):
    mask = 2**distance
    pairs = [(source, source ^ mask) for source in range(lax.axis_size(axis))]
    return lax.ppermute(value, axis, pairs)


def line_terms(classes_local, shifts_local, defocus, radii):
    radius = jnp.arange(radii, dtype=jnp.float32)
    class_ids = jnp.arange(defocus.shape[0], dtype=jnp.int32)
    focus = jnp.sum(
        jnp.where(classes_local[:, None] == class_ids[None, :], defocus[None, :], 0.0), axis=1
    )
    ctf_part = -jnp.sin(CTF_GAIN * focus[:, None] * (radius[None, :] / radii) ** 2 + PHASE_ZERO)
    ctf_rows = jnp.repeat(ctf_part, LPI, axis=0)
    theta = jnp.pi * jnp.arange(LPI, dtype=jnp.float32) / LPI
    theta_rows = jnp.tile(theta, classes_local.shape[0])
    shift_x = jnp.repeat(shifts_local[0].astype(jnp.float32), LPI)
    shift_y = jnp.repeat(shifts_local[1].astype(jnp.float32), LPI)
    along = shift_x * jnp.cos(theta_rows) + shift_y * jnp.sin(theta_rows)
    phase = 2.0 * jnp.pi * radius[None, :] * along[:, None] / (2.0 * radii)
    return (ctf_rows, jnp.cos(phase), jnp.sin(phase))


def weighted_back(proj, data, ctf_rows, cosine, sine_part, radii):
    proj_re, proj_im = (proj[:, :radii], proj[:, radii:])
    data_f = data.astype(jnp.float32)
    res_re = ctf_rows * (cosine * proj_re - sine_part * proj_im) - data_f[:, :radii]
    res_im = ctf_rows * (sine_part * proj_re + cosine * proj_im) - data_f[:, radii:]
    back_re = ctf_rows * (cosine * res_re + sine_part * res_im)
    back_im = ctf_rows * (cosine * res_im - sine_part * res_re)
    return jnp.concatenate([back_re, back_im], axis=1).astype(jnp.bfloat16)


def shell_terms(mine, other, radii):
    num = jnp.sum(mine[:, :radii] * other[:, :radii] + mine[:, radii:] * other[:, radii:], axis=0)
    den_mine = jnp.sum(mine[:, :radii] ** 2 + mine[:, radii:] ** 2, axis=0)
    den_other = jnp.sum(other[:, :radii] ** 2 + other[:, radii:] ** 2, axis=0)
    return (num, den_mine, den_other)


def shell_factor(totals):
    num, den_mine, den_other = totals
    fsc = num / (jnp.sqrt(den_mine * den_other) + 1e-06)
    return jnp.tile((1.0 + fsc) / 2.0, 2)


def spread_back(taps_at, taps_wide, back_wide, start, count):
    total = jnp.zeros((count, back_wide.shape[1]), jnp.float32)
    for tap_num in range(taps_at.shape[0]):
        local = taps_at[tap_num] - start
        inside = jnp.logical_and(local >= 0, local < count)
        local = jnp.where(inside, local, count)
        total = total.at[local].add(taps_wide[tap_num][:, None] * back_wide, mode="drop")
    return total


def body(volume, images, tap_index, tap_weight, classes, shifts, defocus):
    slab_map = volume[0]
    lines_slab = slab_map.shape[0]
    radii = slab_map.shape[1] // 2
    data = images[0]
    rows = data.shape[0]
    taps_at = tap_index[0, 0]
    taps_wide = tap_weight[0, 0].astype(jnp.bfloat16).astype(jnp.float32)
    map_low = slab_map.astype(jnp.bfloat16)
    partial_value = jnp.zeros((rows, 2 * radii), jnp.float32)
    for tap_num in range(taps_at.shape[0]):
        picked = jnp.take(map_low, taps_at[tap_num], axis=0)
        partial_value = partial_value + taps_wide[tap_num][:, None] * picked.astype(jnp.float32)
    ctf_rows, cosine, sine_part = line_terms(classes[0], shifts[0], defocus, radii)
    proj = lax.psum(partial_value, "slab")
    back = weighted_back(proj, data, ctf_rows, cosine, sine_part, radii)
    back_wide = back.astype(jnp.float32)
    step = STEP_SCALE / math.sqrt(rows * lax.axis_size("dom") * taps_at.shape[0] / lines_slab)
    local_grad = spread_back(taps_at, taps_wide, back_wide, 0, lines_slab)
    grad = lax.psum(local_grad, "dom")
    cand = slab_map - step * grad
    other = swapped(cand.astype(jnp.bfloat16), "half", 0).astype(cand.dtype)
    totals = lax.psum(shell_terms(cand, other, radii), "slab")
    result = slab_map - step * shell_factor(totals)[None, :] * grad
    return result[None]


def solution(mesh):
    placed = (
        P("half", "slab", None),
        P("half", "dom", None),
        P("half", "slab", None, "dom"),
        P("half", "slab", None, "dom"),
        P("half", "dom"),
        P("half", None, "dom"),
        P(),
    )
    return jax.shard_map(
        body, mesh=mesh, in_specs=placed, out_specs=P("half", "slab", None), check_vma=False
    )
```

profile of v0, /device:TPU:8, one launch (start us, length us, event | category | flops | bytes accessed | tf_op | source)
XLA Modules:
  0.0 662.7 jit_solution(6634125040692771641)
XLA Ops:
  9.9 5.1 gather_fusion.2
  14.9 5.1 gather_fusion.3
  20.0 5.1 gather_fusion.4
  25.0 5.1 gather_fusion.5
  30.1 5.1 gather_fusion.6
  35.2 5.1 gather_fusion.7
  40.2 5.1 gather_fusion
  45.3 5.1 gather_fusion.1
  50.4 8.4 %multiply_add_fusion = f32[1024,400]{1,0:T(8,128)} fusion(bf16[1024,400]{1,0:T(8,128)(2,1)} %gather_fusion.7, bf16[1024,400]{1,0:T(8,128)(2,1)} %gather_fusion.6, bf16[1024,400]{1,0:T(8,128)(2,1)} %gather_fusion.5, bf16[1024,400]{1,0:T(8,128)(2,1)} %gather_fusion.4, bf16[1024,400]{1,0:T(8,128)(2,1)} %gather_fusion.3, bf16[1024,400]{1,0:T(8,128)(2,1)} %gather_fusion.2, ...), kind=kLoop, calls=%fused_computation.40 | loop fusion | flops 12697600 | bytes 8232960 | tf_op jit(solution)/shard_map/add | solution.py:84
  63.3 134.6 %all-reduce.4.cloned.1.call-done = f32[1024,400]{1,0:T(8,128)} async-done(((f32[1024,400]{1,0:T(8,128)}), f32[1024,400]{1,0:T(8,128)}) %all-reduce.4.cloned.1.call-update) | async-done | bytes 1638416 | tf_op jit(solution)/shard_map/psum | solution.py:86
  197.9 7.9 %fusion.11 = (bf16[1024,200]{1,0:T(8,128)(2,1)S(1)}, bf16[1024,200]{1,0:T(8,128)(2,1)S(1)}) fusion(f32[1024,400]{1,0:T(8,128)} %bitcast_convert_fusion.1, f32[1024,400]{1,0:T(8,128)} %all-reduce.4.cloned.1.call-done, f32[1024]{0:T(1024)S(1)} %add.180, f32[200]{0:T(256)S(1)} %iota_multiply_fusion, f32[16,200]{1,0:T(8,128)S(1)} %sine_negate_fusion), kind=kLoop, calls=%fused_computation.43 | loop fusion | flops 4505600 | bytes 4113696 | tf_op jit(solution)/shard_map/convert.1
  205.8 8.5 %scatter_custom_fusion = f32[1024,400]{1,0:T(8,128)} fusion(s32[1024]{0:T(1024)S(1)} %bitcast.117, f32[1024]{0:T(1024)S(1)} %bitcast.93, f32[]{:T(128)} %constant.21.clone.1, bf16[1024,200]{1,0:T(8,128)(2,1)S(1)} %get-tuple-element.15, bf16[1024,200]{1,0:T(8,128)(2,1)S(1)} %get-tuple-element.14), kind=kCustom, calls=%fused_computation.28 | custom fusion | flops 2457600 | bytes 2691076 | tf_op jit(solution)/shard_map/scatter-add | solution.py:68
  214.3 9.9 %scatter_custom_fusion.1 = f32[1024,400]{1,0:T(8,128)} fusion(f32[1024,400]{1,0:T(8,128)} %scatter_custom_fusion, s32[1024]{0:T(1024)S(1)} %bitcast.116, f32[1024]{0:T(1024)S(1)} %bitcast.91, bf16[1024,200]{1,0:T(8,128)(2,1)S(1)} %get-tuple-element.15, bf16[1024,200]{1,0:T(8,128)(2,1)S(1)} %get-tuple-element.14), kind=kCustom, calls=%fused_computation.29 | custom fusion | flops 2457600 | bytes 2691072 | tf_op jit(solution)/shard_map/scatter-add | solution.py:68
  224.3 10.0 %scatter_custom_fusion.2 = f32[1024,400]{1,0:T(8,128)} fusion(f32[1024,400]{1,0:T(8,128)} %scatter_custom_fusion.1, s32[1024]{0:T(1024)S(1)} %bitcast.115, f32[1024]{0:T(1024)S(1)} %bitcast.89, bf16[1024,200]{1,0:T(8,128)(2,1)S(1)} %get-tuple-element.15, bf16[1024,200]{1,0:T(8,128)(2,1)S(1)} %get-tuple-element.14), kind=kCustom, calls=%fused_computation.30 | custom fusion | flops 2457600 | bytes 2691072 | tf_op jit(solution)/shard_map/scatter-add | solution.py:68
  234.2 9.9 %scatter_custom_fusion.3 = f32[1024,400]{1,0:T(8,128)} fusion(f32[1024,400]{1,0:T(8,128)} %scatter_custom_fusion.2, s32[1024]{0:T(1024)S(1)} %bitcast.114, f32[1024]{0:T(1024)S(1)} %bitcast.87, bf16[1024,200]{1,0:T(8,128)(2,1)S(1)} %get-tuple-element.15, bf16[1024,200]{1,0:T(8,128)(2,1)S(1)} %get-tuple-element.14), kind=kCustom, calls=%fused_computation.31 | custom fusion | flops 2457600 | bytes 2691072 | tf_op jit(solution)/shard_map/scatter-add | solution.py:68
  244.2 10.0 %scatter_custom_fusion.4 = f32[1024,400]{1,0:T(8,128)} fusion(f32[1024,400]{1,0:T(8,128)} %scatter_custom_fusion.3, s32[1024]{0:T(1024)S(1)} %bitcast.113, f32[1024]{0:T(1024)S(1)} %bitcast.85, bf16[1024,200]{1,0:T(8,128)(2,1)S(1)} %get-tuple-element.15, bf16[1024,200]{1,0:T(8,128)(2,1)S(1)} %get-tuple-element.14), kind=kCustom, calls=%fused_computation.32 | custom fusion | flops 2457600 | bytes 2691072 | tf_op jit(solution)/shard_map/scatter-add | solution.py:68
  254.1 9.9 %scatter_custom_fusion.5 = f32[1024,400]{1,0:T(8,128)} fusion(f32[1024,400]{1,0:T(8,128)} %scatter_custom_fusion.4, s32[1024]{0:T(1024)S(1)} %bitcast.112, f32[1024]{0:T(1024)S(1)} %bitcast.83, bf16[1024,200]{1,0:T(8,128)(2,1)S(1)} %get-tuple-element.15, bf16[1024,200]{1,0:T(8,128)(2,1)S(1)} %get-tuple-element.14), kind=kCustom, calls=%fused_computation.33 | custom fusion | flops 2457600 | bytes 2691072 | tf_op jit(solution)/shard_map/scatter-add | solution.py:68
  264.1 10.0 %scatter_custom_fusion.6 = f32[1024,400]{1,0:T(8,128)} fusion(f32[1024,400]{1,0:T(8,128)} %scatter_custom_fusion.5, s32[1024]{0:T(1024)S(1)} %bitcast.111, f32[1024]{0:T(1024)S(1)} %bitcast.81, bf16[1024,200]{1,0:T(8,128)(2,1)S(1)} %get-tuple-element.15, bf16[1024,200]{1,0:T(8,128)(2,1)S(1)} %get-tuple-element.14), kind=kCustom, calls=%fused_computation.34 | custom fusion | flops 2457600 | bytes 2691072 | tf_op jit(solution)/shard_map/scatter-add | solution.py:68
  274.0 9.9 %scatter_custom_fusion.7 = f32[1024,400]{1,0:T(8,128)} fusion(f32[1024,400]{1,0:T(8,128)} %scatter_custom_fusion.6, s32[1024]{0:T(1024)S(1)} %bitcast.110, f32[1024]{0:T(1024)S(1)} %bitcast.79, bf16[1024,200]{1,0:T(8,128)(2,1)S(1)} %get-tuple-element.15, bf16[1024,200]{1,0:T(8,128)(2,1)S(1)} %get-tuple-element.14), kind=kCustom, calls=%fused_computation.35 | custom fusion | flops 2457600 | bytes 2691072 | tf_op jit(solution)/shard_map/scatter-add | solution.py:68
  284.0 324.5 %all-reduce.6.cloned.1.call-done = f32[1024,400]{1,0:T(8,128)} async-done(((f32[1024,400]{1,0:T(8,128)}), f32[1024,400]{1,0:T(8,128)}) %all-reduce.6.cloned.1.call-update) | async-done | bytes 1638416 | tf_op jit(solution)/shard_map/psum | solution.py:91
  608.5 3.4 fusion.35
  621.4 28.2 %all-reduce = (f32[200]{0:T(256)S(1)}, f32[200]{0:T(256)S(1)}, f32[200]{0:T(256)S(1)}) all-reduce(f32[200]{0:T(256)S(1)} %get-tuple-element.7, f32[200]{0:T(256)S(1)} %get-tuple-element.8, f32[200]{0:T(256)S(1)} %get-tuple-element.6), channel_id=1, replica_groups=mesh['half'=2,'dom'=32,'slab'=8] {'slab'}, use_global_device_ids=true, to_apply=%region_12.14 | all-reduce | flops 600 | bytes 4800 | tf_op jit(solution)/shard_map/psum | solution.py:94
  649.8 3.4 fusion.8
  653.2 2.7 copy.23
  (54 shorter events, 17.2 us)
Async XLA Ops:
  6.5 191.4 %all-reduce.4.cloned.1.call-start = ((), (), s32[]{:S(2)}) async-start(), calls=%async_computation | async-start | bytes 4194304 | tf_op jit(solution)/shard_map/psum | solution.py:86
  45.3 5.1 copy-start.2
  58.9 0.7 copy-start.3
  58.9 2.4 copy-start.4
  58.9 2.4 copy-start.5
  58.9 2.7 copy-start.1
  58.9 549.6 %all-reduce.6.cloned.1.call-start = ((), (), s32[]{:S(2)}) async-start(), calls=%async_computation.1 | async-start | bytes 4194304 | tf_op jit(solution)/shard_map/psum | solution.py:91
  613.1 4.6 collective-permute-start
  619.1 1.6 copy-start
Sparse Core Ops, SparseCore 0:
  59.0 138.8 all-reduce.3
  284.1 324.3 all-reduce.5
where the time goes:
time: 664 us; the launch traced here: 663 us
  waiting for transfers between devices  462 us (70%)
  other arithmetic  105 us (16%)
  local copies, waits for them, and re-layouts  52.4 us (8%)
  blocking collectives  28.2 us (4%)
  between operations  13.7 us (2%)
    psum x1, waiting for transfers between devices, body(): grad = lax.psum(local_grad, 'dom')  325 us
    psum x1, waiting for transfers between devices, body(): proj = lax.psum(partial_value, 'slab')  135 us
    scatter-add x8, other arithmetic, spread_back(): total.at[local].add(taps_wide[tap_num][:, None] * back_wide, mode='drop')  78.2 us
    gather x8, local copies, waits for them, and re-layouts, body(): picked = jnp.take(map_low, taps_at[tap_num], axis=0)  40.5 us
    psum x1, blocking collectives, body(): totals = lax.psum(shell_terms(cand, other, radii), 'slab')  28.2 us
  transfers between devices with their start and end apart: 3, of which 3 were waited for; matrix products, arithmetic and copies ran while one was open for 1% of the time, Pallas kernels for 0%

commit v1 on v0

v1 whole, which is shorter than its diff:
```python
import math

import jax
import jax.numpy as jnp
from jax import lax
from jax.experimental import pallas as pl
from jax.experimental.pallas import tpu as pltpu
from jax.sharding import PartitionSpec as P

LPI = 64
CTF_GAIN = 30.0
PHASE_ZERO = 0.1
STEP_SCALE = 0.5

R = 200
K = 8
N_SLAB = 8
N_DOM = 32
LINES = 1024
ROWS = 1024
RB = R // N_SLAB
SHARE = LINES // N_DOM
STEP = STEP_SCALE / math.sqrt(ROWS * N_DOM * K / LINES)

F32 = jnp.float32
BF16 = jnp.bfloat16

IM = 32
PACKED = 64
TIGHT = 56


def lane_group(shape):
    return lax.broadcasted_iota(jnp.int32, shape, len(shape) - 1) // SHARE


def pack_kernel(map_ref, index_ref, weight_ref, out_ref, block):
    index = index_ref[...]
    weight = weight_ref[...]
    base = jnp.min(index, axis=0, keepdims=True)
    place = lax.broadcasted_iota(jnp.int32, index.shape, 0)
    ordered = jnp.zeros(weight.shape, F32)
    for tap in range(K):
        ordered += jnp.where(place == index[tap : tap + 1] - base, weight[tap : tap + 1], 0.0)
    block[RB:IM, :] = ordered[: K - 1]
    block[IM + RB : IM + RB + 1, :] = ordered[K - 1 :]
    block[IM + RB + 1 : IM + RB + 2, :] = (base >> 4).astype(F32)
    block[IM + RB + 2 : IM + RB + 3, :] = (base & 15).astype(F32)
    block[IM + RB + 3 :, :] = jnp.zeros((PACKED - IM - RB - 3, LINES), F32)
    for part in range(N_SLAB):
        block[:RB, :] = map_ref[RB * part : RB * (part + 1), :]
        block[IM : IM + RB, :] = map_ref[R + RB * part : R + RB * (part + 1), :]
        out_ref[part] = block[...].astype(BF16)


def regroup(tiles, y, group):
    out = None
    for slot, tile in enumerate(tiles):
        moved = pltpu.roll(tile, (SHARE * (slot - y)) % 128, 1)
        out = moved if out is None else jnp.where(group == slot, moved, out)
    return out


def image_kernel(place_ref, packed_ref, data_ref, ctf_ref, cos_ref, sin_ref, out_ref, own_ref, taps, proj, back, grad):
    proj[...] = jnp.zeros(proj.shape, F32)

    @pl.loop(0, N_SLAB)
    def _(slab):
        rows = packed_ref[slab].astype(F32)
        low = rows[IM + RB + 2 : IM + RB + 3]
        line = lax.broadcasted_iota(jnp.int32, (16, ROWS), 0).astype(F32)
        first = jnp.zeros((16, ROWS), F32)
        second = jnp.zeros((16, ROWS), F32)
        for tap in range(K):
            row = RB + tap if tap < K - 1 else IM + RB
            weight = rows[row : row + 1]
            first += jnp.where(line == low + tap, weight, 0.0)
            second += jnp.where(line + 16.0 == low + tap, weight, 0.0)
        first = first.astype(BF16)
        second = second.astype(BF16)
        high = jnp.broadcast_to(rows[IM + RB + 1 : IM + RB + 2], (16, ROWS)).astype(BF16)
        none = jnp.zeros((16, ROWS), BF16)
        before = None
        for chunk in range(LINES // 16):
            here = high == jnp.asarray(chunk, BF16)
            value = jnp.where(here, first, none)
            if before is not None:
                value = jnp.where(before, second, value)
            taps[slab, 16 * chunk : 16 * (chunk + 1), :] = value
            before = here
        proj[...] += jnp.dot(packed_ref[slab], taps[slab], preferred_element_type=F32)

    ctf = ctf_ref[...]
    cosine = cos_ref[...]
    sine = sin_ref[...]
    proj_re = proj[:IM]
    proj_im = proj[IM:]
    res_re = ctf * (cosine * proj_re - sine * proj_im) - data_ref[0].astype(F32)
    res_im = ctf * (sine * proj_re + cosine * proj_im) - data_ref[1].astype(F32)
    back_re = ctf * (cosine * res_re + sine * res_im)
    back_im = ctf * (cosine * res_im - sine * res_re)
    back[2 * RB :, :] = jnp.zeros((TIGHT - 2 * RB, ROWS), F32)
    back[:RB, :] = back_re[:RB]
    back[RB : 2 * RB, :] = back_im[:RB]
    back_low = back[...].astype(BF16)

    @pl.loop(0, N_SLAB)
    def _(slab):
        grad[slab] = lax.dot_general(back_low, taps[slab], (((1,), (1,)), ((), ())), preferred_element_type=F32)

    group = lane_group((TIGHT, 128))
    for z in range(8):
        for half in range(2):
            tiles = [grad[4 * half + slot, :, 128 * z : 128 * (z + 1)] for slot in range(4)]
            for y in range(4):
                out_ref[4 * z + y, half] = regroup(tiles, y, group).astype(BF16)

    z = pl.multiple_of(place_ref[0] * 128, 128)
    y = place_ref[1]
    group = lane_group((PACKED, 128))
    for half in range(2):
        out = None
        for slot in range(4):
            tile = packed_ref[4 * half + slot, :, pl.ds(z, 128)].astype(F32)
            moved = pltpu.roll(tile, (SHARE * (slot - y)) & 127, 1)
            out = moved if out is None else jnp.where(group == slot, moved, out)
        own_ref[half] = out


def reduce_kernel(parts_ref, own_ref, grad_ref, cand_ref, total):
    total[...] = jnp.sum(parts_ref[...].astype(F32), axis=0)
    grad_ref[...] = jnp.zeros(grad_ref.shape, F32)
    grad_ref[:, :RB, :] = total[:, :RB, :]
    grad_ref[:, IM : IM + RB, :] = total[:, RB : 2 * RB, :]
    row = lax.broadcasted_iota(jnp.int32, cand_ref.shape, 1) % IM
    cand_ref[...] = jnp.where(row < RB, own_ref[...] - STEP * grad_ref[...], 0.0)


def shell_kernel(grad_ref, cand_ref, other_ref, out_ref, block):
    mine = cand_ref[...]
    other = other_ref[...]

    def shell(value):
        value = value[0] + value[1]
        return value[:IM] + value[IM:]

    sums = jnp.concatenate([shell(mine * other), shell(mine * mine), shell(other * other), jnp.zeros((IM, 128), F32)], axis=0)
    sums = jnp.sum(sums.T, axis=0, keepdims=True)
    group = lane_group((1, 128))
    block[...] = grad_ref[...]
    for item in range(3):
        row = None
        for slot in range(4):
            moved = pltpu.roll(sums, (IM * (slot - item)) % 128, 1)
            row = moved if row is None else jnp.where(group == slot, moved, row)
        high = row.astype(BF16).astype(F32)
        for half in range(2):
            block[half, RB + 2 * item : RB + 2 * item + 1, :] = high
            block[half, RB + 2 * item + 1 : RB + 2 * item + 2, :] = row - high
    group = lane_group((16, 128))
    for half in range(2):
        tiles = [block[half, 16 * fold : 16 * (fold + 1), :] for fold in range(4)]
        for slot in range(4):
            out_ref[4 * half + slot] = regroup(tiles, slot, group).astype(BF16)


def update_kernel(map_ref, parts_ref, out_ref, scale):
    sums = jnp.zeros((N_SLAB, 16, 128), F32)
    for index in range(N_DOM):
        sums += parts_ref[index].astype(F32)
    first = RB - 16
    num = sums[:, first, :] + sums[:, first + 1, :]
    den_mine = sums[:, first + 2, :] + sums[:, first + 3, :]
    den_other = sums[:, first + 4, :] + sums[:, first + 5, :]
    fsc = num / (jnp.sqrt(den_mine * den_other) + 1e-06)
    factor = STEP * (1.0 + fsc) / 2.0
    factor = jnp.where(lane_group((N_SLAB, 128)) == 1, factor, 0.0)
    factor = jnp.concatenate([factor, jnp.zeros((128 - N_SLAB, 128), F32)], axis=0).T
    scale[...] = factor[SHARE : 2 * SHARE, :]
    group = lane_group((16, 128))

    @pl.loop(0, 8)
    def _(z):
        lanes = pl.ds(pl.multiple_of(z * 128, 128), 128)
        for part in range(N_SLAB):
            tiles = [parts_ref[4 * z + y, part].astype(F32) for y in range(4)]
            for fold in range(4):
                count = 16 if fold % 2 == 0 else RB - 16
                start = 16 * (fold % 2)
                at = R * (fold // 2) + RB * part + start
                value = regroup(tiles, fold, group)
                weight = scale[start : start + 16, part : part + 1]
                out_ref[at : at + count, lanes] = map_ref[at : at + count, lanes] - (weight * value)[:count]


def vmem():
    return pl.BlockSpec(memory_space=pltpu.VMEM)


def exchange(value, axis):
    return lax.all_to_all(value, axis, 0, 0, tiled=True)


def line_terms(classes_local, shifts_local, defocus, radius):
    class_ids = jnp.arange(defocus.shape[0], dtype=jnp.int32)
    focus = jnp.sum(jnp.where(classes_local[:, None] == class_ids[None, :], defocus[None, :], 0.0), axis=1)
    ctf = -jnp.sin(CTF_GAIN * focus[None, :] * (radius[:, None] / R) ** 2 + PHASE_ZERO)
    ctf_rows = jnp.repeat(ctf, LPI, axis=1)
    theta = jnp.pi * jnp.arange(LPI, dtype=F32) / LPI
    theta_rows = jnp.tile(theta, classes_local.shape[0])
    shift_x = jnp.repeat(shifts_local[0].astype(F32), LPI)
    shift_y = jnp.repeat(shifts_local[1].astype(F32), LPI)
    along = shift_x * jnp.cos(theta_rows) + shift_y * jnp.sin(theta_rows)
    phase = 2.0 * jnp.pi * radius[:, None] * along[None, :] / (2.0 * R)
    return (ctf_rows, jnp.cos(phase), jnp.sin(phase))


def body(volume, images, tap_index, tap_weight, classes, shifts, defocus):
    map_t = volume[0].T
    data_t = images[0].T
    slab = lax.axis_index("slab")
    dom = lax.axis_index("dom")

    packed = pl.pallas_call(
        pack_kernel,
        out_shape=jax.ShapeDtypeStruct((N_SLAB, PACKED, LINES), BF16),
        in_specs=[vmem()] * 3,
        out_specs=vmem(),
        scratch_shapes=[pltpu.VMEM((PACKED, LINES), F32)],
        name="pack",
    )(map_t, tap_index[0, 0], tap_weight[0, 0])
    packed = exchange(packed, "slab")

    pad = ((0, IM - RB), (0, 0))
    radius = (RB * slab + jnp.arange(RB)).astype(F32)
    ctf, cosine, sine = line_terms(classes[0], shifts[0], defocus, radius)
    ctf, cosine, sine = (jnp.pad(ctf, pad), jnp.pad(cosine, pad), jnp.pad(sine, pad))
    data = lax.dynamic_slice(data_t.reshape(2, R, ROWS), (0, RB * slab, 0), (2, RB, ROWS))
    data = jnp.pad(data, ((0, 0),) + pad)
    place = jnp.stack([dom // 4, dom % 4]).astype(jnp.int32)

    parts, own = pl.pallas_call(
        image_kernel,
        out_shape=(
            jax.ShapeDtypeStruct((N_DOM, 2, TIGHT, 128), BF16),
            jax.ShapeDtypeStruct((2, PACKED, 128), F32),
        ),
        in_specs=[pl.BlockSpec(memory_space=pltpu.SMEM)] + [vmem()] * 5,
        out_specs=(vmem(), vmem()),
        scratch_shapes=[
            pltpu.VMEM((N_SLAB, LINES, ROWS), BF16),
            pltpu.VMEM((PACKED, ROWS), F32),
            pltpu.VMEM((TIGHT, ROWS), F32),
            pltpu.VMEM((N_SLAB, TIGHT, LINES), F32),
        ],
        compiler_params=pltpu.CompilerParams(vmem_limit_bytes=48 << 20),
        name="image",
    )(place, packed, data, ctf, cosine, sine)
    parts = exchange(parts, "dom")

    block = jax.ShapeDtypeStruct((2, PACKED, 128), F32)
    grad, cand = pl.pallas_call(
        reduce_kernel,
        out_shape=(block, block),
        in_specs=[vmem()] * 2,
        out_specs=(vmem(), vmem()),
        scratch_shapes=[pltpu.VMEM((2, TIGHT, 128), F32)],
        name="reduce",
    )(parts, own)
    other = lax.ppermute(cand, "half", [(0, 1), (1, 0)])
    share = pl.pallas_call(
        shell_kernel,
        out_shape=jax.ShapeDtypeStruct((N_SLAB, 16, 128), BF16),
        in_specs=[vmem()] * 3,
        out_specs=vmem(),
        scratch_shapes=[pltpu.VMEM((2, PACKED, 128), F32)],
        name="shell",
    )(grad, cand, other)
    share = exchange(share, "slab")
    every = exchange(jnp.broadcast_to(share[None], (N_DOM,) + share.shape), "dom")
    result = pl.pallas_call(
        update_kernel,
        out_shape=jax.ShapeDtypeStruct((2 * R, LINES), F32),
        in_specs=[vmem()] * 2,
        out_specs=vmem(),
        scratch_shapes=[pltpu.VMEM((SHARE, 128), F32)],
        name="update",
    )(map_t, every)
    return result.T[None]


def solution(mesh):
    placed = (
        P("half", "slab", None),
        P("half", "dom", None),
        P("half", "slab", None, "dom"),
        P("half", "slab", None, "dom"),
        P("half", "dom"),
        P("half", None, "dom"),
        P(),
    )
    return jax.shard_map(
        body, mesh=mesh, in_specs=placed, out_specs=P("half", "slab", None), check_vma=False
    )
```

time: 664 us -> 150 us (0.23)
  waiting for transfers between devices: 462 us -> 28.5 us
  other arithmetic: 105 us -> 1.06 us
  blocking collectives: 28.2 us -> 83.9 us
  local copies, waits for them, and re-layouts: 52.4 us -> 1.35 us
  Pallas kernels: 0 us -> 24.4 us
  between operations: 13.7 us -> 0.15 us
  starting transfers between devices: 1.95 us -> 10.7 us
    psum x2 -> x0, waiting for transfers between devices: 459 us -> none  [the longest x1 325 us: body(): grad = lax.psum(local_grad, 'dom')]
    all_to_all x0 -> x3, blocking collectives: none -> 83.9 us  [exchange(): return lax.all_to_all(value, axis, 0, 0, tiled=True)]
    scatter-add x8 -> x0, other arithmetic: 78.2 us -> none  [spread_back(): total.at[local].add(taps_wide[tap_num][:, None] * back_wide, mode='drop')]
    gather x8 -> x0, local copies, waits for them, and re-layouts: 40.5 us -> none  [body(): picked = jnp.take(map_low, taps_at[tap_num], axis=0)]
    psum x1 -> x0, blocking collectives: 28.2 us -> none  [body(): totals = lax.psum(shell_terms(cand, other, radii), 'slab')]
    all_to_all x0 -> x1, waiting for transfers between devices: none -> 27 us  [exchange(): return lax.all_to_all(value, axis, 0, 0, tiled=True)]
    pallas_call x0 -> x5, Pallas kernels: none -> 24.4 us  [the longest x1 12.6 us: body(): pl.pallas_call(image_kernel, out_shape=(jax.ShapeDtypeStruct((N_DOM, 2, T...]
    all_to_all x0 -> x1, starting transfers between devices: none -> 8.79 us  [exchange(): return lax.all_to_all(value, axis, 0, 0, tiled=True)]
  transfers between devices with their start and end apart: 3 -> 2, of which waited for: 3 -> 2; matrix products, arithmetic and copies ran while one was open for 1% -> 1% of each run, Pallas kernels for 0% -> 0%
where the time goes in v1:
time: 150 us
  blocking collectives  83.9 us (56%)
  waiting for transfers between devices  28.5 us (19%)
  Pallas kernels  24.4 us (16%)
  starting transfers between devices  10.7 us (7%)
    all_to_all x3, blocking collectives, exchange(): return lax.all_to_all(value, axis, 0, 0, tiled=True)  83.9 us
    all_to_all x1, waiting for transfers between devices, exchange(): return lax.all_to_all(value, axis, 0, 0, tiled=True)  27 us
    pallas_call x1, Pallas kernels, body(): pl.pallas_call(image_kernel, out_shape=(jax.ShapeDtypeStruct((N_DOM, 2, T...  12.6 us
    all_to_all x1, starting transfers between devices, exchange(): return lax.all_to_all(value, axis, 0, 0, tiled=True)  8.79 us
    pallas_call x1, Pallas kernels, body(): pl.pallas_call(update_kernel, out_shape=jax.ShapeDtypeStruct((2 * R, LINE...  5.22 us
  transfers between devices with their start and end apart: 2, of which 2 were waited for; matrix products, arithmetic and copies ran while one was open for 1% of the time, Pallas kernels for 0%

profile of v1, /device:TPU:8, one launch (start us, length us, event | category | flops | bytes accessed | tf_op | source)
XLA Modules:
  0.0 150.0 jit_solution(8075183802843251690)
XLA Ops:
  0.0 2.7 %pack.1 = bf16[8,64,1024]{2,1,0:T(8,128)(2,1)} custom-call(f32[400,1024]{1,0:T(8,128)} %bitcast.21, s32[8,1024]{1,0:T(8,128)} %bitcast.23, f32[8,1024]{1,0:T(8,128)} %bitcast.24), custom_call_target="tpu_custom_call" | custom-call | tf_op jit(solution)/shard_map/pack/pallas_call | solution.py:224
  2.7 8.8 %all-to-all-start = ((bf16[8,64,1024]{2,1,0:T(8,128)(2,1)}), bf16[8,64,1024]{2,1,0:T(8,128)(2,1)S(1)}, u32[]{:S(2)}, u32[]{:S(2)}) async-start(bf16[8,64,1024]{2,1,0:T(8,128)(2,1)} %pack.1), calls=%async_computation | async-start | bytes 2097152 | tf_op jit(solution)/shard_map/all_to_all | solution.py:201
  11.6 0.1 multiply_add_fusion
  11.7 0.1 add.52
  11.8 0.2 select_reduce_fusion
  12.0 0.1 sine_negate_fusion
  12.1 0.1 copy.8
  12.2 0.1 broadcast_in_dim.38
  12.3 0.1 reshape.64
  12.4 0.5 fusion
  13.1 0.1 pad_add_fusion.place_ref
  13.2 27.0 %all-to-all-done.packed_ref = bf16[8,64,1024]{2,1,0:T(8,128)(2,1)S(1)} async-done(((bf16[8,64,1024]{2,1,0:T(8,128)(2,1)}), bf16[8,64,1024]{2,1,0:T(8,128)(2,1)S(1)}, u32[]{:S(2)}, u32[]{:S(2)}) %all-to-all-start) | async-done | bytes 1048608 | tf_op jit(solution)/shard_map/all_to_all | solution.py:201
  40.2 12.6 %image.1 = (bf16[32,2,56,128]{3,2,1,0:T(8,128)(2,1)S(1)}, f32[2,64,128]{2,1,0:T(8,128)S(1)}) custom-call(s32[2]{0:T(128)S(1)} %pad_add_fusion.place_ref, bf16[8,64,1024]{2,1,0:T(8,128)(2,1)S(1)} %all-to-all-done.packed_ref, bf16[2,32,1024]{2,1,0:T(8,128)(2,1)S(1)} %pad.14.data_ref, f32[32,1024]{1,0:T(8,128)S(1)} %pad.15.ctf_ref, ...), custom_call_target="tpu_custom_call" | custom-call | tf_op jit(solution)/shard_map/image/pallas_call | solution.py:242
  52.8 0.0 copy-start.1
  52.8 36.7 %all_to_all.20.parts_ref = bf16[32,2,56,128]{3,2,1,0:T(8,128)(2,1)} all-to-all(bf16[32,2,56,128]{3,2,1,0:T(8,128)(2,1)S(1)} %get-tuple-element.9), channel_id=1, replica_groups=mesh['half'=2,'dom'=32,'slab'=8] {'dom'}, dimensions={0} | all-to-all | bytes 1835008 | tf_op jit(solution)/shard_map/all_to_all | solution.py:201
  89.5 2.0 %reduce.1 = (f32[2,64,128]{2,1,0:T(8,128)}, f32[2,64,128]{2,1,0:T(8,128)}) custom-call(bf16[32,2,56,128]{3,2,1,0:T(8,128)(2,1)} %all_to_all.20.parts_ref, f32[2,64,128]{2,1,0:T(8,128)} %copy-done.1), custom_call_target="tpu_custom_call" | custom-call | tf_op jit(solution)/shard_map/reduce/pallas_call | solution.py:262
  91.6 1.9 %collective-permute-start = (f32[2,64,128]{2,1,0:T(8,128)}, f32[2,64,128]{2,1,0:T(8,128)S(1)}, u32[]{:S(2)}, u32[]{:S(2)}) collective-permute-start(f32[2,64,128]{2,1,0:T(8,128)} %get-tuple-element.12.cand_ref), channel_id=1, source_target_pairs={{0,256},{256,0},{1,257},{257,1},{2,258},{258,2},{3,259},{259,3},{4... | collective-permute-start | bytes 196616 | tf_op jit(solution)/shard_map/ppermute | solution.py:270
  93.5 1.4 collective-permute-done.other_ref
  94.9 0.6 copy-done.2
  95.5 1.8 %shell.1 = bf16[8,16,128]{2,1,0:T(8,128)(2,1)} custom-call(f32[2,64,128]{2,1,0:T(8,128)} %get-tuple-element.11.grad_ref, f32[2,64,128]{2,1,0:T(8,128)} %get-tuple-element.12.cand_ref, f32[2,64,128]{2,1,0:T(8,128)} %copy-done.2), custom_call_target="tpu_custom_call" | custom-call | tf_op jit(solution)/shard_map/shell/pallas_call | solution.py:271
  97.3 14.0 %all_to_all.21 = bf16[8,16,128]{2,1,0:T(8,128)(2,1)S(1)} all-to-all(bf16[8,16,128]{2,1,0:T(8,128)(2,1)} %shell.1), channel_id=1, replica_groups=mesh['half'=2,'dom'=32,'slab'=8] {'slab'}, dimensions={0} | all-to-all | bytes 65536 | tf_op jit(solution)/shard_map/all_to_all | solution.py:201
  111.4 0.2 broadcast_in_dim.41
  111.6 33.1 %all_to_all.22.parts_ref = bf16[32,8,16,128]{3,2,1,0:T(8,128)(2,1)} all-to-all(bf16[32,8,16,128]{3,2,1,0:T(8,128)(2,1)S(1)} %broadcast_in_dim.41), channel_id=1, replica_groups=mesh['half'=2,'dom'=32,'slab'=8] {'dom'}, dimensions={0} | all-to-all | bytes 2097152 | tf_op jit(solution)/shard_map/all_to_all | solution.py:201
  144.7 5.2 %update.1 = f32[400,1024]{1,0:T(8,128)} custom-call(f32[400,1024]{1,0:T(8,128)} %bitcast.22, bf16[32,8,16,128]{3,2,1,0:T(8,128)(2,1)} %all_to_all.22.parts_ref), custom_call_target="tpu_custom_call" | custom-call | tf_op jit(solution)/shard_map/update/pallas_call | solution.py:281
  (19 shorter events, 0.2 us)
Async XLA Ops:
  0.0 13.0 %copy-start = (bf16[1,1024,400]{1,2,0:T(8,128)(2,1)S(1)}, bf16[1,1024,400]{1,2,0:T(8,128)(2,1)}, u32[]{:S(2)}) copy-start(bf16[1,1024,400]{1,2,0:T(8,128)(2,1)} %param.8) | copy-start | bytes 2457604
  2.7 8.8 %copy-start.3 = (s32[1,2,16]{2,1,0:T(2,128)S(1)}, s32[1,2,16]{2,1,0:T(2,128)}, u32[]{:S(2)}) copy-start(s32[1,2,16]{2,1,0:T(2,128)} %param.12) | copy-start | bytes 388
  2.7 9.0 %copy-start.4 = (f32[16]{0:T(128)S(1)}, f32[16]{0:T(128)}, u32[]{:S(2)}) copy-start(f32[16]{0:T(128)} %param.13) | copy-start | bytes 196
  2.7 9.0 %copy-start.5 = (s32[1,16]{1,0:T(1,128)S(1)}, s32[1,16]{1,0:T(1,128)}, u32[]{:S(2)}) copy-start(s32[1,16]{1,0:T(1,128)} %param.11) | copy-start | bytes 196
  2.7 37.5 %all-to-all-start = ((bf16[8,64,1024]{2,1,0:T(8,128)(2,1)}), bf16[8,64,1024]{2,1,0:T(8,128)(2,1)S(1)}, u32[]{:S(2)}, u32[]{:S(2)}) async-start(bf16[8,64,1024]{2,1,0:T(8,128)(2,1)} %pack.1), calls=%async_computation | async-start | bytes 2097152 | tf_op jit(solution)/shard_map/all_to_all | solution.py:201
  52.8 36.8 %copy-start.1 = (f32[2,64,128]{2,1,0:T(8,128)}, f32[2,64,128]{2,1,0:T(8,128)S(1)}, u32[]{:S(2)}) copy-start(f32[2,64,128]{2,1,0:T(8,128)S(1)} %get-tuple-element.10.own_ref) | copy-start | bytes 196612
  91.6 3.3 %collective-permute-start = (f32[2,64,128]{2,1,0:T(8,128)}, f32[2,64,128]{2,1,0:T(8,128)S(1)}, u32[]{:S(2)}, u32[]{:S(2)}) collective-permute-start(f32[2,64,128]{2,1,0:T(8,128)} %get-tuple-element.12.cand_ref), channel_id=1, source_target_pairs={{0,256},{256,0},{1,257},{257,1},{2,258},{258,2},{3,259},{259,3},{4... | collective-permute-start | bytes 196616 | tf_op jit(solution)/shard_map/ppermute | solution.py:270
  94.9 0.6 copy-start.2

commit v2 on v1

--- a/solution.py
+++ b/solution.py
@@ -197,8 +197,13 @@
     return pl.BlockSpec(memory_space=pltpu.VMEM)
 
 
+def limit(mib):
+    return pltpu.CompilerParams(vmem_limit_bytes=mib << 20)
+
+
 def exchange(value, axis):
-    return lax.all_to_all(value, axis, 0, 0, tiled=True)
+    flat = value.reshape(value.shape[0], -1, value.shape[-1])
+    return lax.all_to_all(flat, axis, 0, 0, tiled=True).reshape(value.shape)
 
 
 def line_terms(classes_local, shifts_local, defocus, radius):
@@ -227,6 +232,7 @@
         in_specs=[vmem()] * 3,
         out_specs=vmem(),
         scratch_shapes=[pltpu.VMEM((PACKED, LINES), F32)],
+        compiler_params=limit(6),
         name="pack",
     )(map_t, tap_index[0, 0], tap_weight[0, 0])
     packed = exchange(packed, "slab")
@@ -253,7 +259,7 @@
             pltpu.VMEM((TIGHT, ROWS), F32),
             pltpu.VMEM((N_SLAB, TIGHT, LINES), F32),
         ],
-        compiler_params=pltpu.CompilerParams(vmem_limit_bytes=48 << 20),
+        compiler_params=limit(32),
         name="image",
     )(place, packed, data, ctf, cosine, sine)
     parts = exchange(parts, "dom")
@@ -265,6 +271,7 @@
         in_specs=[vmem()] * 2,
         out_specs=(vmem(), vmem()),
         scratch_shapes=[pltpu.VMEM((2, TIGHT, 128), F32)],
+        compiler_params=limit(4),
         name="reduce",
     )(parts, own)
     other = lax.ppermute(cand, "half", [(0, 1), (1, 0)])
@@ -274,6 +281,7 @@
         in_specs=[vmem()] * 3,
         out_specs=vmem(),
         scratch_shapes=[pltpu.VMEM((2, PACKED, 128), F32)],
+        compiler_params=limit(2),
         name="shell",
     )(grad, cand, other)
     share = exchange(share, "slab")
@@ -284,6 +292,7 @@
         in_specs=[vmem()] * 2,
         out_specs=vmem(),
         scratch_shapes=[pltpu.VMEM((SHARE, 128), F32)],
+        compiler_params=limit(8),
         name="update",
     )(map_t, every)
     return result.T[None]

time: 150 us -> 146 us (0.973)
  Pallas kernels: 24.4 us -> 17.8 us
  local copies, waits for them, and re-layouts: 1.35 us -> 3.74 us
    unnamed x12 -> x16, local copies, waits for them, and re-layouts: 0.65 us -> 3.04 us
    pallas_call x1, Pallas kernels: 2.01 us -> 0.19 us  [body(): pl.pallas_call(reduce_kernel, out_shape=(block, block), in_specs=[vmem()]...]
    pallas_call x1, Pallas kernels: 5.22 us -> 3.5 us  [body(): pl.pallas_call(update_kernel, out_shape=jax.ShapeDtypeStruct((2 * R, LINE...]
    pallas_call x1, Pallas kernels: 2.74 us -> 1.21 us  [body(): pl.pallas_call(pack_kernel, out_shape=jax.ShapeDtypeStruct((N_SLAB, PACKE...]
    pallas_call x1, Pallas kernels: 1.82 us -> 0.3 us  [body(): pl.pallas_call(shell_kernel, out_shape=jax.ShapeDtypeStruct((N_SLAB, 16,...]
where the time goes in v2:
time: 146 us; the launch traced here: 145 us
  blocking collectives  83.6 us (57%)
  waiting for transfers between devices  28.2 us (19%)
  Pallas kernels  17.8 us (12%)
  starting transfers between devices  10.7 us (7%)
  local copies, waits for them, and re-layouts  3.74 us (3%)
    all_to_all x3, blocking collectives, exchange(): return lax.all_to_all(flat, axis, 0, 0, tiled=True).reshape(value.shape)  83.6 us
    all_to_all x1, waiting for transfers between devices, exchange(): return lax.all_to_all(flat, axis, 0, 0, tiled=True).reshape(value.shape)  27 us
    pallas_call x1, Pallas kernels, body(): pl.pallas_call(image_kernel, out_shape=(jax.ShapeDtypeStruct((N_DOM, 2, T...  12.6 us
    all_to_all x1, starting transfers between devices, exchange(): return lax.all_to_all(flat, axis, 0, 0, tiled=True).reshape(value.shape)  8.79 us
    pallas_call x1, Pallas kernels, body(): pl.pallas_call(update_kernel, out_shape=jax.ShapeDtypeStruct((2 * R, LINE...  3.5 us
    unnamed x16, local copies, waits for them, and re-layouts  3.04 us
  transfers between devices with their start and end apart: 2, of which 2 were waited for; matrix products, arithmetic and copies ran while one was open for 1% of the time, Pallas kernels for 0%

profile of v2, /device:TPU:8, one launch (start us, length us, event | category | flops | bytes accessed | tf_op | source)
XLA Modules:
  0.0 145.3 jit_solution(2438169314679443189)
XLA Ops:
  0.0 1.5 %copy-done.1 = f32[1,1024,400]{1,2,0:T(8,128)S(1)} copy-done((f32[1,1024,400]{1,2,0:T(8,128)S(1)}, f32[1,1024,400]{1,2,0:T(8,128)}, u32[]{:S(2)}) %copy-start.1) | copy-done | bytes 1638424
  1.5 0.8 copy-done.3
  2.3 0.8 copy-done.4
  3.0 1.2 pack.1
  4.2 8.8 %all-to-all-start = ((bf16[8,64,1024]{2,1,0:T(8,128)(2,1)}), bf16[8,64,1024]{2,1,0:T(8,128)(2,1)S(1)}, u32[]{:S(2)}, u32[]{:S(2)}) async-start(bf16[8,64,1024]{2,1,0:T(8,128)(2,1)} %pack.1), calls=%async_computation | async-start | bytes 2097152 | tf_op jit(solution)/shard_map/all_to_all | solution.py:206
  13.1 0.1 multiply_add_fusion
  13.3 0.2 select_reduce_fusion
  13.5 0.1 sine_negate_fusion
  13.6 0.1 copy.8
  13.7 0.1 broadcast_in_dim.40
  13.8 0.1 reshape.76
  13.9 0.5 fusion
  14.6 0.1 pad_add_fusion.place_ref
  14.7 27.0 %all-to-all-done.packed_ref = bf16[8,64,1024]{2,1,0:T(8,128)(2,1)S(1)} async-done(((bf16[8,64,1024]{2,1,0:T(8,128)(2,1)}), bf16[8,64,1024]{2,1,0:T(8,128)(2,1)S(1)}, u32[]{:S(2)}, u32[]{:S(2)}) %all-to-all-start) | async-done | bytes 1048608 | tf_op jit(solution)/shard_map/all_to_all | solution.py:206
  41.7 12.6 %image.1 = (bf16[32,2,56,128]{3,2,1,0:T(8,128)(2,1)S(1)}, f32[2,64,128]{2,1,0:T(8,128)S(1)}) custom-call(s32[2]{0:T(128)S(1)} %pad_add_fusion.place_ref, bf16[8,64,1024]{2,1,0:T(8,128)(2,1)S(1)} %all-to-all-done.packed_ref, bf16[2,32,1024]{2,1,0:T(8,128)(2,1)S(1)} %pad.14.data_ref, f32[32,1024]{1,0:T(8,128)S(1)} %pad.15.ctf_ref, ...), custom_call_target="tpu_custom_call" | custom-call | tf_op jit(solution)/shard_map/image/pallas_call | solution.py:248
  54.3 36.6 %all_to_all.20 = bf16[32,112,128]{2,1,0:T(8,128)(2,1)S(1)} all-to-all(bf16[32,112,128]{2,1,0:T(8,128)(2,1)S(1)} %bitcast.29), channel_id=1, replica_groups=mesh['half'=2,'dom'=32,'slab'=8] {'dom'}, dimensions={0} | all-to-all | bytes 1835008 | tf_op jit(solution)/shard_map/all_to_all | solution.py:206
  90.9 0.2 reduce.1
  91.1 1.9 %collective-permute-start = (f32[2,64,128]{2,1,0:T(8,128)S(1)}, f32[2,64,128]{2,1,0:T(8,128)S(1)}, u32[]{:S(2)}, u32[]{:S(2)}) collective-permute-start(f32[2,64,128]{2,1,0:T(8,128)S(1)} %get-tuple-element.12.cand_ref), channel_id=1, source_target_pairs={{0,256},{256,0},{1,257},{257,1},{2,258},{258,2},{3,259},{259,3},{4... | collective-permute-start | bytes 196616 | tf_op jit(solution)/shard_map/ppermute | solution.py:277
  93.0 1.2 collective-permute-done.other_ref
  94.3 0.3 shell.1
  94.6 14.0 %all_to_all.21 = bf16[8,16,128]{2,1,0:T(8,128)(2,1)S(1)} all-to-all(bf16[8,16,128]{2,1,0:T(8,128)(2,1)S(1)} %shell.1), channel_id=1, replica_groups=mesh['half'=2,'dom'=32,'slab'=8] {'slab'}, dimensions={0} | all-to-all | bytes 65536 | tf_op jit(solution)/shard_map/all_to_all | solution.py:206
  108.5 0.2 broadcast_in_dim.44
  108.8 33.0 %all_to_all.22 = bf16[32,128,128]{2,1,0:T(8,128)(2,1)S(1)} all-to-all(bf16[32,128,128]{2,1,0:T(8,128)(2,1)S(1)} %broadcast_in_dim.44), channel_id=1, replica_groups=mesh['half'=2,'dom'=32,'slab'=8] {'dom'}, dimensions={0} | all-to-all | bytes 2097152 | tf_op jit(solution)/shard_map/all_to_all | solution.py:206
  141.8 3.5 %update.1 = f32[400,1024]{1,0:T(8,128)} custom-call(f32[400,1024]{1,0:T(8,128)S(1)} %bitcast.26, bf16[32,8,16,128]{3,2,1,0:T(8,128)(2,1)S(1)} %bitcast.27), custom_call_target="tpu_custom_call" | custom-call | tf_op jit(solution)/shard_map/update/pallas_call | solution.py:289
  (23 shorter events, 0.3 us)
Async XLA Ops:
  0.0 14.5 %copy-start = (bf16[1,1024,400]{1,2,0:T(8,128)(2,1)S(1)}, bf16[1,1024,400]{1,2,0:T(8,128)(2,1)}, u32[]{:S(2)}) copy-start(bf16[1,1024,400]{1,2,0:T(8,128)(2,1)} %param.8) | copy-start | bytes 2457604
  0.0 1.5 %copy-start.1 = (f32[1,1024,400]{1,2,0:T(8,128)S(1)}, f32[1,1024,400]{1,2,0:T(8,128)}, u32[]{:S(2)}) copy-start(f32[1,1024,400]{1,2,0:T(8,128)} %param.7) | copy-start | bytes 4915204
  1.5 0.8 copy-start.3
  2.3 0.8 copy-start.4
  4.2 8.8 %copy-start.5 = (s32[1,2,16]{2,1,0:T(2,128)S(1)}, s32[1,2,16]{2,1,0:T(2,128)}, u32[]{:S(2)}) copy-start(s32[1,2,16]{2,1,0:T(2,128)} %param.12) | copy-start | bytes 388
  4.2 9.0 %copy-start.6 = (f32[16]{0:T(128)S(1)}, f32[16]{0:T(128)}, u32[]{:S(2)}) copy-start(f32[16]{0:T(128)} %param.13) | copy-start | bytes 196
  4.2 9.0 %copy-start.7 = (s32[1,16]{1,0:T(1,128)S(1)}, s32[1,16]{1,0:T(1,128)}, u32[]{:S(2)}) copy-start(s32[1,16]{1,0:T(1,128)} %param.11) | copy-start | bytes 196
  4.2 37.5 %all-to-all-start = ((bf16[8,64,1024]{2,1,0:T(8,128)(2,1)}), bf16[8,64,1024]{2,1,0:T(8,128)(2,1)S(1)}, u32[]{:S(2)}, u32[]{:S(2)}) async-start(bf16[8,64,1024]{2,1,0:T(8,128)(2,1)} %pack.1), calls=%async_computation | async-start | bytes 2097152 | tf_op jit(solution)/shard_map/all_to_all | solution.py:206
  91.1 3.1 %collective-permute-start = (f32[2,64,128]{2,1,0:T(8,128)S(1)}, f32[2,64,128]{2,1,0:T(8,128)S(1)}, u32[]{:S(2)}, u32[]{:S(2)}) collective-permute-start(f32[2,64,128]{2,1,0:T(8,128)S(1)} %get-tuple-element.12.cand_ref), channel_id=1, source_target_pairs={{0,256},{256,0},{1,257},{257,1},{2,258},{258,2},{3,259},{259,3},{4... | collective-permute-start | bytes 196616 | tf_op jit(solution)/shard_map/ppermute | solution.py:277
  94.6 47.2 %copy-start.2 = (f32[1,1024,400]{1,2,0:T(8,128)S(1)}, f32[1,1024,400]{1,2,0:T(8,128)}, u32[]{:S(2)}) copy-start(f32[1,1024,400]{1,2,0:T(8,128)} %param.7) | copy-start | bytes 4915204

commit v3 on v2

--- a/solution.py
+++ b/solution.py
@@ -164,7 +164,7 @@
             out_ref[4 * half + slot] = regroup(tiles, slot, group).astype(BF16)
 
 
-def update_kernel(map_ref, parts_ref, out_ref, scale):
+def update_kernel(side_ref, map_ref, parts_ref, out_ref, scale):
     sums = jnp.zeros((N_SLAB, 16, 128), F32)
     for index in range(N_DOM):
         sums += parts_ref[index].astype(F32)
@@ -201,9 +201,12 @@
     return pltpu.CompilerParams(vmem_limit_bytes=mib << 20)
 
 
-def exchange(value, axis):
+def exchange(value, axis, side):
     flat = value.reshape(value.shape[0], -1, value.shape[-1])
-    return lax.all_to_all(flat, axis, 0, 0, tiled=True).reshape(value.shape)
+    flat, side = lax.optimization_barrier((flat, side))
+    moved = lax.all_to_all(flat, axis, 0, 0, tiled=True)
+    moved, side = lax.optimization_barrier((moved, side * 0.5))
+    return moved.reshape(value.shape), side
 
 
 def line_terms(classes_local, shifts_local, defocus, radius):
@@ -235,7 +238,7 @@
         compiler_params=limit(6),
         name="pack",
     )(map_t, tap_index[0, 0], tap_weight[0, 0])
-    packed = exchange(packed, "slab")
+    packed, side = exchange(packed, "slab", defocus[:1])
 
     pad = ((0, IM - RB), (0, 0))
     radius = (RB * slab + jnp.arange(RB)).astype(F32)
@@ -262,7 +265,7 @@
         compiler_params=limit(32),
         name="image",
     )(place, packed, data, ctf, cosine, sine)
-    parts = exchange(parts, "dom")
+    parts, side = exchange(parts, "dom", side)
 
     block = jax.ShapeDtypeStruct((2, PACKED, 128), F32)
     grad, cand = pl.pallas_call(
@@ -284,17 +287,17 @@
         compiler_params=limit(2),
         name="shell",
     )(grad, cand, other)
-    share = exchange(share, "slab")
-    every = exchange(jnp.broadcast_to(share[None], (N_DOM,) + share.shape), "dom")
+    share, side = exchange(share, "slab", side)
+    every, side = exchange(jnp.broadcast_to(share[None], (N_DOM,) + share.shape), "dom", side)
     result = pl.pallas_call(
         update_kernel,
         out_shape=jax.ShapeDtypeStruct((2 * R, LINES), F32),
-        in_specs=[vmem()] * 2,
+        in_specs=[pl.BlockSpec(memory_space=pltpu.SMEM)] + [vmem()] * 2,
         out_specs=vmem(),
         scratch_shapes=[pltpu.VMEM((SHARE, 128), F32)],
         compiler_params=limit(8),
         name="update",
-    )(map_t, every)
+    )(side, map_t, every)
     return result.T[None]
 
 

time: 146 us -> 149 us (1.021)
  blocking collectives: 83.6 us -> 0 us
  waiting for transfers between devices: 28.2 us -> 89 us
  starting transfers between devices: 10.7 us -> 34.1 us
  Pallas kernels: 17.8 us -> 19.3 us
    all_to_all x3 -> x0, blocking collectives: 83.6 us -> none  [exchange(): return lax.all_to_all(flat, axis, 0, 0, tiled=True).reshape(value.shape)]
    all_to_all x1 -> x4, waiting for transfers between devices: 27 us -> 87.8 us  [exchange(): moved = lax.all_to_all(flat, axis, 0, 0, tiled=True)]
    all_to_all x1 -> x4, starting transfers between devices: 8.79 us -> 32.2 us  [exchange(): moved = lax.all_to_all(flat, axis, 0, 0, tiled=True)]
  transfers between devices with their start and end apart: 2 -> 5, of which waited for: 2 -> 5; matrix products, arithmetic and copies ran while one was open for 1% -> 1% of each run, Pallas kernels for 0% -> 0%
where the time goes in v3:
time: 149 us; the launch traced here: 148 us
  waiting for transfers between devices  89 us (60%)
  starting transfers between devices  34.1 us (23%)
  Pallas kernels  19.3 us (13%)
  local copies, waits for them, and re-layouts  4.72 us (3%)
    all_to_all x4, waiting for transfers between devices, exchange(): moved = lax.all_to_all(flat, axis, 0, 0, tiled=True)  87.8 us
    all_to_all x4, starting transfers between devices, exchange(): moved = lax.all_to_all(flat, axis, 0, 0, tiled=True)  32.2 us
    pallas_call x1, Pallas kernels, body(): pl.pallas_call(image_kernel, out_shape=(jax.ShapeDtypeStruct((N_DOM, 2, T...  13.5 us
    pallas_call x1, Pallas kernels, body(): pl.pallas_call(update_kernel, out_shape=jax.ShapeDtypeStruct((2 * R, LINE...  3.5 us
    unnamed x16, local copies, waits for them, and re-layouts  3.04 us
  transfers between devices with their start and end apart: 5, of which 5 were waited for; matrix products, arithmetic and copies ran while one was open for 1% of the time, Pallas kernels for 0%

profile of v3, /device:TPU:8, one launch (start us, length us, event | category | flops | bytes accessed | tf_op | source)
XLA Modules:
  0.0 148.4 jit_solution(1160077805157817097)
XLA Ops:
  0.0 1.5 %copy-done.1 = f32[1,1024,400]{1,2,0:T(8,128)S(1)} copy-done((f32[1,1024,400]{1,2,0:T(8,128)S(1)}, f32[1,1024,400]{1,2,0:T(8,128)}, u32[]{:S(2)}) %copy-start.1) | copy-done | bytes 1638424
  1.5 0.8 copy-done.3
  2.3 0.8 copy-done.4
  3.0 1.2 pack.1
  4.2 8.8 %all-to-all-start = ((bf16[8,64,1024]{2,1,0:T(8,128)(2,1)}), bf16[8,64,1024]{2,1,0:T(8,128)(2,1)S(1)}, u32[]{:S(2)}, u32[]{:S(2)}) async-start(bf16[8,64,1024]{2,1,0:T(8,128)(2,1)} %pack.1), calls=%async_computation | async-start | bytes 2097152 | tf_op jit(solution)/shard_map/all_to_all | solution.py:207
  13.3 0.2 select_reduce_fusion
  13.5 0.1 sine_negate_fusion
  13.7 0.1 broadcast_in_dim.40
  13.8 0.1 reshape.76
  13.9 0.5 fusion
  14.7 27.0 %all-to-all-done.packed_ref = bf16[8,64,1024]{2,1,0:T(8,128)(2,1)S(1)} async-done(((bf16[8,64,1024]{2,1,0:T(8,128)(2,1)}), bf16[8,64,1024]{2,1,0:T(8,128)(2,1)S(1)}, u32[]{:S(2)}, u32[]{:S(2)}) %all-to-all-start) | async-done | bytes 1048608 | tf_op jit(solution)/shard_map/all_to_all | solution.py:207
  41.7 13.5 %image.1 = (bf16[32,2,56,128]{3,2,1,0:T(8,128)(2,1)}, f32[2,64,128]{2,1,0:T(8,128)S(1)}) custom-call(s32[2]{0:T(128)S(1)} %pad_add_fusion.place_ref, bf16[8,64,1024]{2,1,0:T(8,128)(2,1)S(1)} %all-to-all-done.packed_ref, bf16[2,32,1024]{2,1,0:T(8,128)(2,1)S(1)} %pad.14.data_ref, f32[32,1024]{1,0:T(8,128)S(1)} %pad.15.ctf_ref, f32[32,1024]{1,0:T(8,128)S(1)} %pad.16.cos_ref, ...), custom_call_target="tpu_custom_call" | custom-call | tf_op jit(solution)/shard_map/image/pallas_call | solution.py:251
  55.2 12.8 %all-to-all-start.1 = ((bf16[32,112,128]{2,1,0:T(8,128)(2,1)}), bf16[32,112,128]{2,1,0:T(8,128)(2,1)S(1)}, u32[]{:S(2)}, u32[]{:S(2)}) async-start(bf16[32,112,128]{2,1,0:T(8,128)(2,1)} %bitcast.12), calls=%async_computation.1 | async-start | bytes 1835008 | tf_op jit(solution)/shard_map/all_to_all | solution.py:207
  68.0 24.0 %all-to-all-done.1 = bf16[32,112,128]{2,1,0:T(8,128)(2,1)S(1)} async-done(((bf16[32,112,128]{2,1,0:T(8,128)(2,1)}), bf16[32,112,128]{2,1,0:T(8,128)(2,1)S(1)}, u32[]{:S(2)}, u32[]{:S(2)}) %all-to-all-start.1) | async-done | bytes 917536 | tf_op jit(solution)/shard_map/all_to_all | solution.py:207
  92.0 0.2 reduce.1
  92.2 1.9 %collective-permute-start = (f32[2,64,128]{2,1,0:T(8,128)S(1)}, f32[2,64,128]{2,1,0:T(8,128)S(1)}, u32[]{:S(2)}, u32[]{:S(2)}) collective-permute-start(f32[2,64,128]{2,1,0:T(8,128)S(1)} %get-tuple-element.35.cand_ref), channel_id=1, source_target_pairs={{0,256},{256,0},{1,257},{257,1},{2,258},{258,2},{3,259},{259,3},{4... | collective-permute-start | bytes 196616 | tf_op jit(solution)/shard_map/ppermute | solution.py:280
  94.1 1.2 collective-permute-done.other_ref
  95.4 0.9 shell.1
  96.3 4.0 %all-to-all-start.2 = ((bf16[8,16,128]{2,1,0:T(8,128)(2,1)}), bf16[8,16,128]{2,1,0:T(8,128)(2,1)S(1)}, u32[]{:S(2)}, u32[]{:S(2)}) async-start(bf16[8,16,128]{2,1,0:T(8,128)(2,1)} %shell.1), calls=%async_computation.2 | async-start | bytes 65536 | tf_op jit(solution)/shard_map/all_to_all | solution.py:207
  100.3 10.2 %all-to-all-done.2 = bf16[8,16,128]{2,1,0:T(8,128)(2,1)S(1)} async-done(((bf16[8,16,128]{2,1,0:T(8,128)(2,1)}), bf16[8,16,128]{2,1,0:T(8,128)(2,1)S(1)}, u32[]{:S(2)}, u32[]{:S(2)}) %all-to-all-start.2) | async-done | bytes 32800 | tf_op jit(solution)/shard_map/all_to_all | solution.py:207
  110.4 1.2 broadcast_in_dim.44
  111.6 6.6 %all-to-all-start.3 = ((bf16[32,128,128]{2,1,0:T(8,128)(2,1)}), bf16[32,128,128]{2,1,0:T(8,128)(2,1)S(1)}, u32[]{:S(2)}, u32[]{:S(2)}) async-start(bf16[32,128,128]{2,1,0:T(8,128)(2,1)} %broadcast_in_dim.44), calls=%async_computation.3 | async-start | bytes 2097152 | tf_op jit(solution)/shard_map/all_to_all | solution.py:207
  118.3 26.6 %all-to-all-done.3 = bf16[32,128,128]{2,1,0:T(8,128)(2,1)S(1)} async-done(((bf16[32,128,128]{2,1,0:T(8,128)(2,1)}), bf16[32,128,128]{2,1,0:T(8,128)(2,1)S(1)}, u32[]{:S(2)}, u32[]{:S(2)}) %all-to-all-start.3) | async-done | bytes 1048608 | tf_op jit(solution)/shard_map/all_to_all | solution.py:207
  144.9 3.5 %update.1 = f32[400,1024]{1,0:T(8,128)} custom-call(f32[1]{0:T(128)S(6)} %mul.91.side_ref, f32[400,1024]{1,0:T(8,128)S(1)} %bitcast.27, bf16[32,8,16,128]{3,2,1,0:T(8,128)(2,1)S(1)} %bitcast.28), custom_call_target="tpu_custom_call" | custom-call | tf_op jit(solution)/shard_map/update/pallas_call | solution.py:292
  (26 shorter events, 0.5 us)
Async XLA Ops:
  0.0 14.5 %copy-start = (bf16[1,1024,400]{1,2,0:T(8,128)(2,1)S(1)}, bf16[1,1024,400]{1,2,0:T(8,128)(2,1)}, u32[]{:S(2)}) copy-start(bf16[1,1024,400]{1,2,0:T(8,128)(2,1)} %param.8) | copy-start | bytes 2457604
  0.0 1.5 %copy-start.1 = (f32[1,1024,400]{1,2,0:T(8,128)S(1)}, f32[1,1024,400]{1,2,0:T(8,128)}, u32[]{:S(2)}) copy-start(f32[1,1024,400]{1,2,0:T(8,128)} %param.7) | copy-start | bytes 4915204
  1.5 0.8 copy-start.3
  2.3 0.8 copy-start.4
  4.2 8.8 %copy-start.5 = (s32[1,2,16]{2,1,0:T(2,128)S(1)}, s32[1,2,16]{2,1,0:T(2,128)}, u32[]{:S(2)}) copy-start(s32[1,2,16]{2,1,0:T(2,128)} %param.12) | copy-start | bytes 388
  4.2 9.0 %copy-start.6 = (s32[1,16]{1,0:T(1,128)S(1)}, s32[1,16]{1,0:T(1,128)}, u32[]{:S(2)}) copy-start(s32[1,16]{1,0:T(1,128)} %param.11) | copy-start | bytes 196
  4.2 9.0 %copy-start.7 = (f32[16]{0:T(128)S(1)}, f32[16]{0:T(128)}, u32[]{:S(2)}) copy-start(f32[16]{0:T(128)} %param.13) | copy-start | bytes 196
  4.2 37.5 %all-to-all-start = ((bf16[8,64,1024]{2,1,0:T(8,128)(2,1)}), bf16[8,64,1024]{2,1,0:T(8,128)(2,1)S(1)}, u32[]{:S(2)}, u32[]{:S(2)}) async-start(bf16[8,64,1024]{2,1,0:T(8,128)(2,1)} %pack.1), calls=%async_computation | async-start | bytes 2097152 | tf_op jit(solution)/shard_map/all_to_all | solution.py:207
  55.2 36.8 %all-to-all-start.1 = ((bf16[32,112,128]{2,1,0:T(8,128)(2,1)}), bf16[32,112,128]{2,1,0:T(8,128)(2,1)S(1)}, u32[]{:S(2)}, u32[]{:S(2)}) async-start(bf16[32,112,128]{2,1,0:T(8,128)(2,1)} %bitcast.12), calls=%async_computation.1 | async-start | bytes 1835008 | tf_op jit(solution)/shard_map/all_to_all | solution.py:207
  92.2 3.1 %collective-permute-start = (f32[2,64,128]{2,1,0:T(8,128)S(1)}, f32[2,64,128]{2,1,0:T(8,128)S(1)}, u32[]{:S(2)}, u32[]{:S(2)}) collective-permute-start(f32[2,64,128]{2,1,0:T(8,128)S(1)} %get-tuple-element.35.cand_ref), channel_id=1, source_target_pairs={{0,256},{256,0},{1,257},{257,1},{2,258},{258,2},{3,259},{259,3},{4... | collective-permute-start | bytes 196616 | tf_op jit(solution)/shard_map/ppermute | solution.py:280
  96.3 48.6 %copy-start.2 = (f32[1,1024,400]{1,2,0:T(8,128)S(1)}, f32[1,1024,400]{1,2,0:T(8,128)}, u32[]{:S(2)}) copy-start(f32[1,1024,400]{1,2,0:T(8,128)} %param.7) | copy-start | bytes 4915204
  96.3 14.2 %all-to-all-start.2 = ((bf16[8,16,128]{2,1,0:T(8,128)(2,1)}), bf16[8,16,128]{2,1,0:T(8,128)(2,1)S(1)}, u32[]{:S(2)}, u32[]{:S(2)}) async-start(bf16[8,16,128]{2,1,0:T(8,128)(2,1)} %shell.1), calls=%async_computation.2 | async-start | bytes 65536 | tf_op jit(solution)/shard_map/all_to_all | solution.py:207
  111.6 33.2 %all-to-all-start.3 = ((bf16[32,128,128]{2,1,0:T(8,128)(2,1)}), bf16[32,128,128]{2,1,0:T(8,128)(2,1)S(1)}, u32[]{:S(2)}, u32[]{:S(2)}) async-start(bf16[32,128,128]{2,1,0:T(8,128)(2,1)} %broadcast_in_dim.44), calls=%async_computation.3 | async-start | bytes 2097152 | tf_op jit(solution)/shard_map/all_to_all | solution.py:207

commit v4 on v3

v4 whole, which is shorter than its diff:
```python
import math

import jax
import jax.numpy as jnp
from jax import lax
from jax.experimental import pallas as pl
from jax.experimental.pallas import tpu as pltpu
from jax.sharding import PartitionSpec as P

LPI = 64
CTF_GAIN = 30.0
PHASE_ZERO = 0.1
STEP_SCALE = 0.5

R = 200
K = 8
N_SLAB = 8
N_X = 4
N_DOM = 32
LINES = 1024
ROWS = 1024
RB = R // N_X
SHARE = LINES // N_DOM
FOLD = RB // 2
STEP = STEP_SCALE / math.sqrt(ROWS * N_DOM * K / LINES)

F32 = jnp.float32
BF16 = jnp.bfloat16

IM = 56
BLOCK = 112
SENT = BLOCK + 8
TIGHT = 104
TAP_ROWS = (50, 51, 52, 53, 54, 55, 106, 107)
HIGH_ROW = 108
LOW_ROW = 109
SUM_ROWS = (50, 106)
CHUNK = 16


def lane_group(shape):
    return lax.broadcasted_iota(jnp.int32, shape, len(shape) - 1) // SHARE


def regroup(tiles, source, group):
    out = None
    for slot, tile in enumerate(tiles):
        moved = pltpu.roll(tile, (SHARE * (slot - source)) % 128, 1)
        out = moved if out is None else jnp.where(group == slot, moved, out)
    return out


def build_taps(taps, weights, high, low):
    line = lax.broadcasted_iota(jnp.int32, (CHUNK, ROWS), 0).astype(F32)
    first = jnp.zeros((CHUNK, ROWS), F32)
    second = jnp.zeros((CHUNK, ROWS), F32)
    for tap in range(K):
        first += jnp.where(line == low + tap, weights[tap], 0.0)
        second += jnp.where(line + CHUNK == low + tap, weights[tap], 0.0)
    first = first.astype(BF16)
    second = second.astype(BF16)
    high = jnp.broadcast_to(high, (CHUNK, ROWS)).astype(BF16)
    none = jnp.zeros((CHUNK, ROWS), BF16)
    before = None
    for chunk in range(LINES // CHUNK):
        here = high == jnp.asarray(chunk, BF16)
        value = jnp.where(here, first, none)
        if before is not None:
            value = jnp.where(before, second, value)
        taps[CHUNK * chunk : CHUNK * (chunk + 1), :] = value
        before = here


def project_kernel(place_ref, index_ref, weight_ref, map_hbm, out_ref, map_ref, block, taps, arrived):
    copy = pltpu.make_async_copy(map_hbm, map_ref, arrived)
    copy.start()
    index = index_ref[...]
    weight = weight_ref[...]
    base = jnp.min(index, axis=0, keepdims=True)
    place = lax.broadcasted_iota(jnp.int32, index.shape, 0)
    ordered = jnp.zeros(weight.shape, F32)
    for tap in range(K):
        ordered += jnp.where(place == index[tap : tap + 1] - base, weight[tap : tap + 1], 0.0)
    high = (base >> 4).astype(F32)
    low = (base & 15).astype(F32)
    weights = [ordered[tap : tap + 1] for tap in range(K)]
    build_taps(taps, weights, high, low)
    copy.wait()

    z = pl.multiple_of(place_ref[0] * 128, 128)
    y = place_ref[1]
    group = lane_group((8, 128))
    for part in range(N_X):
        at = BLOCK * part
        block[at + RB : at + IM, :] = jnp.zeros((IM - RB, LINES), F32)
        block[at + IM + RB : at + BLOCK, :] = jnp.zeros((IM - RB, LINES), F32)
        block[at : at + RB, :] = map_ref[RB * part : RB * (part + 1), :]
        block[at + IM : at + IM + RB, :] = map_ref[R + RB * part : R + RB * (part + 1), :]
        for lanes in range(LINES // 128):
            own = jnp.zeros((8, 128), F32)
            for slot in range(4):
                eight = 4 * lanes + slot
                if eight < BLOCK // 8:
                    tile = block[at + 8 * eight : at + 8 * eight + 8, pl.ds(z, 128)]
                    moved = pltpu.roll(tile, (SHARE * (slot - y)) & 127, 1)
                    own = jnp.where(group == slot, moved, own)
            out_ref[part, BLOCK:, 128 * lanes : 128 * (lanes + 1)] = own.astype(BF16)
    block[...] = jnp.dot(block[...].astype(BF16), taps[...], preferred_element_type=F32)
    for part in range(N_X):
        at = BLOCK * part
        for row, value in zip(TAP_ROWS + (HIGH_ROW, LOW_ROW), weights + [high, low], strict=True):
            block[at + row : at + row + 1, :] = value
        out_ref[part, :BLOCK, :] = block[at : at + BLOCK, :].astype(BF16)


def gather_kernel(parts_ref, mine_ref, low_ref, own_ref):
    total = parts_ref[0, :BLOCK].astype(F32)
    for part in range(1, N_X):
        total += parts_ref[part, :BLOCK].astype(F32)
    mine_ref[...] = total
    low_ref[...] = total.astype(BF16)
    group = lane_group((8, 128))
    for eight in range(BLOCK // 8):
        lanes = 128 * (eight // 4)
        tiles = [parts_ref[part, BLOCK:, lanes : lanes + 128].astype(F32) for part in range(N_X)]
        own_ref[8 * eight : 8 * eight + 8, :] = regroup(tiles, eight % 4, group)


def taps_kernel(parts_ref, taps_ref):
    @pl.loop(0, N_X)
    def _(part):
        rows = parts_ref[part].astype(F32)
        weights = [rows[row : row + 1] for row in TAP_ROWS]
        build_taps(taps_ref.at[part], weights, rows[HIGH_ROW : HIGH_ROW + 1], rows[LOW_ROW : LOW_ROW + 1])


def back_kernel(mine_ref, other_ref, data_ref, ctf_ref, cos_ref, sin_ref, taps_ref, out_ref, back, grad):
    ctf = ctf_ref[...]
    cosine = cos_ref[...]
    sine = sin_ref[...]
    proj = mine_ref[...] + other_ref[...].astype(F32)
    proj_re = proj[:IM]
    proj_im = proj[IM:]
    res_re = ctf * (cosine * proj_re - sine * proj_im) - data_ref[0].astype(F32)
    res_im = ctf * (sine * proj_re + cosine * proj_im) - data_ref[1].astype(F32)
    back_re = ctf * (cosine * res_re + sine * res_im)
    back_im = ctf * (cosine * res_im - sine * res_re)
    back[2 * RB :, :] = jnp.zeros((TIGHT - 2 * RB, ROWS), F32)
    back[:RB, :] = back_re[:RB]
    back[RB : 2 * RB, :] = back_im[:RB]
    back_low = back[...].astype(BF16)

    @pl.loop(0, N_X)
    def _(part):
        grad[part] = lax.dot_general(back_low, taps_ref[part], (((1,), (1,)), ((), ())), preferred_element_type=F32)

    group = lane_group((TIGHT, 128))
    for z in range(8):
        tiles = [grad[part, :, 128 * z : 128 * (z + 1)] for part in range(N_X)]
        for y in range(4):
            out_ref[4 * z + y] = regroup(tiles, y, group).astype(BF16)


def reduce_kernel(parts_ref, own_ref, grad_ref, cand_ref, total):
    total[...] = jnp.sum(parts_ref[...].astype(F32), axis=0)
    grad_ref[...] = jnp.zeros(grad_ref.shape, F32)
    grad_ref[:RB, :] = total[:RB, :]
    grad_ref[IM : IM + RB, :] = total[RB : 2 * RB, :]
    row = lax.broadcasted_iota(jnp.int32, cand_ref.shape, 0) % IM
    cand_ref[...] = jnp.where(row < RB, own_ref[...] - STEP * grad_ref[...], 0.0)


def split(value):
    high = value.astype(BF16).astype(F32)
    return high, value - high


def shell_kernel(grad_ref, cand_ref, other_ref, out_ref, block):
    mine = cand_ref[...]
    other = other_ref[...]
    for item, product in enumerate((mine * other, mine * mine, other * other)):
        shell = product[:IM] + product[IM:]
        shell = jnp.concatenate([shell, jnp.zeros((128 - IM, 128), F32)], axis=0)
        row = jnp.sum(shell.T, axis=0, keepdims=True)
        row = row + pltpu.roll(row, 64, 1)
        high, low = split(row)
        block[FOLD + 2 * item : FOLD + 2 * item + 1, :] = high
        block[FOLD + 2 * item + 1 : FOLD + 2 * item + 2, :] = low
    block[FOLD + 6 :, :] = jnp.zeros((32 - FOLD - 6, 128), F32)
    group = lane_group((FOLD, 128))
    tiles = [grad_ref[at : at + FOLD, :] for at in (0, FOLD, IM, IM + FOLD)]
    for slot in range(N_X):
        block[:FOLD, :] = regroup(tiles, slot, group)
        value = block[...].astype(BF16)
        out_ref[slot] = value
        out_ref[N_X + slot] = value


def share_kernel(place_ref, parts_ref, out_ref, block, whole, sent, left):
    first = place_ref[2] * N_X
    for part in range(N_X):
        block[part] = parts_ref[first + part].astype(F32)
    tiles = [block[part, :FOLD, :] for part in range(N_X)]
    group = lane_group((FOLD, 128))
    for fold, at in enumerate((0, FOLD, IM, IM + FOLD)):
        whole[at : at + FOLD, :] = regroup(tiles, fold, group)
    sums = []
    for part in range(N_X):
        block[part] = parts_ref[part].astype(F32) + parts_ref[N_X + part].astype(F32)
    lane = lax.broadcasted_iota(jnp.int32, (1, 128), 1)
    for pair, at in enumerate(SUM_ROWS):
        for item in range(3):
            row = FOLD + 2 * item
            sums = [block[2 * pair + side, row : row + 1, :] + block[2 * pair + side, row + 1 : row + 2, :] for side in (0, 1)]
            high, low = split(jnp.where(lane < 64, sums[0], sums[1]))
            whole[at + 2 * item : at + 2 * item + 1, :] = high
            whole[at + 2 * item + 1 : at + 2 * item + 2, :] = low
    sent[...] = whole[...].astype(BF16)
    copies = [pltpu.make_async_copy(sent, out_ref.at[dom], left.at[dom]) for dom in range(N_DOM)]
    for copy in copies:
        copy.start()
    for copy in copies:
        copy.wait()


def update_kernel(side_ref, map_ref, parts_ref, out_ref, sums, scale):
    total = parts_ref[0].astype(F32)
    for dom in range(1, N_DOM):
        total += parts_ref[dom].astype(F32)
    sums[...] = total
    factors = []
    for at in SUM_ROWS:
        num, den_mine, den_other = [sums[row : row + 1, :] + sums[row + 1 : row + 2, :] for row in (at, at + 2, at + 4)]
        fsc = num / (jnp.sqrt(den_mine * den_other) + 1e-06)
        factors.append(STEP * (1.0 + fsc) / 2.0)
    factors.append(jnp.zeros((128 - len(factors), 128), F32))
    scale[...] = jnp.concatenate(factors, axis=0).T
    group = lane_group((BLOCK, 128))

    @pl.loop(0, 8)
    def _(z):
        lanes = pl.ds(pl.multiple_of(z * 128, 128), 128)
        tiles = [parts_ref[4 * z + y].astype(F32) for y in range(4)]
        for part in range(N_X):
            value = regroup(tiles, part, group)
            side = 64 * (part % 2)
            weight = scale[side : side + IM, part // 2 : part // 2 + 1]
            for at, rows in ((RB * part, value[:IM]), (R + RB * part, value[IM:])):
                out_ref[at : at + RB, lanes] = map_ref[at : at + RB, lanes] - (weight * rows)[:RB]


def vmem():
    return pl.BlockSpec(memory_space=pltpu.VMEM)


def smem():
    return pl.BlockSpec(memory_space=pltpu.SMEM)


def limit(mib):
    return pltpu.CompilerParams(vmem_limit_bytes=mib << 20)


def cost(flops, moved):
    return pl.CostEstimate(flops=flops, bytes_accessed=moved, transcendentals=0)


def exchange(value, axis, side, groups=None):
    value, side = lax.optimization_barrier((value, side))
    moved = lax.all_to_all(value, axis, 0, 0, tiled=True, axis_index_groups=groups)
    return lax.optimization_barrier((moved, side * 0.5))


def line_terms(classes_local, shifts_local, defocus, radius):
    class_ids = jnp.arange(defocus.shape[0], dtype=jnp.int32)
    focus = jnp.sum(jnp.where(classes_local[:, None] == class_ids[None, :], defocus[None, :], 0.0), axis=1)
    ctf = -jnp.sin(CTF_GAIN * focus[None, :] * (radius[:, None] / R) ** 2 + PHASE_ZERO)
    ctf_rows = jnp.repeat(ctf, LPI, axis=1)
    theta = jnp.pi * jnp.arange(LPI, dtype=F32) / LPI
    theta_rows = jnp.tile(theta, classes_local.shape[0])
    shift_x = jnp.repeat(shifts_local[0].astype(F32), LPI)
    shift_y = jnp.repeat(shifts_local[1].astype(F32), LPI)
    along = shift_x * jnp.cos(theta_rows) + shift_y * jnp.sin(theta_rows)
    phase = 2.0 * jnp.pi * radius[:, None] * along[None, :] / (2.0 * R)
    return (ctf_rows, jnp.cos(phase), jnp.sin(phase))


def body(volume, images, tap_index, tap_weight, classes, shifts, defocus):
    map_t = volume[0].T
    data_t = images[0].T
    slab = lax.axis_index("slab")
    dom = lax.axis_index("dom")
    x = slab & 3
    place = jnp.stack([dom >> 2, dom & 3, slab >> 2]).astype(jnp.int32)
    runs = [[N_X * run + at for at in range(N_X)] for run in range(N_SLAB // N_X)]

    sent = jax.ShapeDtypeStruct((N_X, SENT, ROWS), BF16)
    parts = pl.pallas_call(
        project_kernel,
        out_shape=sent,
        in_specs=[smem(), vmem(), vmem(), pl.BlockSpec(memory_space=pl.ANY)],
        out_specs=vmem(),
        scratch_shapes=[
            pltpu.VMEM((2 * R, LINES), F32),
            pltpu.VMEM((N_X * BLOCK, LINES), F32),
            pltpu.VMEM((LINES, ROWS), BF16),
            pltpu.SemaphoreType.DMA(()),
        ],
        name="project",
    )(place, tap_index[0, 0], tap_weight[0, 0], map_t)
    parts, side = exchange(parts, "slab", defocus[:1], runs)

    pad = ((0, IM - RB), (0, 0))
    radius = (RB * x + jnp.arange(RB)).astype(F32)
    ctf, cosine, sine = line_terms(classes[0], shifts[0], defocus, radius)
    ctf, cosine, sine = (jnp.pad(ctf, pad), jnp.pad(cosine, pad), jnp.pad(sine, pad))
    data = lax.dynamic_slice(data_t.reshape(2, R, ROWS), (0, RB * x, 0), (2, RB, ROWS))
    data = jnp.pad(data, ((0, 0),) + pad)

    shard = jax.ShapeDtypeStruct((BLOCK, 128), F32)
    mine, low, own = pl.pallas_call(
        gather_kernel,
        out_shape=(
            jax.ShapeDtypeStruct((BLOCK, ROWS), F32),
            jax.ShapeDtypeStruct((BLOCK, ROWS), BF16),
            shard,
        ),
        in_specs=[vmem()],
        out_specs=(vmem(), vmem(), vmem()),
        compiler_params=limit(4),
        name="gather",
    )(parts)
    other = lax.ppermute(low, "slab", [(at, at ^ N_X) for at in range(N_SLAB)])
    taps = pl.pallas_call(
        taps_kernel,
        out_shape=jax.ShapeDtypeStruct((N_X, LINES, ROWS), BF16),
        in_specs=[vmem()],
        out_specs=vmem(),
        compiler_params=limit(16),
        cost_estimate=cost(1 << 24, 10 << 20),
        name="taps",
    )(parts)
    parts = pl.pallas_call(
        back_kernel,
        out_shape=jax.ShapeDtypeStruct((N_DOM, TIGHT, 128), BF16),
        in_specs=[vmem()] * 7,
        out_specs=vmem(),
        scratch_shapes=[
            pltpu.VMEM((TIGHT, ROWS), F32),
            pltpu.VMEM((N_X, TIGHT, LINES), F32),
        ],
        compiler_params=limit(16),
        name="back",
    )(mine, other, data, ctf, cosine, sine, taps)
    parts, side = exchange(parts, "dom", side)

    grad, cand = pl.pallas_call(
        reduce_kernel,
        out_shape=(shard, shard),
        in_specs=[vmem()] * 2,
        out_specs=(vmem(), vmem()),
        scratch_shapes=[pltpu.VMEM((TIGHT, 128), F32)],
        compiler_params=limit(4),
        name="reduce",
    )(parts, own)
    other = lax.ppermute(cand, "half", [(0, 1), (1, 0)])
    share = pl.pallas_call(
        shell_kernel,
        out_shape=jax.ShapeDtypeStruct((N_SLAB, 32, 128), BF16),
        in_specs=[vmem()] * 3,
        out_specs=vmem(),
        scratch_shapes=[pltpu.VMEM((32, 128), F32)],
        compiler_params=limit(2),
        name="shell",
    )(grad, cand, other)
    share, side = exchange(share, "slab", side)
    every = pl.pallas_call(
        share_kernel,
        out_shape=jax.ShapeDtypeStruct((N_DOM, BLOCK, 128), BF16),
        in_specs=[smem(), vmem()],
        out_specs=pl.BlockSpec(memory_space=pltpu.HBM),
        scratch_shapes=[
            pltpu.VMEM((N_X, 32, 128), F32),
            pltpu.VMEM((BLOCK, 128), F32),
            pltpu.VMEM((BLOCK, 128), BF16),
            pltpu.SemaphoreType.DMA((N_DOM,)),
        ],
        compiler_params=limit(4),
        name="share",
    )(place, share)
    every, side = exchange(every, "dom", side)
    result = pl.pallas_call(
        update_kernel,
        out_shape=jax.ShapeDtypeStruct((2 * R, LINES), F32),
        in_specs=[smem(), vmem(), vmem()],
        out_specs=vmem(),
        scratch_shapes=[pltpu.VMEM((BLOCK, 128), F32), pltpu.VMEM((128, 128), F32)],
        compiler_params=limit(8),
        name="update",
    )(side, map_t, every)
    return result.T[None]


def solution(mesh):
    placed = (
        P("half", "slab", None),
        P("half", "dom", None),
        P("half", "slab", None, "dom"),
        P("half", "slab", None, "dom"),
        P("half", "dom"),
        P("half", None, "dom"),
        P(),
    )
    return jax.shard_map(
        body, mesh=mesh, in_specs=placed, out_specs=P("half", "slab", None), check_vma=False
    )
```

time: 149 us -> 139 us (0.933)
  waiting for transfers between devices: 89 us -> 75.8 us
  starting transfers between devices: 34.1 us -> 38.2 us
  Pallas kernels: 19.3 us -> 17.7 us
    all_to_all x4, waiting for transfers between devices: 87.8 us -> 70.3 us  [exchange(): lax.all_to_all(value, axis, 0, 0, tiled=True, axis_index_groups=groups)]
    ppermute x0 -> x1, starting transfers between devices: none -> 6.83 us  [body(): other = lax.ppermute(low, 'slab', [(at, at ^ N_X) for at in range(N_SLAB)])]
    ppermute x0 -> x1, waiting for transfers between devices: none -> 4.3 us  [body(): other = lax.ppermute(low, 'slab', [(at, at ^ N_X) for at in range(N_SLAB)])]
    all_to_all x4, starting transfers between devices: 32.2 us -> 29.3 us  [exchange(): lax.all_to_all(value, axis, 0, 0, tiled=True, axis_index_groups=groups)]
    unnamed x16 -> x14, local copies, waits for them, and re-layouts: 3.04 us -> 0.95 us
    reshape x1, local copies, waits for them, and re-layouts: 0.11 us -> 1.81 us  [line_terms(): ctf_rows = jnp.repeat(ctf, LPI, axis=1)]
    pallas_call x4 -> x7, Pallas kernels: 15.8 us -> 14.8 us  [the longest x1 5.27 us: body(): pl.pallas_call(back_kernel, out_shape=jax.ShapeDtypeStruct((N_DOM, TIGHT,...]
  transfers between devices with their start and end apart: 5 -> 6, of which waited for: 5 -> 6; matrix products, arithmetic and copies ran while one was open for 1% -> 4% of each run, Pallas kernels for 0% -> 1%
where the time goes in v4:
time: 139 us
  waiting for transfers between devices  75.8 us (55%)
  starting transfers between devices  38.2 us (27%)
  Pallas kernels  17.7 us (13%)
  local copies, waits for them, and re-layouts  4.92 us (4%)
  other arithmetic  1.94 us (1%)
    all_to_all x4, waiting for transfers between devices, exchange(): lax.all_to_all(value, axis, 0, 0, tiled=True, axis_index_groups=groups)  70.3 us
    all_to_all x4, starting transfers between devices, exchange(): lax.all_to_all(value, axis, 0, 0, tiled=True, axis_index_groups=groups)  29.3 us
    ppermute x1, starting transfers between devices, body(): other = lax.ppermute(low, 'slab', [(at, at ^ N_X) for at in range(N_SLAB)])  6.83 us
    pallas_call x1, Pallas kernels, body(): pl.pallas_call(back_kernel, out_shape=jax.ShapeDtypeStruct((N_DOM, TIGHT,...  5.27 us
    pallas_call x1, Pallas kernels, body(): pl.pallas_call(project_kernel, out_shape=sent, in_specs=[smem(), vmem(),...  4.39 us
    ppermute x1, waiting for transfers between devices, body(): other = lax.ppermute(low, 'slab', [(at, at ^ N_X) for at in range(N_SLAB)])  4.3 us
    pallas_call x1, Pallas kernels, body(): pl.pallas_call(update_kernel, out_shape=jax.ShapeDtypeStruct((2 * R, LINE...  2.91 us
  transfers between devices with their start and end apart: 6, of which 6 were waited for; matrix products, arithmetic and copies ran while one was open for 4% of the time, Pallas kernels for 1%

profile of v4, /device:TPU:8, one launch (start us, length us, event | category | flops | bytes accessed | tf_op | source)
XLA Modules:
  0.0 138.8 jit_solution(3782273233976488858)
XLA Ops:
  0.0 0.6 pad_add_fusion.place_ref
  0.6 4.4 %project.1 = bf16[4,120,1024]{2,1,0:T(8,128)(2,1)} custom-call(s32[3]{0:T(128)} %pad_add_fusion.place_ref, s32[8,1024]{1,0:T(8,128)} %bitcast.25, f32[8,1024]{1,0:T(8,128)} %bitcast.26, f32[400,1024]{1,0:T(8,128)} %bitcast.23), custom_call_target="tpu_custom_call" | custom-call | tf_op jit(solution)/shard_map/project/pallas_call | solution.py:298
  5.1 4.4 %all-to-all-start = ((bf16[4,120,1024]{2,1,0:T(8,128)(2,1)}), bf16[4,120,1024]{2,1,0:T(8,128)(2,1)S(1)}, u32[]{:S(2)}, u32[]{:S(2)}) async-start(bf16[4,120,1024]{2,1,0:T(8,128)(2,1)} %project.1), calls=%async_computation | async-start | bytes 1966080 | tf_op jit(solution)/shard_map/all_to_all | solution.py:270
  10.0 0.9 fusion
  10.9 13.0 %all-to-all-done.parts_ref = bf16[4,120,1024]{2,1,0:T(8,128)(2,1)S(1)} async-done(((bf16[4,120,1024]{2,1,0:T(8,128)(2,1)}), bf16[4,120,1024]{2,1,0:T(8,128)(2,1)S(1)}, u32[]{:S(2)}, u32[]{:S(2)}) %all-to-all-start) | async-done | bytes 983072 | tf_op jit(solution)/shard_map/all_to_all | solution.py:270
  24.1 6.8 %collective-permute-start = (bf16[112,1024]{1,0:T(8,128)(2,1)S(1)}, bf16[112,1024]{1,0:T(8,128)(2,1)S(1)}, u32[]{:S(2)}, u32[]{:S(2)}) collective-permute-start(bf16[112,1024]{1,0:T(8,128)(2,1)S(1)} %get-tuple-element.30), channel_id=1, source_target_pairs={{0,4},{1,5},{2,6},{3,7},{4,0},{5,1},{6,2},{7,3},{8,12},{9,13},{10,... | collective-permute-start | bytes 688136 | tf_op jit(solution)/shard_map/ppermute | solution.py:333
  31.2 0.9 broadcast_in_dim.32
  32.1 1.8 %reshape.63 = f32[50,1024]{1,0:T(8,128)} reshape(f32[50,16,64]{2,1,0:T(8,128)} %broadcast_in_dim.32) | data formatting | bytes 409600 | tf_op jit(solution)/shard_map/reshape | solution.py:278
  33.9 1.0 pad.15.ctf_ref
  35.0 1.7 %taps.1.taps_ref = bf16[4,1024,1024]{2,1,0:T(8,128)(2,1)S(1)} custom-call(bf16[4,120,1024]{2,1,0:T(8,128)(2,1)S(1)} %all-to-all-done.parts_ref), custom_call_target="tpu_custom_call" | custom-call | flops 16777216 | bytes 10485760 | tf_op jit(solution)/shard_map/taps/pallas_call | solution.py:334
  36.7 4.3 %collective-permute-done.other_ref = bf16[112,1024]{1,0:T(8,128)(2,1)S(1)} collective-permute-done((bf16[112,1024]{1,0:T(8,128)(2,1)S(1)}, bf16[112,1024]{1,0:T(8,128)(2,1)S(1)}, u32[]{:S(2)}, u32[]{:S(2)}) %collective-permute-start) | collective-permute-done | bytes 229408 | tf_op jit(solution)/shard_map/ppermute | solution.py:333
  41.0 5.3 %back.1 = bf16[32,104,128]{2,1,0:T(8,128)(2,1)} custom-call(f32[112,1024]{1,0:T(8,128)S(1)} %get-tuple-element.29.mine_ref, bf16[112,1024]{1,0:T(8,128)(2,1)S(1)} %collective-permute-done.other_ref, bf16[2,56,1024]{2,1,0:T(8,128)(2,1)S(1)} %pad.14.data_ref, f32[56,1024]{1,0:T(8,128)S(1)} %pad.15.ctf_ref, f32[56,1024]{1,0:T(8,128)S(1)} %pad.16.cos_ref, ...), custom_call_target="tpu_custom_call" | custom-call | tf_op jit(solution)/shard_map/back/pallas_call | solution.py:343
  46.3 13.2 %all-to-all-start.1 = ((bf16[32,104,128]{2,1,0:T(8,128)(2,1)}), bf16[32,104,128]{2,1,0:T(8,128)(2,1)S(1)}, u32[]{:S(2)}, u32[]{:S(2)}) async-start(bf16[32,104,128]{2,1,0:T(8,128)(2,1)} %back.1), calls=%async_computation.1 | async-start | bytes 1703936 | tf_op jit(solution)/shard_map/all_to_all | solution.py:270
  59.5 23.2 %all-to-all-done.1.parts_ref = bf16[32,104,128]{2,1,0:T(8,128)(2,1)S(1)} async-done(((bf16[32,104,128]{2,1,0:T(8,128)(2,1)}), bf16[32,104,128]{2,1,0:T(8,128)(2,1)S(1)}, u32[]{:S(2)}, u32[]{:S(2)}) %all-to-all-start.1) | async-done | bytes 852000 | tf_op jit(solution)/shard_map/all_to_all | solution.py:270
  82.9 2.1 %collective-permute-start.1 = (f32[112,128]{1,0:T(8,128)S(1)}, f32[112,128]{1,0:T(8,128)S(1)}, u32[]{:S(2)}, u32[]{:S(2)}) collective-permute-start(f32[112,128]{1,0:T(8,128)S(1)} %get-tuple-element.37.cand_ref), channel_id=1, source_target_pairs={{0,256},{256,0},{1,257},{257,1},{2,258},{258,2},{3,259},{259,3},{4... | collective-permute-start | bytes 172040 | tf_op jit(solution)/shard_map/ppermute | solution.py:366
  84.9 1.2 collective-permute-done.1.other_ref
  86.1 0.9 shell.1
  87.0 5.5 %all-to-all-start.2 = ((bf16[8,32,128]{2,1,0:T(8,128)(2,1)}), bf16[8,32,128]{2,1,0:T(8,128)(2,1)S(1)}, u32[]{:S(2)}, u32[]{:S(2)}) async-start(bf16[8,32,128]{2,1,0:T(8,128)(2,1)} %shell.1), calls=%async_computation.2 | async-start | bytes 131072 | tf_op jit(solution)/shard_map/all_to_all | solution.py:270
  92.5 10.3 %all-to-all-done.2.parts_ref = bf16[8,32,128]{2,1,0:T(8,128)(2,1)S(1)} async-done(((bf16[8,32,128]{2,1,0:T(8,128)(2,1)}), bf16[8,32,128]{2,1,0:T(8,128)(2,1)S(1)}, u32[]{:S(2)}, u32[]{:S(2)}) %all-to-all-start.2) | async-done | bytes 65568 | tf_op jit(solution)/shard_map/all_to_all | solution.py:270
  102.8 2.2 %share.1 = bf16[32,112,128]{2,1,0:T(8,128)(2,1)S(1)} custom-call(s32[3]{0:T(128)S(1)} %copy-done.3, bf16[8,32,128]{2,1,0:T(8,128)(2,1)S(1)} %all-to-all-done.2.parts_ref), custom_call_target="tpu_custom_call" | custom-call | tf_op jit(solution)/shard_map/share/pallas_call | solution.py:377
  105.0 0.9 copy-done.2
  105.9 6.2 %all-to-all-start.3 = ((bf16[32,112,128]{2,1,0:T(8,128)(2,1)}), bf16[32,112,128]{2,1,0:T(8,128)(2,1)S(1)}, u32[]{:S(2)}, u32[]{:S(2)}) async-start(bf16[32,112,128]{2,1,0:T(8,128)(2,1)} %copy-done.2), calls=%async_computation.3 | async-start | bytes 1835008 | tf_op jit(solution)/shard_map/all_to_all | solution.py:270
  112.1 23.8 %all-to-all-done.3.parts_ref = bf16[32,112,128]{2,1,0:T(8,128)(2,1)S(1)} async-done(((bf16[32,112,128]{2,1,0:T(8,128)(2,1)}), bf16[32,112,128]{2,1,0:T(8,128)(2,1)S(1)}, u32[]{:S(2)}, u32[]{:S(2)}) %all-to-all-start.3) | async-done | bytes 917536 | tf_op jit(solution)/shard_map/all_to_all | solution.py:270
  135.9 2.9 %update.1 = f32[400,1024]{1,0:T(8,128)} custom-call(f32[1]{0:T(128)S(6)} %mul.95.side_ref, f32[400,1024]{1,0:T(8,128)S(1)} %bitcast.24, bf16[32,112,128]{2,1,0:T(8,128)(2,1)S(1)} %all-to-all-done.3.parts_ref), custom_call_target="tpu_custom_call" | custom-call | tf_op jit(solution)/shard_map/update/pallas_call | solution.py:392
  (28 shorter events, 1.2 us)
Async XLA Ops:
  0.0 34.9 %copy-start = (bf16[1,1024,400]{1,2,0:T(8,128)(2,1)S(1)}, bf16[1,1024,400]{1,2,0:T(8,128)(2,1)}, u32[]{:S(2)}) copy-start(bf16[1,1024,400]{1,2,0:T(8,128)(2,1)} %param.8) | copy-start | bytes 2457604
  5.0 4.5 %copy-start.4 = (s32[1,2,16]{2,1,0:T(2,128)S(1)}, s32[1,2,16]{2,1,0:T(2,128)}, u32[]{:S(2)}) copy-start(s32[1,2,16]{2,1,0:T(2,128)} %param.12) | copy-start | bytes 388
  5.0 4.7 %copy-start.5 = (f32[16]{0:T(128)S(1)}, f32[16]{0:T(128)}, u32[]{:S(2)}) copy-start(f32[16]{0:T(128)} %param.13) | copy-start | bytes 196
  5.0 4.7 %copy-start.6 = (s32[1,16]{1,0:T(1,128)S(1)}, s32[1,16]{1,0:T(1,128)}, u32[]{:S(2)}) copy-start(s32[1,16]{1,0:T(1,128)} %param.11) | copy-start | bytes 196
  5.1 18.8 %all-to-all-start = ((bf16[4,120,1024]{2,1,0:T(8,128)(2,1)}), bf16[4,120,1024]{2,1,0:T(8,128)(2,1)S(1)}, u32[]{:S(2)}, u32[]{:S(2)}) async-start(bf16[4,120,1024]{2,1,0:T(8,128)(2,1)} %project.1), calls=%async_computation | async-start | bytes 1966080 | tf_op jit(solution)/shard_map/all_to_all | solution.py:270
  24.1 16.9 %collective-permute-start = (bf16[112,1024]{1,0:T(8,128)(2,1)S(1)}, bf16[112,1024]{1,0:T(8,128)(2,1)S(1)}, u32[]{:S(2)}, u32[]{:S(2)}) collective-permute-start(bf16[112,1024]{1,0:T(8,128)(2,1)S(1)} %get-tuple-element.30), channel_id=1, source_target_pairs={{0,4},{1,5},{2,6},{3,7},{4,0},{5,1},{6,2},{7,3},{8,12},{9,13},{10,... | collective-permute-start | bytes 688136 | tf_op jit(solution)/shard_map/ppermute | solution.py:333
  46.3 56.5 %copy-start.3 = (s32[3]{0:T(128)S(1)}, s32[3]{0:T(128)}, u32[]{:S(2)}) copy-start(s32[3]{0:T(128)} %pad_add_fusion.place_ref) | copy-start | bytes 40
  46.3 36.4 %all-to-all-start.1 = ((bf16[32,104,128]{2,1,0:T(8,128)(2,1)}), bf16[32,104,128]{2,1,0:T(8,128)(2,1)S(1)}, u32[]{:S(2)}, u32[]{:S(2)}) async-start(bf16[32,104,128]{2,1,0:T(8,128)(2,1)} %back.1), calls=%async_computation.1 | async-start | bytes 1703936 | tf_op jit(solution)/shard_map/all_to_all | solution.py:270
  82.9 53.0 %copy-start.1 = (f32[1,1024,400]{1,2,0:T(8,128)S(1)}, f32[1,1024,400]{1,2,0:T(8,128)}, u32[]{:S(2)}) copy-start(f32[1,1024,400]{1,2,0:T(8,128)} %param.7) | copy-start | bytes 4915204
  82.9 3.3 %collective-permute-start.1 = (f32[112,128]{1,0:T(8,128)S(1)}, f32[112,128]{1,0:T(8,128)S(1)}, u32[]{:S(2)}, u32[]{:S(2)}) collective-permute-start(f32[112,128]{1,0:T(8,128)S(1)} %get-tuple-element.37.cand_ref), channel_id=1, source_target_pairs={{0,256},{256,0},{1,257},{257,1},{2,258},{258,2},{3,259},{259,3},{4... | collective-permute-start | bytes 172040 | tf_op jit(solution)/shard_map/ppermute | solution.py:366
  87.0 15.7 %all-to-all-start.2 = ((bf16[8,32,128]{2,1,0:T(8,128)(2,1)}), bf16[8,32,128]{2,1,0:T(8,128)(2,1)S(1)}, u32[]{:S(2)}, u32[]{:S(2)}) async-start(bf16[8,32,128]{2,1,0:T(8,128)(2,1)} %shell.1), calls=%async_computation.2 | async-start | bytes 131072 | tf_op jit(solution)/shard_map/all_to_all | solution.py:270
  105.0 0.9 copy-start.2
  105.9 30.0 %all-to-all-start.3 = ((bf16[32,112,128]{2,1,0:T(8,128)(2,1)}), bf16[32,112,128]{2,1,0:T(8,128)(2,1)S(1)}, u32[]{:S(2)}, u32[]{:S(2)}) async-start(bf16[32,112,128]{2,1,0:T(8,128)(2,1)} %copy-done.2), calls=%async_computation.3 | async-start | bytes 1835008 | tf_op jit(solution)/shard_map/all_to_all | solution.py:270

commit v5 on v4

--- a/solution.py
+++ b/solution.py
@@ -47,6 +47,18 @@
     for slot, tile in enumerate(tiles):
         moved = pltpu.roll(tile, (SHARE * (slot - source)) % 128, 1)
         out = moved if out is None else jnp.where(group == slot, moved, out)
+    return out
+
+
+def regroup_all(tiles, group):
+    low = group < 2
+    even = (group & 1) == 0
+    half = [jnp.where(low, tiles[at], pltpu.roll(tiles[at + 2], 2 * SHARE, 1)) for at in range(2)]
+    half += [jnp.where(low, pltpu.roll(tiles[at], 2 * SHARE, 1), tiles[at + 2]) for at in range(2)]
+    out = []
+    for at in (0, 2):
+        out.append(jnp.where(even, half[at], pltpu.roll(half[at + 1], SHARE, 1)))
+        out.append(jnp.where(even, pltpu.roll(half[at], 3 * SHARE, 1), half[at + 1]))
     return out
 
 
@@ -71,7 +83,7 @@
         before = here
 
 
-def project_kernel(place_ref, index_ref, weight_ref, map_hbm, out_ref, map_ref, block, taps, arrived):
+def project_kernel(index_ref, weight_ref, map_hbm, out_ref, map_ref, block, taps, arrived):
     copy = pltpu.make_async_copy(map_hbm, map_ref, arrived)
     copy.start()
     index = index_ref[...]
@@ -87,8 +99,9 @@
     build_taps(taps, weights, high, low)
     copy.wait()
 
-    z = pl.multiple_of(place_ref[0] * 128, 128)
-    y = place_ref[1]
+    dom = lax.axis_index("dom")
+    z = pl.multiple_of((dom >> 2) * 128, 128)
+    y = dom & 3
     group = lane_group((8, 128))
     for part in range(N_X):
         at = BLOCK * part
@@ -150,15 +163,14 @@
     back[RB : 2 * RB, :] = back_im[:RB]
     back_low = back[...].astype(BF16)
 
-    @pl.loop(0, N_X)
-    def _(part):
+    for part in range(N_X):
         grad[part] = lax.dot_general(back_low, taps_ref[part], (((1,), (1,)), ((), ())), preferred_element_type=F32)
 
     group = lane_group((TIGHT, 128))
     for z in range(8):
         tiles = [grad[part, :, 128 * z : 128 * (z + 1)] for part in range(N_X)]
-        for y in range(4):
-            out_ref[4 * z + y] = regroup(tiles, y, group).astype(BF16)
+        for y, value in enumerate(regroup_all(tiles, group)):
+            out_ref[4 * z + y] = value.astype(BF16)
 
 
 def reduce_kernel(parts_ref, own_ref, grad_ref, cand_ref, total):
@@ -189,22 +201,21 @@
     block[FOLD + 6 :, :] = jnp.zeros((32 - FOLD - 6, 128), F32)
     group = lane_group((FOLD, 128))
     tiles = [grad_ref[at : at + FOLD, :] for at in (0, FOLD, IM, IM + FOLD)]
-    for slot in range(N_X):
-        block[:FOLD, :] = regroup(tiles, slot, group)
+    for slot, folded in enumerate(regroup_all(tiles, group)):
+        block[:FOLD, :] = folded
         value = block[...].astype(BF16)
         out_ref[slot] = value
         out_ref[N_X + slot] = value
 
 
-def share_kernel(place_ref, parts_ref, out_ref, block, whole, sent, left):
-    first = place_ref[2] * N_X
+def share_kernel(parts_ref, out_ref, block, whole):
+    first = (lax.axis_index("slab") >> 2) * N_X
     for part in range(N_X):
         block[part] = parts_ref[first + part].astype(F32)
     tiles = [block[part, :FOLD, :] for part in range(N_X)]
     group = lane_group((FOLD, 128))
-    for fold, at in enumerate((0, FOLD, IM, IM + FOLD)):
-        whole[at : at + FOLD, :] = regroup(tiles, fold, group)
-    sums = []
+    for at, value in zip((0, FOLD, IM, IM + FOLD), regroup_all(tiles, group), strict=True):
+        whole[at : at + FOLD, :] = value
     for part in range(N_X):
         block[part] = parts_ref[part].astype(F32) + parts_ref[N_X + part].astype(F32)
     lane = lax.broadcasted_iota(jnp.int32, (1, 128), 1)
@@ -215,15 +226,12 @@
             high, low = split(jnp.where(lane < 64, sums[0], sums[1]))
             whole[at + 2 * item : at + 2 * item + 1, :] = high
             whole[at + 2 * item + 1 : at + 2 * item + 2, :] = low
-    sent[...] = whole[...].astype(BF16)
-    copies = [pltpu.make_async_copy(sent, out_ref.at[dom], left.at[dom]) for dom in range(N_DOM)]
-    for copy in copies:
-        copy.start()
-    for copy in copies:
-        copy.wait()
-
-
-def update_kernel(side_ref, map_ref, parts_ref, out_ref, sums, scale):
+    value = whole[...].astype(BF16)
+    for dom in range(N_DOM):
+        out_ref[dom] = value
+
+
+def update_kernel(map_ref, parts_ref, out_hbm, out_ref, sums, scale, left):
     total = parts_ref[0].astype(F32)
     for dom in range(1, N_DOM):
         total += parts_ref[dom].astype(F32)
@@ -237,26 +245,29 @@
     scale[...] = jnp.concatenate(factors, axis=0).T
     group = lane_group((BLOCK, 128))
 
+    def copy(z):
+        lanes = pl.ds(pl.multiple_of(z * 128, 128), 128)
+        return pltpu.make_async_copy(out_ref.at[:, lanes], out_hbm.at[:, lanes], left.at[z])
+
     @pl.loop(0, 8)
     def _(z):
         lanes = pl.ds(pl.multiple_of(z * 128, 128), 128)
         tiles = [parts_ref[4 * z + y].astype(F32) for y in range(4)]
-        for part in range(N_X):
-            value = regroup(tiles, part, group)
+        for part, value in enumerate(regroup_all(tiles, group)):
             side = 64 * (part % 2)
             weight = scale[side : side + IM, part // 2 : part // 2 + 1]
             for at, rows in ((RB * part, value[:IM]), (R + RB * part, value[IM:])):
                 out_ref[at : at + RB, lanes] = map_ref[at : at + RB, lanes] - (weight * rows)[:RB]
+        copy(z).start()
+
+    for z in range(8):
+        copy(z).wait()
 
 
 def vmem():
     return pl.BlockSpec(memory_space=pltpu.VMEM)
 
 
-def smem():
-    return pl.BlockSpec(memory_space=pltpu.SMEM)
-
-
 def limit(mib):
     return pltpu.CompilerParams(vmem_limit_bytes=mib << 20)
 
@@ -265,10 +276,8 @@
     return pl.CostEstimate(flops=flops, bytes_accessed=moved, transcendentals=0)
 
 
-def exchange(value, axis, side, groups=None):
-    value, side = lax.optimization_barrier((value, side))
-    moved = lax.all_to_all(value, axis, 0, 0, tiled=True, axis_index_groups=groups)
-    return lax.optimization_barrier((moved, side * 0.5))
+def exchange(value, axis, groups=None):
+    return lax.all_to_all(value, axis, 0, 0, tiled=True, axis_index_groups=groups)
 
 
 def line_terms(classes_local, shifts_local, defocus, radius):
@@ -289,16 +298,14 @@
     map_t = volume[0].T
     data_t = images[0].T
     slab = lax.axis_index("slab")
-    dom = lax.axis_index("dom")
     x = slab & 3
-    place = jnp.stack([dom >> 2, dom & 3, slab >> 2]).astype(jnp.int32)
     runs = [[N_X * run + at for at in range(N_X)] for run in range(N_SLAB // N_X)]
 
     sent = jax.ShapeDtypeStruct((N_X, SENT, ROWS), BF16)
     parts = pl.pallas_call(
         project_kernel,
         out_shape=sent,
-        in_specs=[smem(), vmem(), vmem(), pl.BlockSpec(memory_space=pl.ANY)],
+        in_specs=[vmem(), vmem(), pl.BlockSpec(memory_space=pl.ANY)],
         out_specs=vmem(),
         scratch_shapes=[
             pltpu.VMEM((2 * R, LINES), F32),
@@ -307,8 +314,8 @@
             pltpu.SemaphoreType.DMA(()),
         ],
         name="project",
-    )(place, tap_index[0, 0], tap_weight[0, 0], map_t)
-    parts, side = exchange(parts, "slab", defocus[:1], runs)
+    )(tap_index[0, 0], tap_weight[0, 0], map_t)
+    parts = exchange(parts, "slab", runs)
 
     pad = ((0, IM - RB), (0, 0))
     radius = (RB * x + jnp.arange(RB)).astype(F32)
@@ -316,6 +323,7 @@
     ctf, cosine, sine = (jnp.pad(ctf, pad), jnp.pad(cosine, pad), jnp.pad(sine, pad))
     data = lax.dynamic_slice(data_t.reshape(2, R, ROWS), (0, RB * x, 0), (2, RB, ROWS))
     data = jnp.pad(data, ((0, 0),) + pad)
+    parts, ctf, cosine, sine, data = lax.optimization_barrier((parts, ctf, cosine, sine, data))
 
     shard = jax.ShapeDtypeStruct((BLOCK, 128), F32)
     mine, low, own = pl.pallas_call(
@@ -352,7 +360,7 @@
         compiler_params=limit(16),
         name="back",
     )(mine, other, data, ctf, cosine, sine, taps)
-    parts, side = exchange(parts, "dom", side)
+    parts = exchange(parts, "dom")
 
     grad, cand = pl.pallas_call(
         reduce_kernel,
@@ -373,31 +381,31 @@
         compiler_params=limit(2),
         name="shell",
     )(grad, cand, other)
-    share, side = exchange(share, "slab", side)
+    share = exchange(share, "slab")
     every = pl.pallas_call(
         share_kernel,
         out_shape=jax.ShapeDtypeStruct((N_DOM, BLOCK, 128), BF16),
-        in_specs=[smem(), vmem()],
-        out_specs=pl.BlockSpec(memory_space=pltpu.HBM),
-        scratch_shapes=[
-            pltpu.VMEM((N_X, 32, 128), F32),
-            pltpu.VMEM((BLOCK, 128), F32),
-            pltpu.VMEM((BLOCK, 128), BF16),
-            pltpu.SemaphoreType.DMA((N_DOM,)),
-        ],
+        in_specs=[vmem()],
+        out_specs=vmem(),
+        scratch_shapes=[pltpu.VMEM((N_X, 32, 128), F32), pltpu.VMEM((BLOCK, 128), F32)],
         compiler_params=limit(4),
         name="share",
-    )(place, share)
-    every, side = exchange(every, "dom", side)
+    )(share)
+    every = exchange(every, "dom")
     result = pl.pallas_call(
         update_kernel,
         out_shape=jax.ShapeDtypeStruct((2 * R, LINES), F32),
-        in_specs=[smem(), vmem(), vmem()],
-        out_specs=vmem(),
-        scratch_shapes=[pltpu.VMEM((BLOCK, 128), F32), pltpu.VMEM((128, 128), F32)],
+        in_specs=[vmem(), vmem()],
+        out_specs=pl.BlockSpec(memory_space=pl.ANY),
+        scratch_shapes=[
+            pltpu.VMEM((2 * R, LINES), F32),
+            pltpu.VMEM((BLOCK, 128), F32),
+            pltpu.VMEM((128, 128), F32),
+            pltpu.SemaphoreType.DMA((8,)),
+        ],
         compiler_params=limit(8),
         name="update",
-    )(side, map_t, every)
+    )(map_t, every)
     return result.T[None]
 
 

time: 139 us -> 133 us (0.957)
  blocking collectives: 0 us -> 81.5 us
  waiting for transfers between devices: 75.8 us -> 21.9 us
  starting transfers between devices: 38.2 us -> 13.3 us
  Pallas kernels: 17.7 us -> 13.4 us
  local copies, waits for them, and re-layouts: 4.92 us -> 0.65 us
    all_to_all x0 -> x3, blocking collectives: none -> 81.5 us  [exchange(): lax.all_to_all(value, axis, 0, 0, tiled=True, axis_index_groups=groups)]
    all_to_all x4 -> x1, waiting for transfers between devices: 70.3 us -> 12.3 us  [exchange(): lax.all_to_all(value, axis, 0, 0, tiled=True, axis_index_groups=groups)]
    all_to_all x4 -> x1, starting transfers between devices: 29.3 us -> 4.44 us  [exchange(): lax.all_to_all(value, axis, 0, 0, tiled=True, axis_index_groups=groups)]
    ppermute x1, waiting for transfers between devices: 4.3 us -> 8.37 us  [body(): other = lax.ppermute(low, 'slab', [(at, at ^ N_X) for at in range(N_SLAB)])]
    pallas_call x1, Pallas kernels: 2.18 us -> 0.21 us  [body(): pl.pallas_call(share_kernel, out_shape=jax.ShapeDtypeStruct((N_DOM, BLOCK...]
    reshape x1, local copies, waits for them, and re-layouts: 1.81 us -> 0.16 us  [line_terms(): ctf_rows = jnp.repeat(ctf, LPI, axis=1)]
    pallas_call x1, Pallas kernels: 5.27 us -> 3.82 us  [body(): pl.pallas_call(back_kernel, out_shape=jax.ShapeDtypeStruct((N_DOM, TIGHT,...]
  transfers between devices with their start and end apart: 6 -> 3, of which waited for: 6 -> 3; matrix products, arithmetic and copies ran while one was open for 4% -> 1% of each run, Pallas kernels for 1% -> 1%
where the time goes in v5:
time: 133 us; the launch traced here: 132 us
  blocking collectives  81.5 us (61%)
  waiting for transfers between devices  21.9 us (16%)
  Pallas kernels  13.4 us (10%)
  starting transfers between devices  13.3 us (10%)
    all_to_all x3, blocking collectives, exchange(): lax.all_to_all(value, axis, 0, 0, tiled=True, axis_index_groups=groups)  81.5 us
    all_to_all x1, waiting for transfers between devices, exchange(): lax.all_to_all(value, axis, 0, 0, tiled=True, axis_index_groups=groups)  12.3 us
    ppermute x1, waiting for transfers between devices, body(): other = lax.ppermute(low, 'slab', [(at, at ^ N_X) for at in range(N_SLAB)])  8.37 us
    ppermute x1, starting transfers between devices, body(): other = lax.ppermute(low, 'slab', [(at, at ^ N_X) for at in range(N_SLAB)])  6.83 us
    pallas_call x1, Pallas kernels, body(): pl.pallas_call(project_kernel, out_shape=sent, in_specs=[vmem(), vmem(),...  4.45 us
    all_to_all x1, starting transfers between devices, exchange(): lax.all_to_all(value, axis, 0, 0, tiled=True, axis_index_groups=groups)  4.44 us
    pallas_call x1, Pallas kernels, body(): pl.pallas_call(back_kernel, out_shape=jax.ShapeDtypeStruct((N_DOM, TIGHT,...  3.82 us
  transfers between devices with their start and end apart: 3, of which 3 were waited for; matrix products, arithmetic and copies ran while one was open for 1% of the time, Pallas kernels for 1%

profile of v5, /device:TPU:8, one launch (start us, length us, event | category | flops | bytes accessed | tf_op | source)
XLA Modules:
  0.0 132.3 jit_solution(2378469999577437966)
XLA Ops:
  0.0 4.5 %project.1 = bf16[4,120,1024]{2,1,0:T(8,128)(2,1)} custom-call(s32[8,1024]{1,0:T(8,128)} %bitcast.21, f32[8,1024]{1,0:T(8,128)} %bitcast.22, f32[400,1024]{1,0:T(8,128)} %bitcast.19), custom_call_target="tpu_custom_call" | custom-call | tf_op jit(solution)/shard_map/project/pallas_call | solution.py:305
  4.5 4.4 %all-to-all-start = ((bf16[4,120,1024]{2,1,0:T(8,128)(2,1)}), bf16[4,120,1024]{2,1,0:T(8,128)(2,1)S(1)}, u32[]{:S(2)}, u32[]{:S(2)}) async-start(bf16[4,120,1024]{2,1,0:T(8,128)(2,1)} %project.1), calls=%async_computation | async-start | bytes 1966080 | tf_op jit(solution)/shard_map/all_to_all | solution.py:280
  9.0 0.2 select_reduce_fusion
  9.2 0.1 multiply_add_fusion
  9.4 0.1 sine_negate_fusion
  9.5 0.1 copy.8
  9.6 0.2 broadcast_in_dim.32
  9.8 0.2 reshape.62
  9.9 0.9 fusion
  11.0 12.3 %all-to-all-done.parts_ref = bf16[4,120,1024]{2,1,0:T(8,128)(2,1)S(1)} async-done(((bf16[4,120,1024]{2,1,0:T(8,128)(2,1)}), bf16[4,120,1024]{2,1,0:T(8,128)(2,1)S(1)}, u32[]{:S(2)}, u32[]{:S(2)}) %all-to-all-start) | async-done | bytes 983072 | tf_op jit(solution)/shard_map/all_to_all | solution.py:280
  23.3 0.2 gather.1
  23.6 6.8 %collective-permute-start = (bf16[112,1024]{1,0:T(8,128)(2,1)S(1)}, bf16[112,1024]{1,0:T(8,128)(2,1)S(1)}, u32[]{:S(2)}, u32[]{:S(2)}) collective-permute-start(bf16[112,1024]{1,0:T(8,128)(2,1)S(1)} %get-tuple-element.17), channel_id=1, source_target_pairs={{0,4},{1,5},{2,6},{3,7},{4,0},{5,1},{6,2},{7,3},{8,12},{9,13},{10,... | collective-permute-start | bytes 688136 | tf_op jit(solution)/shard_map/ppermute | solution.py:341
  30.4 1.7 %taps.1.taps_ref = bf16[4,1024,1024]{2,1,0:T(8,128)(2,1)S(1)} custom-call(bf16[4,120,1024]{2,1,0:T(8,128)(2,1)S(1)} %all-to-all-done.parts_ref), custom_call_target="tpu_custom_call" | custom-call | flops 16777216 | bytes 10485760 | tf_op jit(solution)/shard_map/taps/pallas_call | solution.py:342
  32.1 8.4 %collective-permute-done.other_ref = bf16[112,1024]{1,0:T(8,128)(2,1)S(1)} collective-permute-done((bf16[112,1024]{1,0:T(8,128)(2,1)S(1)}, bf16[112,1024]{1,0:T(8,128)(2,1)S(1)}, u32[]{:S(2)}, u32[]{:S(2)}) %collective-permute-start) | collective-permute-done | bytes 229408 | tf_op jit(solution)/shard_map/ppermute | solution.py:341
  40.5 3.8 %back.1 = bf16[32,104,128]{2,1,0:T(8,128)(2,1)S(1)} custom-call(f32[112,1024]{1,0:T(8,128)S(1)} %get-tuple-element.16.mine_ref, bf16[112,1024]{1,0:T(8,128)(2,1)S(1)} %collective-permute-done.other_ref, bf16[2,56,1024]{2,1,0:T(8,128)(2,1)S(1)} %pad.17.data_ref, f32[56,1024]{1,0:T(8,128)S(1)} %pad.14.ctf_ref, f32[56,1024]{1,0:T(8,128)S(1)} %pad.15.cos_ref, ...), custom_call_target="tpu_custom_call" | custom-call | tf_op jit(solution)/shard_map/back/pallas_call | solution.py:351
  44.3 36.0 %all_to_all.20.parts_ref = bf16[32,104,128]{2,1,0:T(8,128)(2,1)S(1)} all-to-all(bf16[32,104,128]{2,1,0:T(8,128)(2,1)S(1)} %back.1), channel_id=1, replica_groups=mesh['half'=2,'dom'=32,'slab'=8] {'dom'}, dimensions={0} | all-to-all | bytes 1703936 | tf_op jit(solution)/shard_map/all_to_all | solution.py:280
  80.3 0.2 reduce.1
  80.5 2.1 %collective-permute-start.1 = (f32[112,128]{1,0:T(8,128)S(1)}, f32[112,128]{1,0:T(8,128)S(1)}, u32[]{:S(2)}, u32[]{:S(2)}) collective-permute-start(f32[112,128]{1,0:T(8,128)S(1)} %get-tuple-element.24.cand_ref), channel_id=1, source_target_pairs={{0,256},{256,0},{1,257},{257,1},{2,258},{258,2},{3,259},{259,3},{4... | collective-permute-start | bytes 172040 | tf_op jit(solution)/shard_map/ppermute | solution.py:374
  82.6 1.2 collective-permute-done.1.other_ref
  83.8 0.2 shell.1
  84.0 15.6 %all_to_all.21.parts_ref = bf16[8,32,128]{2,1,0:T(8,128)(2,1)S(1)} all-to-all(bf16[8,32,128]{2,1,0:T(8,128)(2,1)S(1)} %shell.1), channel_id=1, replica_groups=mesh['half'=2,'dom'=32,'slab'=8] {'slab'}, dimensions={0} | all-to-all | bytes 131072 | tf_op jit(solution)/shard_map/all_to_all | solution.py:280
  99.6 0.2 share.1
  99.8 29.9 %all_to_all.22.parts_ref = bf16[32,112,128]{2,1,0:T(8,128)(2,1)S(1)} all-to-all(bf16[32,112,128]{2,1,0:T(8,128)(2,1)S(1)} %share.1), channel_id=1, replica_groups=mesh['half'=2,'dom'=32,'slab'=8] {'dom'}, dimensions={0} | all-to-all | bytes 1835008 | tf_op jit(solution)/shard_map/all_to_all | solution.py:280
  129.7 2.6 %update.1 = f32[400,1024]{1,0:T(8,128)} custom-call(f32[400,1024]{1,0:T(8,128)S(1)} %bitcast.20, bf16[32,112,128]{2,1,0:T(8,128)(2,1)S(1)} %all_to_all.22.parts_ref), custom_call_target="tpu_custom_call" | custom-call | tf_op jit(solution)/shard_map/update/pallas_call | solution.py:395
  (20 shorter events, 0.3 us)
Async XLA Ops:
  0.0 10.9 %copy-start = (bf16[1,1024,400]{1,2,0:T(8,128)(2,1)S(1)}, bf16[1,1024,400]{1,2,0:T(8,128)(2,1)}, u32[]{:S(2)}) copy-start(bf16[1,1024,400]{1,2,0:T(8,128)(2,1)} %param.8) | copy-start | bytes 2457604
  4.5 4.5 %copy-start.2 = (s32[1,2,16]{2,1,0:T(2,128)S(1)}, s32[1,2,16]{2,1,0:T(2,128)}, u32[]{:S(2)}) copy-start(s32[1,2,16]{2,1,0:T(2,128)} %param.12) | copy-start | bytes 388
  4.5 4.5 %copy-start.3 = (f32[16]{0:T(128)S(1)}, f32[16]{0:T(128)}, u32[]{:S(2)}) copy-start(f32[16]{0:T(128)} %param.13) | copy-start | bytes 196
  4.5 4.5 %copy-start.4 = (s32[1,16]{1,0:T(1,128)S(1)}, s32[1,16]{1,0:T(1,128)}, u32[]{:S(2)}) copy-start(s32[1,16]{1,0:T(1,128)} %param.11) | copy-start | bytes 196
  4.5 18.8 %all-to-all-start = ((bf16[4,120,1024]{2,1,0:T(8,128)(2,1)}), bf16[4,120,1024]{2,1,0:T(8,128)(2,1)S(1)}, u32[]{:S(2)}, u32[]{:S(2)}) async-start(bf16[4,120,1024]{2,1,0:T(8,128)(2,1)} %project.1), calls=%async_computation | async-start | bytes 1966080 | tf_op jit(solution)/shard_map/all_to_all | solution.py:280
  23.6 16.9 %collective-permute-start = (bf16[112,1024]{1,0:T(8,128)(2,1)S(1)}, bf16[112,1024]{1,0:T(8,128)(2,1)S(1)}, u32[]{:S(2)}, u32[]{:S(2)}) collective-permute-start(bf16[112,1024]{1,0:T(8,128)(2,1)S(1)} %get-tuple-element.17), channel_id=1, source_target_pairs={{0,4},{1,5},{2,6},{3,7},{4,0},{5,1},{6,2},{7,3},{8,12},{9,13},{10,... | collective-permute-start | bytes 688136 | tf_op jit(solution)/shard_map/ppermute | solution.py:341
  80.5 49.2 %copy-start.1 = (f32[1,1024,400]{1,2,0:T(8,128)S(1)}, f32[1,1024,400]{1,2,0:T(8,128)}, u32[]{:S(2)}) copy-start(f32[1,1024,400]{1,2,0:T(8,128)} %param.7) | copy-start | bytes 4915204
  80.5 3.3 %collective-permute-start.1 = (f32[112,128]{1,0:T(8,128)S(1)}, f32[112,128]{1,0:T(8,128)S(1)}, u32[]{:S(2)}, u32[]{:S(2)}) collective-permute-start(f32[112,128]{1,0:T(8,128)S(1)} %get-tuple-element.24.cand_ref), channel_id=1, source_target_pairs={{0,256},{256,0},{1,257},{257,1},{2,258},{258,2},{3,259},{259,3},{4... | collective-permute-start | bytes 172040 | tf_op jit(solution)/shard_map/ppermute | solution.py:374

commit v6 on v5

--- a/solution.py
+++ b/solution.py
@@ -35,7 +35,9 @@
 HIGH_ROW = 108
 LOW_ROW = 109
 SUM_ROWS = (50, 106)
+SUM_TILES = (48, 96)
 CHUNK = 16
+PIECES = (0, 56, 104, 152, 200, 256, 304, 352, 400)
 
 
 def lane_group(shape):
@@ -83,9 +85,14 @@
         before = here
 
 
-def project_kernel(index_ref, weight_ref, map_hbm, out_ref, map_ref, block, taps, arrived):
-    copy = pltpu.make_async_copy(map_hbm, map_ref, arrived)
-    copy.start()
+def project_kernel(index_ref, weight_ref, map_hbm, out_hbm, map_ref, block, taps, out_ref, arrived, left):
+    pieces = []
+    for piece in range(2 * N_X):
+        rows = slice(PIECES[piece], PIECES[piece + 1])
+        pieces.append(pltpu.make_async_copy(map_hbm.at[rows], map_ref.at[rows], arrived.at[piece]))
+    for part in range(N_X):
+        pieces[part].start()
+        pieces[N_X + part].start()
     index = index_ref[...]
     weight = weight_ref[...]
     base = jnp.min(index, axis=0, keepdims=True)
@@ -97,7 +104,6 @@
     low = (base & 15).astype(F32)
     weights = [ordered[tap : tap + 1] for tap in range(K)]
     build_taps(taps, weights, high, low)
-    copy.wait()
 
     dom = lax.axis_index("dom")
     z = pl.multiple_of((dom >> 2) * 128, 128)
@@ -105,6 +111,8 @@
     group = lane_group((8, 128))
     for part in range(N_X):
         at = BLOCK * part
+        pieces[part].wait()
+        pieces[N_X + part].wait()
         block[at + RB : at + IM, :] = jnp.zeros((IM - RB, LINES), F32)
         block[at + IM + RB : at + BLOCK, :] = jnp.zeros((IM - RB, LINES), F32)
         block[at : at + RB, :] = map_ref[RB * part : RB * (part + 1), :]
@@ -124,6 +132,9 @@
         for row, value in zip(TAP_ROWS + (HIGH_ROW, LOW_ROW), weights + [high, low], strict=True):
             block[at + row : at + row + 1, :] = value
         out_ref[part, :BLOCK, :] = block[at : at + BLOCK, :].astype(BF16)
+        pltpu.make_async_copy(out_ref.at[part], out_hbm.at[part], left.at[part]).start()
+    for part in range(N_X):
+        pltpu.make_async_copy(out_ref.at[part], out_hbm.at[part], left.at[part]).wait()
 
 
 def gather_kernel(parts_ref, mine_ref, low_ref, own_ref):
@@ -147,30 +158,30 @@
         build_taps(taps_ref.at[part], weights, rows[HIGH_ROW : HIGH_ROW + 1], rows[LOW_ROW : LOW_ROW + 1])
 
 
-def back_kernel(mine_ref, other_ref, data_ref, ctf_ref, cos_ref, sin_ref, taps_ref, out_ref, back, grad):
-    ctf = ctf_ref[...]
-    cosine = cos_ref[...]
-    sine = sin_ref[...]
-    proj = mine_ref[...] + other_ref[...].astype(F32)
-    proj_re = proj[:IM]
-    proj_im = proj[IM:]
-    res_re = ctf * (cosine * proj_re - sine * proj_im) - data_ref[0].astype(F32)
-    res_im = ctf * (sine * proj_re + cosine * proj_im) - data_ref[1].astype(F32)
-    back_re = ctf * (cosine * res_re + sine * res_im)
-    back_im = ctf * (cosine * res_im - sine * res_re)
+def back_kernel(mine_ref, other_ref, data_ref, ctf_ref, cos_ref, sin_ref, taps_ref, out_ref, back):
     back[2 * RB :, :] = jnp.zeros((TIGHT - 2 * RB, ROWS), F32)
-    back[:RB, :] = back_re[:RB]
-    back[RB : 2 * RB, :] = back_im[:RB]
+    for chunk in range(ROWS // 128):
+        at = slice(128 * chunk, 128 * (chunk + 1))
+        ctf = ctf_ref[:, at]
+        cosine = cos_ref[:, at]
+        sine = sin_ref[:, at]
+        proj_re = mine_ref[:IM, at] + other_ref[:IM, at].astype(F32)
+        proj_im = mine_ref[IM:, at] + other_ref[IM:, at].astype(F32)
+        res_re = ctf * (cosine * proj_re - sine * proj_im) - data_ref[0, :, at].astype(F32)
+        res_im = ctf * (sine * proj_re + cosine * proj_im) - data_ref[1, :, at].astype(F32)
+        back[:RB, at] = (ctf * (cosine * res_re + sine * res_im))[:RB]
+        back[RB : 2 * RB, at] = (ctf * (cosine * res_im - sine * res_re))[:RB]
     back_low = back[...].astype(BF16)
-
-    for part in range(N_X):
-        grad[part] = lax.dot_general(back_low, taps_ref[part], (((1,), (1,)), ((), ())), preferred_element_type=F32)
-
     group = lane_group((TIGHT, 128))
-    for z in range(8):
-        tiles = [grad[part, :, 128 * z : 128 * (z + 1)] for part in range(N_X)]
-        for y, value in enumerate(regroup_all(tiles, group)):
-            out_ref[4 * z + y] = value.astype(BF16)
+    for pair in range(4):
+        grads = []
+        for part in range(N_X):
+            lines = taps_ref[part, 256 * pair : 256 * (pair + 1), :]
+            grads.append(lax.dot_general(back_low, lines, (((1,), (1,)), ((), ())), preferred_element_type=F32))
+        for side in range(2):
+            tiles = [grad[:, 128 * side : 128 * (side + 1)] for grad in grads]
+            for y, value in enumerate(regroup_all(tiles, group)):
+                out_ref[4 * (2 * pair + side) + y] = value.astype(BF16)
 
 
 def reduce_kernel(parts_ref, own_ref, grad_ref, cand_ref, total):
@@ -232,12 +243,14 @@
 
 
 def update_kernel(map_ref, parts_ref, out_hbm, out_ref, sums, scale, left):
-    total = parts_ref[0].astype(F32)
-    for dom in range(1, N_DOM):
-        total += parts_ref[dom].astype(F32)
-    sums[...] = total
+    for pair, at in enumerate(SUM_TILES):
+        total = parts_ref[0, at : at + 16].astype(F32)
+        for dom in range(1, N_DOM):
+            total += parts_ref[dom, at : at + 16].astype(F32)
+        sums[16 * pair : 16 * (pair + 1), :] = total
     factors = []
-    for at in SUM_ROWS:
+    for pair in range(2):
+        at = 16 * pair + SUM_ROWS[pair] - SUM_TILES[pair]
         num, den_mine, den_other = [sums[row : row + 1, :] + sums[row + 1 : row + 2, :] for row in (at, at + 2, at + 4)]
         fsc = num / (jnp.sqrt(den_mine * den_other) + 1e-06)
         factors.append(STEP * (1.0 + fsc) / 2.0)
@@ -245,23 +258,19 @@
     scale[...] = jnp.concatenate(factors, axis=0).T
     group = lane_group((BLOCK, 128))
 
-    def copy(z):
-        lanes = pl.ds(pl.multiple_of(z * 128, 128), 128)
-        return pltpu.make_async_copy(out_ref.at[:, lanes], out_hbm.at[:, lanes], left.at[z])
-
-    @pl.loop(0, 8)
-    def _(z):
-        lanes = pl.ds(pl.multiple_of(z * 128, 128), 128)
+    copies = []
+    for z in range(8):
+        lanes = slice(128 * z, 128 * (z + 1))
         tiles = [parts_ref[4 * z + y].astype(F32) for y in range(4)]
         for part, value in enumerate(regroup_all(tiles, group)):
             side = 64 * (part % 2)
             weight = scale[side : side + IM, part // 2 : part // 2 + 1]
             for at, rows in ((RB * part, value[:IM]), (R + RB * part, value[IM:])):
                 out_ref[at : at + RB, lanes] = map_ref[at : at + RB, lanes] - (weight * rows)[:RB]
-        copy(z).start()
-
-    for z in range(8):
-        copy(z).wait()
+        copies.append(pltpu.make_async_copy(out_ref.at[:, lanes], out_hbm.at[:, lanes], left.at[z]))
+        copies[-1].start()
+    for copy in copies:
+        copy.wait()
 
 
 def vmem():
@@ -306,12 +315,14 @@
         project_kernel,
         out_shape=sent,
         in_specs=[vmem(), vmem(), pl.BlockSpec(memory_space=pl.ANY)],
-        out_specs=vmem(),
+        out_specs=pl.BlockSpec(memory_space=pl.ANY),
         scratch_shapes=[
             pltpu.VMEM((2 * R, LINES), F32),
             pltpu.VMEM((N_X * BLOCK, LINES), F32),
             pltpu.VMEM((LINES, ROWS), BF16),
-            pltpu.SemaphoreType.DMA(()),
+            pltpu.VMEM((N_X, SENT, ROWS), BF16),
+            pltpu.SemaphoreType.DMA((2 * N_X,)),
+            pltpu.SemaphoreType.DMA((N_X,)),
         ],
         name="project",
     )(tap_index[0, 0], tap_weight[0, 0], map_t)
@@ -353,10 +364,7 @@
         out_shape=jax.ShapeDtypeStruct((N_DOM, TIGHT, 128), BF16),
         in_specs=[vmem()] * 7,
         out_specs=vmem(),
-        scratch_shapes=[
-            pltpu.VMEM((TIGHT, ROWS), F32),
-            pltpu.VMEM((N_X, TIGHT, LINES), F32),
-        ],
+        scratch_shapes=[pltpu.VMEM((TIGHT, ROWS), F32)],
         compiler_params=limit(16),
         name="back",
     )(mine, other, data, ctf, cosine, sine, taps)
@@ -399,7 +407,7 @@
         out_specs=pl.BlockSpec(memory_space=pl.ANY),
         scratch_shapes=[
             pltpu.VMEM((2 * R, LINES), F32),
-            pltpu.VMEM((BLOCK, 128), F32),
+            pltpu.VMEM((32, 128), F32),
             pltpu.VMEM((128, 128), F32),
             pltpu.SemaphoreType.DMA((8,)),
         ],

time: 133 us -> 132 us (level)
  no operation moved by 1% of the time
where the time goes in v6:
time: 132 us; the launch traced here: 131 us
  blocking collectives  81.4 us (62%)
  waiting for transfers between devices  21.9 us (17%)
  starting transfers between devices  13.3 us (10%)
  Pallas kernels  12.6 us (10%)
    all_to_all x3, blocking collectives, exchange(): lax.all_to_all(value, axis, 0, 0, tiled=True, axis_index_groups=groups)  81.4 us
    all_to_all x1, waiting for transfers between devices, exchange(): lax.all_to_all(value, axis, 0, 0, tiled=True, axis_index_groups=groups)  12.3 us
    ppermute x1, waiting for transfers between devices, body(): other = lax.ppermute(low, 'slab', [(at, at ^ N_X) for at in range(N_SLAB)])  8.37 us
    ppermute x1, starting transfers between devices, body(): other = lax.ppermute(low, 'slab', [(at, at ^ N_X) for at in range(N_SLAB)])  6.83 us
    all_to_all x1, starting transfers between devices, exchange(): lax.all_to_all(value, axis, 0, 0, tiled=True, axis_index_groups=groups)  4.44 us
    pallas_call x1, Pallas kernels, body(): pl.pallas_call(project_kernel, out_shape=sent, in_specs=[vmem(), vmem(),...  4.44 us
    pallas_call x1, Pallas kernels, body(): pl.pallas_call(back_kernel, out_shape=jax.ShapeDtypeStruct((N_DOM, TIGHT,...  3.07 us
  transfers between devices with their start and end apart: 3, of which 3 were waited for; matrix products, arithmetic and copies ran while one was open for 1% of the time, Pallas kernels for 1%

profile of v6, /device:TPU:8, one launch (start us, length us, event | category | flops | bytes accessed | tf_op | source)
XLA Modules:
  0.0 131.3 jit_solution(5732647211363783028)
XLA Ops:
  0.0 4.4 %project.1 = bf16[4,120,1024]{2,1,0:T(8,128)(2,1)} custom-call(s32[8,1024]{1,0:T(8,128)} %bitcast.21, f32[8,1024]{1,0:T(8,128)} %bitcast.22, f32[400,1024]{1,0:T(8,128)} %bitcast.19), custom_call_target="tpu_custom_call" | custom-call | tf_op jit(solution)/shard_map/project/pallas_call | solution.py:314
  4.5 4.4 %all-to-all-start = ((bf16[4,120,1024]{2,1,0:T(8,128)(2,1)}), bf16[4,120,1024]{2,1,0:T(8,128)(2,1)S(1)}, u32[]{:S(2)}, u32[]{:S(2)}) async-start(bf16[4,120,1024]{2,1,0:T(8,128)(2,1)} %project.1), calls=%async_computation | async-start | bytes 1966080 | tf_op jit(solution)/shard_map/all_to_all | solution.py:289
  9.0 0.2 select_reduce_fusion
  9.2 0.1 multiply_add_fusion
  9.3 0.1 sine_negate_fusion
  9.5 0.1 copy.8
  9.6 0.2 broadcast_in_dim.32
  9.7 0.2 reshape.62
  9.9 0.9 fusion
  11.0 12.3 %all-to-all-done.parts_ref = bf16[4,120,1024]{2,1,0:T(8,128)(2,1)S(1)} async-done(((bf16[4,120,1024]{2,1,0:T(8,128)(2,1)}), bf16[4,120,1024]{2,1,0:T(8,128)(2,1)S(1)}, u32[]{:S(2)}, u32[]{:S(2)}) %all-to-all-start) | async-done | bytes 983072 | tf_op jit(solution)/shard_map/all_to_all | solution.py:289
  23.3 0.2 gather.1
  23.5 6.8 %collective-permute-start = (bf16[112,1024]{1,0:T(8,128)(2,1)S(1)}, bf16[112,1024]{1,0:T(8,128)(2,1)S(1)}, u32[]{:S(2)}, u32[]{:S(2)}) collective-permute-start(bf16[112,1024]{1,0:T(8,128)(2,1)S(1)} %get-tuple-element.17), channel_id=1, source_target_pairs={{0,4},{1,5},{2,6},{3,7},{4,0},{5,1},{6,2},{7,3},{8,12},{9,13},{10,... | collective-permute-start | bytes 688136 | tf_op jit(solution)/shard_map/ppermute | solution.py:352
  30.4 1.7 %taps.1.taps_ref = bf16[4,1024,1024]{2,1,0:T(8,128)(2,1)S(1)} custom-call(bf16[4,120,1024]{2,1,0:T(8,128)(2,1)S(1)} %all-to-all-done.parts_ref), custom_call_target="tpu_custom_call" | custom-call | flops 16777216 | bytes 10485760 | tf_op jit(solution)/shard_map/taps/pallas_call | solution.py:353
  32.1 8.4 %collective-permute-done.other_ref = bf16[112,1024]{1,0:T(8,128)(2,1)S(1)} collective-permute-done((bf16[112,1024]{1,0:T(8,128)(2,1)S(1)}, bf16[112,1024]{1,0:T(8,128)(2,1)S(1)}, u32[]{:S(2)}, u32[]{:S(2)}) %collective-permute-start) | collective-permute-done | bytes 229408 | tf_op jit(solution)/shard_map/ppermute | solution.py:352
  40.5 3.1 %back.1 = bf16[32,104,128]{2,1,0:T(8,128)(2,1)S(1)} custom-call(f32[112,1024]{1,0:T(8,128)S(1)} %get-tuple-element.16.mine_ref, bf16[112,1024]{1,0:T(8,128)(2,1)S(1)} %collective-permute-done.other_ref, bf16[2,56,1024]{2,1,0:T(8,128)(2,1)S(1)} %pad.17.data_ref, f32[56,1024]{1,0:T(8,128)S(1)} %pad.14.ctf_ref, f32[56,1024]{1,0:T(8,128)S(1)} %pad.15.cos_ref, ...), custom_call_target="tpu_custom_call" | custom-call | tf_op jit(solution)/shard_map/back/pallas_call | solution.py:362
  43.5 36.0 %all_to_all.20.parts_ref = bf16[32,104,128]{2,1,0:T(8,128)(2,1)S(1)} all-to-all(bf16[32,104,128]{2,1,0:T(8,128)(2,1)S(1)} %back.1), channel_id=1, replica_groups=mesh['half'=2,'dom'=32,'slab'=8] {'dom'}, dimensions={0} | all-to-all | bytes 1703936 | tf_op jit(solution)/shard_map/all_to_all | solution.py:289
  79.6 0.2 reduce.1
  79.8 2.1 %collective-permute-start.1 = (f32[112,128]{1,0:T(8,128)S(1)}, f32[112,128]{1,0:T(8,128)S(1)}, u32[]{:S(2)}, u32[]{:S(2)}) collective-permute-start(f32[112,128]{1,0:T(8,128)S(1)} %get-tuple-element.24.cand_ref), channel_id=1, source_target_pairs={{0,256},{256,0},{1,257},{257,1},{2,258},{258,2},{3,259},{259,3},{4... | collective-permute-start | bytes 172040 | tf_op jit(solution)/shard_map/ppermute | solution.py:382
  81.8 1.2 collective-permute-done.1.other_ref
  83.0 0.2 shell.1
  83.3 15.5 %all_to_all.21.parts_ref = bf16[8,32,128]{2,1,0:T(8,128)(2,1)S(1)} all-to-all(bf16[8,32,128]{2,1,0:T(8,128)(2,1)S(1)} %shell.1), channel_id=1, replica_groups=mesh['half'=2,'dom'=32,'slab'=8] {'slab'}, dimensions={0} | all-to-all | bytes 131072 | tf_op jit(solution)/shard_map/all_to_all | solution.py:289
  98.8 0.2 share.1
  99.0 29.8 %all_to_all.22.parts_ref = bf16[32,112,128]{2,1,0:T(8,128)(2,1)S(1)} all-to-all(bf16[32,112,128]{2,1,0:T(8,128)(2,1)S(1)} %share.1), channel_id=1, replica_groups=mesh['half'=2,'dom'=32,'slab'=8] {'dom'}, dimensions={0} | all-to-all | bytes 1835008 | tf_op jit(solution)/shard_map/all_to_all | solution.py:289
  128.8 2.5 %update.1 = f32[400,1024]{1,0:T(8,128)} custom-call(f32[400,1024]{1,0:T(8,128)S(1)} %bitcast.20, bf16[32,112,128]{2,1,0:T(8,128)(2,1)S(1)} %all_to_all.22.parts_ref), custom_call_target="tpu_custom_call" | custom-call | tf_op jit(solution)/shard_map/update/pallas_call | solution.py:403
  (20 shorter events, 0.3 us)
Async XLA Ops:
  0.0 10.9 %copy-start = (bf16[1,1024,400]{1,2,0:T(8,128)(2,1)S(1)}, bf16[1,1024,400]{1,2,0:T(8,128)(2,1)}, u32[]{:S(2)}) copy-start(bf16[1,1024,400]{1,2,0:T(8,128)(2,1)} %param.8) | copy-start | bytes 2457604
  4.4 4.5 %copy-start.2 = (s32[1,2,16]{2,1,0:T(2,128)S(1)}, s32[1,2,16]{2,1,0:T(2,128)}, u32[]{:S(2)}) copy-start(s32[1,2,16]{2,1,0:T(2,128)} %param.12) | copy-start | bytes 388
  4.5 4.5 %copy-start.3 = (f32[16]{0:T(128)S(1)}, f32[16]{0:T(128)}, u32[]{:S(2)}) copy-start(f32[16]{0:T(128)} %param.13) | copy-start | bytes 196
  4.5 4.5 %copy-start.4 = (s32[1,16]{1,0:T(1,128)S(1)}, s32[1,16]{1,0:T(1,128)}, u32[]{:S(2)}) copy-start(s32[1,16]{1,0:T(1,128)} %param.11) | copy-start | bytes 196
  4.5 18.8 %all-to-all-start = ((bf16[4,120,1024]{2,1,0:T(8,128)(2,1)}), bf16[4,120,1024]{2,1,0:T(8,128)(2,1)S(1)}, u32[]{:S(2)}, u32[]{:S(2)}) async-start(bf16[4,120,1024]{2,1,0:T(8,128)(2,1)} %project.1), calls=%async_computation | async-start | bytes 1966080 | tf_op jit(solution)/shard_map/all_to_all | solution.py:289
  23.5 16.9 %collective-permute-start = (bf16[112,1024]{1,0:T(8,128)(2,1)S(1)}, bf16[112,1024]{1,0:T(8,128)(2,1)S(1)}, u32[]{:S(2)}, u32[]{:S(2)}) collective-permute-start(bf16[112,1024]{1,0:T(8,128)(2,1)S(1)} %get-tuple-element.17), channel_id=1, source_target_pairs={{0,4},{1,5},{2,6},{3,7},{4,0},{5,1},{6,2},{7,3},{8,12},{9,13},{10,... | collective-permute-start | bytes 688136 | tf_op jit(solution)/shard_map/ppermute | solution.py:352
  79.8 49.1 %copy-start.1 = (f32[1,1024,400]{1,2,0:T(8,128)S(1)}, f32[1,1024,400]{1,2,0:T(8,128)}, u32[]{:S(2)}) copy-start(f32[1,1024,400]{1,2,0:T(8,128)} %param.7) | copy-start | bytes 4915204
  79.8 3.3 %collective-permute-start.1 = (f32[112,128]{1,0:T(8,128)S(1)}, f32[112,128]{1,0:T(8,128)S(1)}, u32[]{:S(2)}, u32[]{:S(2)}) collective-permute-start(f32[112,128]{1,0:T(8,128)S(1)} %get-tuple-element.24.cand_ref), channel_id=1, source_target_pairs={{0,256},{256,0},{1,257},{257,1},{2,258},{258,2},{3,259},{259,3},{4... | collective-permute-start | bytes 172040 | tf_op jit(solution)/shard_map/ppermute | solution.py:382

commit v7 on v6

--- a/solution.py
+++ b/solution.py
@@ -85,7 +85,11 @@
         before = here
 
 
-def project_kernel(index_ref, weight_ref, map_hbm, out_hbm, map_ref, block, taps, out_ref, arrived, left):
+def project_kernel(index_hbm, weight_hbm, map_hbm, out_hbm, index_ref, weight_ref, map_ref, block, taps, out_ref, arrived, left):
+    first = pltpu.make_async_copy(index_hbm, index_ref, arrived.at[2 * N_X])
+    second = pltpu.make_async_copy(weight_hbm, weight_ref, arrived.at[2 * N_X + 1])
+    first.start()
+    second.start()
     pieces = []
     for piece in range(2 * N_X):
         rows = slice(PIECES[piece], PIECES[piece + 1])
@@ -93,6 +97,8 @@
     for part in range(N_X):
         pieces[part].start()
         pieces[N_X + part].start()
+    first.wait()
+    second.wait()
     index = index_ref[...]
     weight = weight_ref[...]
     base = jnp.min(index, axis=0, keepdims=True)
@@ -158,7 +164,7 @@
         build_taps(taps_ref.at[part], weights, rows[HIGH_ROW : HIGH_ROW + 1], rows[LOW_ROW : LOW_ROW + 1])
 
 
-def back_kernel(mine_ref, other_ref, data_ref, ctf_ref, cos_ref, sin_ref, taps_ref, out_ref, back):
+def back_kernel(mine_ref, other_ref, data_ref, ctf_ref, cos_ref, sin_ref, taps_ref, out_ref, back, grad):
     back[2 * RB :, :] = jnp.zeros((TIGHT - 2 * RB, ROWS), F32)
     for chunk in range(ROWS // 128):
         at = slice(128 * chunk, 128 * (chunk + 1))
@@ -172,16 +178,11 @@
         back[:RB, at] = (ctf * (cosine * res_re + sine * res_im))[:RB]
         back[RB : 2 * RB, at] = (ctf * (cosine * res_im - sine * res_re))[:RB]
     back_low = back[...].astype(BF16)
-    group = lane_group((TIGHT, 128))
-    for pair in range(4):
-        grads = []
-        for part in range(N_X):
-            lines = taps_ref[part, 256 * pair : 256 * (pair + 1), :]
-            grads.append(lax.dot_general(back_low, lines, (((1,), (1,)), ((), ())), preferred_element_type=F32))
-        for side in range(2):
-            tiles = [grad[:, 128 * side : 128 * (side + 1)] for grad in grads]
-            for y, value in enumerate(regroup_all(tiles, group)):
-                out_ref[4 * (2 * pair + side) + y] = value.astype(BF16)
+    for part in range(N_X):
+        grad[part] = lax.dot_general(taps_ref[part], back_low, (((1,), (1,)), ((), ())), preferred_element_type=F32)
+    for dom in range(N_DOM):
+        lines = [grad[part, SHARE * dom : SHARE * (dom + 1), :] for part in range(N_X)]
+        out_ref[dom] = jnp.concatenate(lines, axis=0).T.astype(BF16)
 
 
 def reduce_kernel(parts_ref, own_ref, grad_ref, cand_ref, total):
@@ -314,14 +315,16 @@
     parts = pl.pallas_call(
         project_kernel,
         out_shape=sent,
-        in_specs=[vmem(), vmem(), pl.BlockSpec(memory_space=pl.ANY)],
+        in_specs=[pl.BlockSpec(memory_space=pl.ANY)] * 3,
         out_specs=pl.BlockSpec(memory_space=pl.ANY),
         scratch_shapes=[
+            pltpu.VMEM((K, ROWS), jnp.int32),
+            pltpu.VMEM((K, ROWS), F32),
             pltpu.VMEM((2 * R, LINES), F32),
             pltpu.VMEM((N_X * BLOCK, LINES), F32),
             pltpu.VMEM((LINES, ROWS), BF16),
             pltpu.VMEM((N_X, SENT, ROWS), BF16),
-            pltpu.SemaphoreType.DMA((2 * N_X,)),
+            pltpu.SemaphoreType.DMA((2 * N_X + 2,)),
             pltpu.SemaphoreType.DMA((N_X,)),
         ],
         name="project",
@@ -364,7 +367,7 @@
         out_shape=jax.ShapeDtypeStruct((N_DOM, TIGHT, 128), BF16),
         in_specs=[vmem()] * 7,
         out_specs=vmem(),
-        scratch_shapes=[pltpu.VMEM((TIGHT, ROWS), F32)],
+        scratch_shapes=[pltpu.VMEM((TIGHT, ROWS), F32), pltpu.VMEM((N_X, LINES, TIGHT), F32)],
         compiler_params=limit(16),
         name="back",
     )(mine, other, data, ctf, cosine, sine, taps)

time: 132 us -> 131 us (level)
  no operation moved by 1% of the time
where the time goes in v7:
time: 131 us; the launch traced here: 130 us
  blocking collectives  81.4 us (62%)
  waiting for transfers between devices  21.9 us (17%)
  starting transfers between devices  13.3 us (10%)
  Pallas kernels  11.4 us (9%)
  other arithmetic  1.31 us (1%)
    all_to_all x3, blocking collectives, exchange(): lax.all_to_all(value, axis, 0, 0, tiled=True, axis_index_groups=groups)  81.4 us
    all_to_all x1, waiting for transfers between devices, exchange(): lax.all_to_all(value, axis, 0, 0, tiled=True, axis_index_groups=groups)  12.3 us
    ppermute x1, waiting for transfers between devices, body(): other = lax.ppermute(low, 'slab', [(at, at ^ N_X) for at in range(N_SLAB)])  8.36 us
    ppermute x1, starting transfers between devices, body(): other = lax.ppermute(low, 'slab', [(at, at ^ N_X) for at in range(N_SLAB)])  6.84 us
    all_to_all x1, starting transfers between devices, exchange(): lax.all_to_all(value, axis, 0, 0, tiled=True, axis_index_groups=groups)  4.44 us
    pallas_call x1, Pallas kernels, body(): pl.pallas_call(project_kernel, out_shape=sent, in_specs=[pl.BlockSpec(mem...  3.78 us
  transfers between devices with their start and end apart: 3, of which 3 were waited for; matrix products, arithmetic and copies ran while one was open for 1% of the time, Pallas kernels for 1%

profile of v7, /device:TPU:8, one launch (start us, length us, event | category | flops | bytes accessed | tf_op | source)
XLA Modules:
  0.0 130.2 jit_solution(11666750728663264613)
XLA Ops:
  0.0 3.8 %project.1 = bf16[4,120,1024]{2,1,0:T(8,128)(2,1)} custom-call(s32[8,1024]{1,0:T(8,128)} %bitcast.21, f32[8,1024]{1,0:T(8,128)} %bitcast.22, f32[400,1024]{1,0:T(8,128)} %bitcast.19), custom_call_target="tpu_custom_call" | custom-call | tf_op jit(solution)/shard_map/project/pallas_call | solution.py:315
  3.8 4.4 %all-to-all-start = ((bf16[4,120,1024]{2,1,0:T(8,128)(2,1)}), bf16[4,120,1024]{2,1,0:T(8,128)(2,1)S(1)}, u32[]{:S(2)}, u32[]{:S(2)}) async-start(bf16[4,120,1024]{2,1,0:T(8,128)(2,1)} %project.1), calls=%async_computation | async-start | bytes 1966080 | tf_op jit(solution)/shard_map/all_to_all | solution.py:290
  8.4 0.2 select_reduce_fusion
  8.5 0.1 multiply_add_fusion
  8.7 0.1 sine_negate_fusion
  8.8 0.1 copy.8
  8.9 0.2 broadcast_in_dim.32
  9.1 0.2 reshape.62
  9.3 0.9 fusion
  10.3 12.3 %all-to-all-done.parts_ref = bf16[4,120,1024]{2,1,0:T(8,128)(2,1)S(1)} async-done(((bf16[4,120,1024]{2,1,0:T(8,128)(2,1)}), bf16[4,120,1024]{2,1,0:T(8,128)(2,1)S(1)}, u32[]{:S(2)}, u32[]{:S(2)}) %all-to-all-start) | async-done | bytes 983072 | tf_op jit(solution)/shard_map/all_to_all | solution.py:290
  22.7 0.2 gather.1
  22.9 6.8 %collective-permute-start = (bf16[112,1024]{1,0:T(8,128)(2,1)S(1)}, bf16[112,1024]{1,0:T(8,128)(2,1)S(1)}, u32[]{:S(2)}, u32[]{:S(2)}) collective-permute-start(bf16[112,1024]{1,0:T(8,128)(2,1)S(1)} %get-tuple-element.17), channel_id=1, source_target_pairs={{0,4},{1,5},{2,6},{3,7},{4,0},{5,1},{6,2},{7,3},{8,12},{9,13},{10,... | collective-permute-start | bytes 688136 | tf_op jit(solution)/shard_map/ppermute | solution.py:355
  29.7 1.7 %taps.1.taps_ref = bf16[4,1024,1024]{2,1,0:T(8,128)(2,1)S(1)} custom-call(bf16[4,120,1024]{2,1,0:T(8,128)(2,1)S(1)} %all-to-all-done.parts_ref), custom_call_target="tpu_custom_call" | custom-call | flops 16777216 | bytes 10485760 | tf_op jit(solution)/shard_map/taps/pallas_call | solution.py:356
  31.4 8.4 %collective-permute-done.other_ref = bf16[112,1024]{1,0:T(8,128)(2,1)S(1)} collective-permute-done((bf16[112,1024]{1,0:T(8,128)(2,1)S(1)}, bf16[112,1024]{1,0:T(8,128)(2,1)S(1)}, u32[]{:S(2)}, u32[]{:S(2)}) %collective-permute-start) | collective-permute-done | bytes 229408 | tf_op jit(solution)/shard_map/ppermute | solution.py:355
  39.8 2.6 %back.1 = bf16[32,104,128]{2,1,0:T(8,128)(2,1)S(1)} custom-call(f32[112,1024]{1,0:T(8,128)S(1)} %get-tuple-element.16.mine_ref, bf16[112,1024]{1,0:T(8,128)(2,1)S(1)} %collective-permute-done.other_ref, bf16[2,56,1024]{2,1,0:T(8,128)(2,1)S(1)} %pad.17.data_ref, f32[56,1024]{1,0:T(8,128)S(1)} %pad.14.ctf_ref, f32[56,1024]{1,0:T(8,128)S(1)} %pad.15.cos_ref, ...), custom_call_target="tpu_custom_call" | custom-call | tf_op jit(solution)/shard_map/back/pallas_call | solution.py:365
  42.4 36.0 %all_to_all.20.parts_ref = bf16[32,104,128]{2,1,0:T(8,128)(2,1)S(1)} all-to-all(bf16[32,104,128]{2,1,0:T(8,128)(2,1)S(1)} %back.1), channel_id=1, replica_groups=mesh['half'=2,'dom'=32,'slab'=8] {'dom'}, dimensions={0} | all-to-all | bytes 1703936 | tf_op jit(solution)/shard_map/all_to_all | solution.py:290
  78.4 0.2 reduce.1
  78.6 2.1 %collective-permute-start.1 = (f32[112,128]{1,0:T(8,128)S(1)}, f32[112,128]{1,0:T(8,128)S(1)}, u32[]{:S(2)}, u32[]{:S(2)}) collective-permute-start(f32[112,128]{1,0:T(8,128)S(1)} %get-tuple-element.24.cand_ref), channel_id=1, source_target_pairs={{0,256},{256,0},{1,257},{257,1},{2,258},{258,2},{3,259},{259,3},{4... | collective-permute-start | bytes 172040 | tf_op jit(solution)/shard_map/ppermute | solution.py:385
  80.7 1.2 collective-permute-done.1.other_ref
  81.9 0.2 shell.1
  82.2 15.5 %all_to_all.21.parts_ref = bf16[8,32,128]{2,1,0:T(8,128)(2,1)S(1)} all-to-all(bf16[8,32,128]{2,1,0:T(8,128)(2,1)S(1)} %shell.1), channel_id=1, replica_groups=mesh['half'=2,'dom'=32,'slab'=8] {'slab'}, dimensions={0} | all-to-all | bytes 131072 | tf_op jit(solution)/shard_map/all_to_all | solution.py:290
  97.7 0.2 share.1
  97.9 29.8 %all_to_all.22.parts_ref = bf16[32,112,128]{2,1,0:T(8,128)(2,1)S(1)} all-to-all(bf16[32,112,128]{2,1,0:T(8,128)(2,1)S(1)} %share.1), channel_id=1, replica_groups=mesh['half'=2,'dom'=32,'slab'=8] {'dom'}, dimensions={0} | all-to-all | bytes 1835008 | tf_op jit(solution)/shard_map/all_to_all | solution.py:290
  127.7 2.5 %update.1 = f32[400,1024]{1,0:T(8,128)} custom-call(f32[400,1024]{1,0:T(8,128)S(1)} %bitcast.20, bf16[32,112,128]{2,1,0:T(8,128)(2,1)S(1)} %all_to_all.22.parts_ref), custom_call_target="tpu_custom_call" | custom-call | tf_op jit(solution)/shard_map/update/pallas_call | solution.py:406
  (20 shorter events, 0.3 us)
Async XLA Ops:
  0.0 10.2 %copy-start = (bf16[1,1024,400]{1,2,0:T(8,128)(2,1)S(1)}, bf16[1,1024,400]{1,2,0:T(8,128)(2,1)}, u32[]{:S(2)}) copy-start(bf16[1,1024,400]{1,2,0:T(8,128)(2,1)} %param.8) | copy-start | bytes 2457604
  3.8 4.5 %copy-start.2 = (s32[1,2,16]{2,1,0:T(2,128)S(1)}, s32[1,2,16]{2,1,0:T(2,128)}, u32[]{:S(2)}) copy-start(s32[1,2,16]{2,1,0:T(2,128)} %param.12) | copy-start | bytes 388
  3.8 4.5 %copy-start.3 = (f32[16]{0:T(128)S(1)}, f32[16]{0:T(128)}, u32[]{:S(2)}) copy-start(f32[16]{0:T(128)} %param.13) | copy-start | bytes 196
  3.8 4.5 %copy-start.4 = (s32[1,16]{1,0:T(1,128)S(1)}, s32[1,16]{1,0:T(1,128)}, u32[]{:S(2)}) copy-start(s32[1,16]{1,0:T(1,128)} %param.11) | copy-start | bytes 196
  3.8 18.8 %all-to-all-start = ((bf16[4,120,1024]{2,1,0:T(8,128)(2,1)}), bf16[4,120,1024]{2,1,0:T(8,128)(2,1)S(1)}, u32[]{:S(2)}, u32[]{:S(2)}) async-start(bf16[4,120,1024]{2,1,0:T(8,128)(2,1)} %project.1), calls=%async_computation | async-start | bytes 1966080 | tf_op jit(solution)/shard_map/all_to_all | solution.py:290
  22.9 16.9 %collective-permute-start = (bf16[112,1024]{1,0:T(8,128)(2,1)S(1)}, bf16[112,1024]{1,0:T(8,128)(2,1)S(1)}, u32[]{:S(2)}, u32[]{:S(2)}) collective-permute-start(bf16[112,1024]{1,0:T(8,128)(2,1)S(1)} %get-tuple-element.17), channel_id=1, source_target_pairs={{0,4},{1,5},{2,6},{3,7},{4,0},{5,1},{6,2},{7,3},{8,12},{9,13},{10,... | collective-permute-start | bytes 688136 | tf_op jit(solution)/shard_map/ppermute | solution.py:355
  78.6 49.1 %copy-start.1 = (f32[1,1024,400]{1,2,0:T(8,128)S(1)}, f32[1,1024,400]{1,2,0:T(8,128)}, u32[]{:S(2)}) copy-start(f32[1,1024,400]{1,2,0:T(8,128)} %param.7) | copy-start | bytes 4915204
  78.6 3.3 %collective-permute-start.1 = (f32[112,128]{1,0:T(8,128)S(1)}, f32[112,128]{1,0:T(8,128)S(1)}, u32[]{:S(2)}, u32[]{:S(2)}) collective-permute-start(f32[112,128]{1,0:T(8,128)S(1)} %get-tuple-element.24.cand_ref), channel_id=1, source_target_pairs={{0,256},{256,0},{1,257},{257,1},{2,258},{258,2},{3,259},{259,3},{4... | collective-permute-start | bytes 172040 | tf_op jit(solution)/shard_map/ppermute | solution.py:385

commit v8 on v7

--- a/solution.py
+++ b/solution.py
@@ -143,12 +143,14 @@
         pltpu.make_async_copy(out_ref.at[part], out_hbm.at[part], left.at[part]).wait()
 
 
-def gather_kernel(parts_ref, mine_ref, low_ref, own_ref):
+def gather_kernel(parts_ref, mine_ref, low_ref, own_ref, tight):
     total = parts_ref[0, :BLOCK].astype(F32)
     for part in range(1, N_X):
         total += parts_ref[part, :BLOCK].astype(F32)
     mine_ref[...] = total
-    low_ref[...] = total.astype(BF16)
+    tight[: TIGHT // 2, :] = total[: TIGHT // 2]
+    tight[TIGHT // 2 :, :] = total[IM : IM + TIGHT // 2]
+    low_ref[...] = tight[...].astype(BF16)
     group = lane_group((8, 128))
     for eight in range(BLOCK // 8):
         lanes = 128 * (eight // 4)
@@ -164,15 +166,17 @@
         build_taps(taps_ref.at[part], weights, rows[HIGH_ROW : HIGH_ROW + 1], rows[LOW_ROW : LOW_ROW + 1])
 
 
-def back_kernel(mine_ref, other_ref, data_ref, ctf_ref, cos_ref, sin_ref, taps_ref, out_ref, back, grad):
+def back_kernel(mine_ref, other_ref, data_ref, ctf_ref, cos_ref, sin_ref, taps_ref, out_ref, back, grad, theirs):
     back[2 * RB :, :] = jnp.zeros((TIGHT - 2 * RB, ROWS), F32)
+    theirs[:, TIGHT:, :] = jnp.zeros((2, BLOCK - TIGHT, 128), F32)
     for chunk in range(ROWS // 128):
         at = slice(128 * chunk, 128 * (chunk + 1))
         ctf = ctf_ref[:, at]
         cosine = cos_ref[:, at]
         sine = sin_ref[:, at]
-        proj_re = mine_ref[:IM, at] + other_ref[:IM, at].astype(F32)
-        proj_im = mine_ref[IM:, at] + other_ref[IM:, at].astype(F32)
+        theirs[chunk % 2, :TIGHT, :] = other_ref[:, at].astype(F32)
+        proj_re = mine_ref[:IM, at] + theirs[chunk % 2, :IM, :]
+        proj_im = mine_ref[IM:, at] + theirs[chunk % 2, TIGHT // 2 : TIGHT // 2 + IM, :]
         res_re = ctf * (cosine * proj_re - sine * proj_im) - data_ref[0, :, at].astype(F32)
         res_im = ctf * (sine * proj_re + cosine * proj_im) - data_ref[1, :, at].astype(F32)
         back[:RB, at] = (ctf * (cosine * res_re + sine * res_im))[:RB]
@@ -344,11 +348,12 @@
         gather_kernel,
         out_shape=(
             jax.ShapeDtypeStruct((BLOCK, ROWS), F32),
-            jax.ShapeDtypeStruct((BLOCK, ROWS), BF16),
+            jax.ShapeDtypeStruct((TIGHT, ROWS), BF16),
             shard,
         ),
         in_specs=[vmem()],
         out_specs=(vmem(), vmem(), vmem()),
+        scratch_shapes=[pltpu.VMEM((TIGHT, ROWS), F32)],
         compiler_params=limit(4),
         name="gather",
     )(parts)
@@ -367,7 +372,7 @@
         out_shape=jax.ShapeDtypeStruct((N_DOM, TIGHT, 128), BF16),
         in_specs=[vmem()] * 7,
         out_specs=vmem(),
-        scratch_shapes=[pltpu.VMEM((TIGHT, ROWS), F32), pltpu.VMEM((N_X, LINES, TIGHT), F32)],
+        scratch_shapes=[pltpu.VMEM((TIGHT, ROWS), F32), pltpu.VMEM((N_X, LINES, TIGHT), F32), pltpu.VMEM((2, BLOCK, 128), F32)],
         compiler_params=limit(16),
         name="back",
     )(mine, other, data, ctf, cosine, sine, taps)

time: 131 us -> 130 us (level)
  no operation moved by 1% of the time
where the time goes in v8:
time: 130 us
  blocking collectives  81.9 us (63%)
  waiting for transfers between devices  21.2 us (16%)
  starting transfers between devices  13.3 us (10%)
  Pallas kernels  11.5 us (9%)
  other arithmetic  1.31 us (1%)
    all_to_all x3, blocking collectives, exchange(): lax.all_to_all(value, axis, 0, 0, tiled=True, axis_index_groups=groups)  81.9 us
    all_to_all x1, waiting for transfers between devices, exchange(): lax.all_to_all(value, axis, 0, 0, tiled=True, axis_index_groups=groups)  12.3 us
    ppermute x1, waiting for transfers between devices, body(): other = lax.ppermute(low, 'slab', [(at, at ^ N_X) for at in range(N_SLAB)])  7.66 us
    ppermute x1, starting transfers between devices, body(): other = lax.ppermute(low, 'slab', [(at, at ^ N_X) for at in range(N_SLAB)])  6.84 us
    all_to_all x1, starting transfers between devices, exchange(): lax.all_to_all(value, axis, 0, 0, tiled=True, axis_index_groups=groups)  4.44 us
    pallas_call x1, Pallas kernels, body(): pl.pallas_call(project_kernel, out_shape=sent, in_specs=[pl.BlockSpec(mem...  3.78 us
    pallas_call x1, Pallas kernels, body(): pl.pallas_call(back_kernel, out_shape=jax.ShapeDtypeStruct((N_DOM, TIGHT,...  2.61 us
  transfers between devices with their start and end apart: 3, of which 3 were waited for; matrix products, arithmetic and copies ran while one was open for 1% of the time, Pallas kernels for 1%

profile of v8, /device:TPU:8, one launch (start us, length us, event | category | flops | bytes accessed | tf_op | source)
XLA Modules:
  0.0 130.1 jit_solution(2292281886297504247)
XLA Ops:
  0.0 3.8 %project.1 = bf16[4,120,1024]{2,1,0:T(8,128)(2,1)} custom-call(s32[8,1024]{1,0:T(8,128)} %bitcast.21, f32[8,1024]{1,0:T(8,128)} %bitcast.22, f32[400,1024]{1,0:T(8,128)} %bitcast.19), custom_call_target="tpu_custom_call" | custom-call | tf_op jit(solution)/shard_map/project/pallas_call | solution.py:319
  3.8 4.4 %all-to-all-start = ((bf16[4,120,1024]{2,1,0:T(8,128)(2,1)}), bf16[4,120,1024]{2,1,0:T(8,128)(2,1)S(1)}, u32[]{:S(2)}, u32[]{:S(2)}) async-start(bf16[4,120,1024]{2,1,0:T(8,128)(2,1)} %project.1), calls=%async_computation | async-start | bytes 1966080 | tf_op jit(solution)/shard_map/all_to_all | solution.py:294
  8.4 0.2 select_reduce_fusion
  8.5 0.1 multiply_add_fusion
  8.7 0.1 sine_negate_fusion
  8.8 0.1 copy.8
  8.9 0.2 broadcast_in_dim.32
  9.1 0.2 reshape.62
  9.3 0.9 fusion
  10.3 12.3 %all-to-all-done.parts_ref = bf16[4,120,1024]{2,1,0:T(8,128)(2,1)S(1)} async-done(((bf16[4,120,1024]{2,1,0:T(8,128)(2,1)}), bf16[4,120,1024]{2,1,0:T(8,128)(2,1)S(1)}, u32[]{:S(2)}, u32[]{:S(2)}) %all-to-all-start) | async-done | bytes 983072 | tf_op jit(solution)/shard_map/all_to_all | solution.py:294
  22.7 0.2 gather.1
  22.9 6.8 %collective-permute-start = (bf16[104,1024]{1,0:T(8,128)(2,1)S(1)}, bf16[104,1024]{1,0:T(8,128)(2,1)S(1)}, u32[]{:S(2)}, u32[]{:S(2)}) collective-permute-start(bf16[104,1024]{1,0:T(8,128)(2,1)S(1)} %get-tuple-element.17), channel_id=1, source_target_pairs={{0,4},{1,5},{2,6},{3,7},{4,0},{5,1},{6,2},{7,3},{8,12},{9,13},{10,... | collective-permute-start | bytes 638984 | tf_op jit(solution)/shard_map/ppermute | solution.py:360
  29.7 1.7 %taps.1.taps_ref = bf16[4,1024,1024]{2,1,0:T(8,128)(2,1)S(1)} custom-call(bf16[4,120,1024]{2,1,0:T(8,128)(2,1)S(1)} %all-to-all-done.parts_ref), custom_call_target="tpu_custom_call" | custom-call | flops 16777216 | bytes 10485760 | tf_op jit(solution)/shard_map/taps/pallas_call | solution.py:361
  31.4 7.7 %collective-permute-done.other_ref = bf16[104,1024]{1,0:T(8,128)(2,1)S(1)} collective-permute-done((bf16[104,1024]{1,0:T(8,128)(2,1)S(1)}, bf16[104,1024]{1,0:T(8,128)(2,1)S(1)}, u32[]{:S(2)}, u32[]{:S(2)}) %collective-permute-start) | collective-permute-done | bytes 213024 | tf_op jit(solution)/shard_map/ppermute | solution.py:360
  39.1 2.6 %back.1 = bf16[32,104,128]{2,1,0:T(8,128)(2,1)S(1)} custom-call(f32[112,1024]{1,0:T(8,128)S(1)} %get-tuple-element.16.mine_ref, bf16[104,1024]{1,0:T(8,128)(2,1)S(1)} %collective-permute-done.other_ref, bf16[2,56,1024]{2,1,0:T(8,128)(2,1)S(1)} %pad.17.data_ref, f32[56,1024]{1,0:T(8,128)S(1)} %pad.14.ctf_ref, f32[56,1024]{1,0:T(8,128)S(1)} %pad.15.cos_ref, ...), custom_call_target="tpu_custom_call" | custom-call | tf_op jit(solution)/shard_map/back/pallas_call | solution.py:370
  41.7 36.0 %all_to_all.20.parts_ref = bf16[32,104,128]{2,1,0:T(8,128)(2,1)S(1)} all-to-all(bf16[32,104,128]{2,1,0:T(8,128)(2,1)S(1)} %back.1), channel_id=1, replica_groups=mesh['half'=2,'dom'=32,'slab'=8] {'dom'}, dimensions={0} | all-to-all | bytes 1703936 | tf_op jit(solution)/shard_map/all_to_all | solution.py:294
  77.8 0.2 reduce.1
  78.0 2.1 %collective-permute-start.1 = (f32[112,128]{1,0:T(8,128)S(1)}, f32[112,128]{1,0:T(8,128)S(1)}, u32[]{:S(2)}, u32[]{:S(2)}) collective-permute-start(f32[112,128]{1,0:T(8,128)S(1)} %get-tuple-element.24.cand_ref), channel_id=1, source_target_pairs={{0,256},{256,0},{1,257},{257,1},{2,258},{258,2},{3,259},{259,3},{4... | collective-permute-start | bytes 172040 | tf_op jit(solution)/shard_map/ppermute | solution.py:390
  80.0 1.2 collective-permute-done.1.other_ref
  81.2 0.2 shell.1
  81.5 15.7 %all_to_all.21.parts_ref = bf16[8,32,128]{2,1,0:T(8,128)(2,1)S(1)} all-to-all(bf16[8,32,128]{2,1,0:T(8,128)(2,1)S(1)} %shell.1), channel_id=1, replica_groups=mesh['half'=2,'dom'=32,'slab'=8] {'slab'}, dimensions={0} | all-to-all | bytes 131072 | tf_op jit(solution)/shard_map/all_to_all | solution.py:294
  97.2 0.2 share.1
  97.4 30.2 %all_to_all.22.parts_ref = bf16[32,112,128]{2,1,0:T(8,128)(2,1)S(1)} all-to-all(bf16[32,112,128]{2,1,0:T(8,128)(2,1)S(1)} %share.1), channel_id=1, replica_groups=mesh['half'=2,'dom'=32,'slab'=8] {'dom'}, dimensions={0} | all-to-all | bytes 1835008 | tf_op jit(solution)/shard_map/all_to_all | solution.py:294
  127.6 2.5 %update.1 = f32[400,1024]{1,0:T(8,128)} custom-call(f32[400,1024]{1,0:T(8,128)S(1)} %bitcast.20, bf16[32,112,128]{2,1,0:T(8,128)(2,1)S(1)} %all_to_all.22.parts_ref), custom_call_target="tpu_custom_call" | custom-call | tf_op jit(solution)/shard_map/update/pallas_call | solution.py:411
  (20 shorter events, 0.3 us)
Async XLA Ops:
  0.0 10.2 %copy-start = (bf16[1,1024,400]{1,2,0:T(8,128)(2,1)S(1)}, bf16[1,1024,400]{1,2,0:T(8,128)(2,1)}, u32[]{:S(2)}) copy-start(bf16[1,1024,400]{1,2,0:T(8,128)(2,1)} %param.8) | copy-start | bytes 2457604
  3.8 4.5 %copy-start.2 = (s32[1,2,16]{2,1,0:T(2,128)S(1)}, s32[1,2,16]{2,1,0:T(2,128)}, u32[]{:S(2)}) copy-start(s32[1,2,16]{2,1,0:T(2,128)} %param.12) | copy-start | bytes 388
  3.8 4.5 %copy-start.3 = (f32[16]{0:T(128)S(1)}, f32[16]{0:T(128)}, u32[]{:S(2)}) copy-start(f32[16]{0:T(128)} %param.13) | copy-start | bytes 196
  3.8 4.5 %copy-start.4 = (s32[1,16]{1,0:T(1,128)S(1)}, s32[1,16]{1,0:T(1,128)}, u32[]{:S(2)}) copy-start(s32[1,16]{1,0:T(1,128)} %param.11) | copy-start | bytes 196
  3.8 18.8 %all-to-all-start = ((bf16[4,120,1024]{2,1,0:T(8,128)(2,1)}), bf16[4,120,1024]{2,1,0:T(8,128)(2,1)S(1)}, u32[]{:S(2)}, u32[]{:S(2)}) async-start(bf16[4,120,1024]{2,1,0:T(8,128)(2,1)} %project.1), calls=%async_computation | async-start | bytes 1966080 | tf_op jit(solution)/shard_map/all_to_all | solution.py:294
  22.9 16.2 %collective-permute-start = (bf16[104,1024]{1,0:T(8,128)(2,1)S(1)}, bf16[104,1024]{1,0:T(8,128)(2,1)S(1)}, u32[]{:S(2)}, u32[]{:S(2)}) collective-permute-start(bf16[104,1024]{1,0:T(8,128)(2,1)S(1)} %get-tuple-element.17), channel_id=1, source_target_pairs={{0,4},{1,5},{2,6},{3,7},{4,0},{5,1},{6,2},{7,3},{8,12},{9,13},{10,... | collective-permute-start | bytes 638984 | tf_op jit(solution)/shard_map/ppermute | solution.py:360
  78.0 49.6 %copy-start.1 = (f32[1,1024,400]{1,2,0:T(8,128)S(1)}, f32[1,1024,400]{1,2,0:T(8,128)}, u32[]{:S(2)}) copy-start(f32[1,1024,400]{1,2,0:T(8,128)} %param.7) | copy-start | bytes 4915204
  78.0 3.3 %collective-permute-start.1 = (f32[112,128]{1,0:T(8,128)S(1)}, f32[112,128]{1,0:T(8,128)S(1)}, u32[]{:S(2)}, u32[]{:S(2)}) collective-permute-start(f32[112,128]{1,0:T(8,128)S(1)} %get-tuple-element.24.cand_ref), channel_id=1, source_target_pairs={{0,256},{256,0},{1,257},{257,1},{2,258},{258,2},{3,259},{259,3},{4... | collective-permute-start | bytes 172040 | tf_op jit(solution)/shard_map/ppermute | solution.py:390

commit v9 on v8

--- a/solution.py
+++ b/solution.py
@@ -189,13 +189,15 @@
         out_ref[dom] = jnp.concatenate(lines, axis=0).T.astype(BF16)
 
 
-def reduce_kernel(parts_ref, own_ref, grad_ref, cand_ref, total):
+def reduce_kernel(parts_ref, own_ref, grad_ref, cand_ref, low_ref, total):
     total[...] = jnp.sum(parts_ref[...].astype(F32), axis=0)
     grad_ref[...] = jnp.zeros(grad_ref.shape, F32)
     grad_ref[:RB, :] = total[:RB, :]
     grad_ref[IM : IM + RB, :] = total[RB : 2 * RB, :]
     row = lax.broadcasted_iota(jnp.int32, cand_ref.shape, 0) % IM
-    cand_ref[...] = jnp.where(row < RB, own_ref[...] - STEP * grad_ref[...], 0.0)
+    cand = jnp.where(row < RB, own_ref[...] - STEP * grad_ref[...], 0.0)
+    cand_ref[...] = cand
+    low_ref[...] = cand.astype(BF16)
 
 
 def split(value):
@@ -205,7 +207,7 @@
 
 def shell_kernel(grad_ref, cand_ref, other_ref, out_ref, block):
     mine = cand_ref[...]
-    other = other_ref[...]
+    other = other_ref[...].astype(F32)
     for item, product in enumerate((mine * other, mine * mine, other * other)):
         shell = product[:IM] + product[IM:]
         shell = jnp.concatenate([shell, jnp.zeros((128 - IM, 128), F32)], axis=0)
@@ -378,16 +380,16 @@
     )(mine, other, data, ctf, cosine, sine, taps)
     parts = exchange(parts, "dom")
 
-    grad, cand = pl.pallas_call(
+    grad, cand, low = pl.pallas_call(
         reduce_kernel,
-        out_shape=(shard, shard),
+        out_shape=(shard, shard, jax.ShapeDtypeStruct((BLOCK, 128), BF16)),
         in_specs=[vmem()] * 2,
-        out_specs=(vmem(), vmem()),
+        out_specs=(vmem(), vmem(), vmem()),
         scratch_shapes=[pltpu.VMEM((TIGHT, 128), F32)],
         compiler_params=limit(4),
         name="reduce",
     )(parts, own)
-    other = lax.ppermute(cand, "half", [(0, 1), (1, 0)])
+    other = lax.ppermute(low, "half", [(0, 1), (1, 0)])
     share = pl.pallas_call(
         shell_kernel,
         out_shape=jax.ShapeDtypeStruct((N_SLAB, 32, 128), BF16),

time: 130 us -> 130 us (level)
  no operation moved by 1% of the time
where the time goes in v9:
time: 130 us
  blocking collectives  81.9 us (63%)
  waiting for transfers between devices  21.2 us (16%)
  starting transfers between devices  13.3 us (10%)
  Pallas kernels  11.4 us (9%)
  other arithmetic  1.31 us (1%)
    all_to_all x3, blocking collectives, exchange(): lax.all_to_all(value, axis, 0, 0, tiled=True, axis_index_groups=groups)  81.9 us
    all_to_all x1, waiting for transfers between devices, exchange(): lax.all_to_all(value, axis, 0, 0, tiled=True, axis_index_groups=groups)  12.3 us
    ppermute x1, waiting for transfers between devices, body(): other = lax.ppermute(low, 'slab', [(at, at ^ N_X) for at in range(N_SLAB)])  7.66 us
    ppermute x1, starting transfers between devices, body(): other = lax.ppermute(low, 'slab', [(at, at ^ N_X) for at in range(N_SLAB)])  6.84 us
    all_to_all x1, starting transfers between devices, exchange(): lax.all_to_all(value, axis, 0, 0, tiled=True, axis_index_groups=groups)  4.44 us
    pallas_call x1, Pallas kernels, body(): pl.pallas_call(project_kernel, out_shape=sent, in_specs=[pl.BlockSpec(mem...  3.78 us
    pallas_call x1, Pallas kernels, body(): pl.pallas_call(back_kernel, out_shape=jax.ShapeDtypeStruct((N_DOM, TIGHT,...  2.61 us
  transfers between devices with their start and end apart: 3, of which 3 were waited for; matrix products, arithmetic and copies ran while one was open for 1% of the time, Pallas kernels for 1%

profile of v9, /device:TPU:8, one launch (start us, length us, event | category | flops | bytes accessed | tf_op | source)
XLA Modules:
  0.0 130.0 jit_solution(5135363445876569218)
XLA Ops:
  0.0 3.8 %project.1 = bf16[4,120,1024]{2,1,0:T(8,128)(2,1)} custom-call(s32[8,1024]{1,0:T(8,128)} %bitcast.21, f32[8,1024]{1,0:T(8,128)} %bitcast.22, f32[400,1024]{1,0:T(8,128)} %bitcast.19), custom_call_target="tpu_custom_call" | custom-call | tf_op jit(solution)/shard_map/project/pallas_call | solution.py:321
  3.8 4.4 %all-to-all-start = ((bf16[4,120,1024]{2,1,0:T(8,128)(2,1)}), bf16[4,120,1024]{2,1,0:T(8,128)(2,1)S(1)}, u32[]{:S(2)}, u32[]{:S(2)}) async-start(bf16[4,120,1024]{2,1,0:T(8,128)(2,1)} %project.1), calls=%async_computation | async-start | bytes 1966080 | tf_op jit(solution)/shard_map/all_to_all | solution.py:296
  8.4 0.2 select_reduce_fusion
  8.5 0.1 multiply_add_fusion
  8.7 0.1 sine_negate_fusion
  8.8 0.1 copy.8
  8.9 0.2 broadcast_in_dim.32
  9.1 0.2 reshape.62
  9.3 0.9 fusion
  10.3 12.3 %all-to-all-done.parts_ref = bf16[4,120,1024]{2,1,0:T(8,128)(2,1)S(1)} async-done(((bf16[4,120,1024]{2,1,0:T(8,128)(2,1)}), bf16[4,120,1024]{2,1,0:T(8,128)(2,1)S(1)}, u32[]{:S(2)}, u32[]{:S(2)}) %all-to-all-start) | async-done | bytes 983072 | tf_op jit(solution)/shard_map/all_to_all | solution.py:296
  22.7 0.2 gather.1
  22.9 6.8 %collective-permute-start = (bf16[104,1024]{1,0:T(8,128)(2,1)S(1)}, bf16[104,1024]{1,0:T(8,128)(2,1)S(1)}, u32[]{:S(2)}, u32[]{:S(2)}) collective-permute-start(bf16[104,1024]{1,0:T(8,128)(2,1)S(1)} %get-tuple-element.18), channel_id=1, source_target_pairs={{0,4},{1,5},{2,6},{3,7},{4,0},{5,1},{6,2},{7,3},{8,12},{9,13},{10,... | collective-permute-start | bytes 638984 | tf_op jit(solution)/shard_map/ppermute | solution.py:362
  29.7 1.7 %taps.1.taps_ref = bf16[4,1024,1024]{2,1,0:T(8,128)(2,1)S(1)} custom-call(bf16[4,120,1024]{2,1,0:T(8,128)(2,1)S(1)} %all-to-all-done.parts_ref), custom_call_target="tpu_custom_call" | custom-call | flops 16777216 | bytes 10485760 | tf_op jit(solution)/shard_map/taps/pallas_call | solution.py:363
  31.4 7.7 %collective-permute-done.other_ref = bf16[104,1024]{1,0:T(8,128)(2,1)S(1)} collective-permute-done((bf16[104,1024]{1,0:T(8,128)(2,1)S(1)}, bf16[104,1024]{1,0:T(8,128)(2,1)S(1)}, u32[]{:S(2)}, u32[]{:S(2)}) %collective-permute-start) | collective-permute-done | bytes 213024 | tf_op jit(solution)/shard_map/ppermute | solution.py:362
  39.1 2.6 %back.1 = bf16[32,104,128]{2,1,0:T(8,128)(2,1)S(1)} custom-call(f32[112,1024]{1,0:T(8,128)S(1)} %get-tuple-element.17.mine_ref, bf16[104,1024]{1,0:T(8,128)(2,1)S(1)} %collective-permute-done.other_ref, bf16[2,56,1024]{2,1,0:T(8,128)(2,1)S(1)} %pad.17.data_ref, f32[56,1024]{1,0:T(8,128)S(1)} %pad.14.ctf_ref, f32[56,1024]{1,0:T(8,128)S(1)} %pad.15.cos_ref, ...), custom_call_target="tpu_custom_call" | custom-call | tf_op jit(solution)/shard_map/back/pallas_call | solution.py:372
  41.7 36.0 %all_to_all.20.parts_ref = bf16[32,104,128]{2,1,0:T(8,128)(2,1)S(1)} all-to-all(bf16[32,104,128]{2,1,0:T(8,128)(2,1)S(1)} %back.1), channel_id=1, replica_groups=mesh['half'=2,'dom'=32,'slab'=8] {'dom'}, dimensions={0} | all-to-all | bytes 1703936 | tf_op jit(solution)/shard_map/all_to_all | solution.py:296
  77.8 0.2 reduce.1
  78.0 2.1 %collective-permute-start.1 = (bf16[112,128]{1,0:T(8,128)(2,1)S(1)}, bf16[112,128]{1,0:T(8,128)(2,1)S(1)}, u32[]{:S(2)}, u32[]{:S(2)}) collective-permute-start(bf16[112,128]{1,0:T(8,128)(2,1)S(1)} %get-tuple-element.26), channel_id=1, source_target_pairs={{0,256},{256,0},{1,257},{257,1},{2,258},{258,2},{3,259},{259,3},{4... | collective-permute-start | bytes 86024 | tf_op jit(solution)/shard_map/ppermute | solution.py:392
  80.0 1.2 collective-permute-done.1.other_ref
  81.2 0.2 shell.1
  81.5 15.7 %all_to_all.21.parts_ref = bf16[8,32,128]{2,1,0:T(8,128)(2,1)S(1)} all-to-all(bf16[8,32,128]{2,1,0:T(8,128)(2,1)S(1)} %shell.1), channel_id=1, replica_groups=mesh['half'=2,'dom'=32,'slab'=8] {'slab'}, dimensions={0} | all-to-all | bytes 131072 | tf_op jit(solution)/shard_map/all_to_all | solution.py:296
  97.2 0.2 share.1
  97.4 30.2 %all_to_all.22.parts_ref = bf16[32,112,128]{2,1,0:T(8,128)(2,1)S(1)} all-to-all(bf16[32,112,128]{2,1,0:T(8,128)(2,1)S(1)} %share.1), channel_id=1, replica_groups=mesh['half'=2,'dom'=32,'slab'=8] {'dom'}, dimensions={0} | all-to-all | bytes 1835008 | tf_op jit(solution)/shard_map/all_to_all | solution.py:296
  127.6 2.5 %update.1 = f32[400,1024]{1,0:T(8,128)} custom-call(f32[400,1024]{1,0:T(8,128)S(1)} %bitcast.20, bf16[32,112,128]{2,1,0:T(8,128)(2,1)S(1)} %all_to_all.22.parts_ref), custom_call_target="tpu_custom_call" | custom-call | tf_op jit(solution)/shard_map/update/pallas_call | solution.py:413
  (20 shorter events, 0.3 us)
Async XLA Ops:
  0.0 10.2 %copy-start = (bf16[1,1024,400]{1,2,0:T(8,128)(2,1)S(1)}, bf16[1,1024,400]{1,2,0:T(8,128)(2,1)}, u32[]{:S(2)}) copy-start(bf16[1,1024,400]{1,2,0:T(8,128)(2,1)} %param.8) | copy-start | bytes 2457604
  3.8 4.5 %copy-start.2 = (s32[1,2,16]{2,1,0:T(2,128)S(1)}, s32[1,2,16]{2,1,0:T(2,128)}, u32[]{:S(2)}) copy-start(s32[1,2,16]{2,1,0:T(2,128)} %param.12) | copy-start | bytes 388
  3.8 4.5 %copy-start.3 = (f32[16]{0:T(128)S(1)}, f32[16]{0:T(128)}, u32[]{:S(2)}) copy-start(f32[16]{0:T(128)} %param.13) | copy-start | bytes 196
  3.8 4.5 %copy-start.4 = (s32[1,16]{1,0:T(1,128)S(1)}, s32[1,16]{1,0:T(1,128)}, u32[]{:S(2)}) copy-start(s32[1,16]{1,0:T(1,128)} %param.11) | copy-start | bytes 196
  3.8 18.8 %all-to-all-start = ((bf16[4,120,1024]{2,1,0:T(8,128)(2,1)}), bf16[4,120,1024]{2,1,0:T(8,128)(2,1)S(1)}, u32[]{:S(2)}, u32[]{:S(2)}) async-start(bf16[4,120,1024]{2,1,0:T(8,128)(2,1)} %project.1), calls=%async_computation | async-start | bytes 1966080 | tf_op jit(solution)/shard_map/all_to_all | solution.py:296
  22.9 16.2 %collective-permute-start = (bf16[104,1024]{1,0:T(8,128)(2,1)S(1)}, bf16[104,1024]{1,0:T(8,128)(2,1)S(1)}, u32[]{:S(2)}, u32[]{:S(2)}) collective-permute-start(bf16[104,1024]{1,0:T(8,128)(2,1)S(1)} %get-tuple-element.18), channel_id=1, source_target_pairs={{0,4},{1,5},{2,6},{3,7},{4,0},{5,1},{6,2},{7,3},{8,12},{9,13},{10,... | collective-permute-start | bytes 638984 | tf_op jit(solution)/shard_map/ppermute | solution.py:362
  78.0 49.6 %copy-start.1 = (f32[1,1024,400]{1,2,0:T(8,128)S(1)}, f32[1,1024,400]{1,2,0:T(8,128)}, u32[]{:S(2)}) copy-start(f32[1,1024,400]{1,2,0:T(8,128)} %param.7) | copy-start | bytes 4915204
  78.0 3.2 %collective-permute-start.1 = (bf16[112,128]{1,0:T(8,128)(2,1)S(1)}, bf16[112,128]{1,0:T(8,128)(2,1)S(1)}, u32[]{:S(2)}, u32[]{:S(2)}) collective-permute-start(bf16[112,128]{1,0:T(8,128)(2,1)S(1)} %get-tuple-element.26), channel_id=1, source_target_pairs={{0,256},{256,0},{1,257},{257,1},{2,258},{258,2},{3,259},{259,3},{4... | collective-permute-start | bytes 86024 | tf_op jit(solution)/shard_map/ppermute | solution.py:392
